TPU v7x, 256 devices: a whole 4x4x8 slice. The times are simulated.
256 devices in a mesh: chan: 4 (over z_hi), rows: 64 (over x, z_lo, y, core).
Axes of the slice: x: 4, y: 4, z: 8 (z_hi: 4, z_lo: 2; z = z_hi * 2 + z_lo), core: 2. Of those that a mesh axis runs over, the one named last changes fastest.
Arguments:
- tokens: bfloat16 [512, 512, 512], P('rows', None, 'chan'), may hold values from -60 to 60
- gain_in: float32 [512], P('chan'), may hold values from 0.1 to 1.9
- spectral_w1: float32 [2, 8, 64, 64], P(None, 'chan'), may hold values from -0.75 to 0.75
- spectral_b1: float32 [2, 8, 64], P(None, 'chan'), may hold values from -3 to 3
- spectral_w2: float32 [2, 8, 64, 64], P(None, 'chan'), may hold values from -0.75 to 0.75
- spectral_b2: float32 [2, 8, 64], P(None, 'chan'), may hold values from -3 to 3
- gain_out: float32 [512], replicated, may hold values from 0.1 to 1.9
- fc1_weight: bfloat16 [512, 2048], P(None, 'chan'), may hold values from -0.25 to 0.25
- fc1_bias: bfloat16 [2048], P('chan'), may hold values from -3 to 3
- fc2_weight: bfloat16 [2048, 512], P('chan'), may hold values from -0.1875 to 0.1875
- fc2_bias: bfloat16 [512], P('chan'), may hold values from -3 to 3
Outputs:
- block_out: bfloat16 [512, 512, 512], P('rows', None, 'chan')
All inputs are finite; a program needn't handle non-finite values.
Results may differ from a plain program's by a relative error of at most 0.0055.
Values may be sent and summed in bfloat16 or wider, within the bound.
No kernel may reach another device: no remote copies, remote signals or barrier semaphores. Data moves between devices by JAX's collectives and lax.ppermute only.
A program may use at most 64 MiB of HBM per device.

v0:
```python
import math
from functools import partial

import jax
import jax.numpy as jnp
import numpy as np
from jax import lax
from jax.experimental import pallas as pl
from jax.experimental.pallas import tpu as pltpu
from jax.sharding import PartitionSpec as P

norm_eps = 1e-05
shrink_level = 0.01
bf16 = jnp.bfloat16
f32 = jnp.float32


def tables(rows, width, per_owner):
    owners = width // 2 // per_owner
    place = np.arange(width)
    freq = np.arange(width // 2).reshape(owners, 1, per_owner)
    freq = np.broadcast_to(freq, (owners, 2, per_owner)).reshape(-1)
    part = np.broadcast_to(np.arange(2).reshape(1, 2, 1), (owners, 2, per_owner)).reshape(-1)
    angle = 2.0 * np.pi / width * ((freq[:, None] * place[None, :]) % width)
    forward = np.where(part[:, None] == 0, np.cos(angle), -np.sin(angle))
    inverse = (forward * np.where(freq == 0, 1.0, 2.0)[:, None]).T
    grid = np.arange(rows)
    turn = 2.0 * np.pi / rows * ((grid[:, None] * grid[None, :]) % rows)
    return forward, inverse, np.cos(turn), np.sin(turn)


def mm(left, right):
    return jnp.dot(left, right, preferred_element_type=f32)


def mm_t(left, right):
    return lax.dot_general(left, right, (((1,), (1,)), ((), ())), preferred_element_type=f32)


def stats_kernel(x_ref, bias_ref, o_ref):
    rows, width, lanes = x_ref.shape
    o_ref[2] = jnp.zeros((rows, width), f32)
    o_ref[2, 0:1, 0:lanes] = bias_ref[...].astype(f32)
    ones = jnp.ones((8, x_ref.shape[2]), bf16)
    for row in range(rows):
        x = x_ref[row]
        wide = x.astype(f32)
        square = wide * wide
        high = square.astype(bf16)
        low = (square - high.astype(f32)).astype(bf16)
        o_ref[0, row : row + 1, :] = mm_t(ones, x)[0:1]
        o_ref[1, row : row + 1, :] = (mm_t(ones, high) + mm_t(ones, low))[0:1]


def forward_kernel(channels, scale, x_ref, s0_ref, s1_ref, s2_ref, s3_ref, gain_ref, table_hbm, o_ref, f_ref, table_ref, sem):
    rows, _, lanes = x_ref.shape
    fetch = pltpu.make_async_copy(table_hbm, table_ref, sem)
    fetch.start()
    owners = o_ref.shape[0]
    total = (s0_ref[0] + s1_ref[0]) + (s2_ref[0] + s3_ref[0])
    square = (s0_ref[1] + s1_ref[1]) + (s2_ref[1] + s3_ref[1])
    center = total / channels
    spread = square / channels - center * center
    flipped = jnp.transpose(jnp.concatenate([center, lax.rsqrt(spread + norm_eps)], axis=0))
    f_ref[...] = flipped
    gain = gain_ref[...]
    for pair in range(rows // 2):
        sides = []
        for row in (2 * pair, 2 * pair + 1):
            x = x_ref[row].astype(f32)
            normed = (x - flipped[:, row : row + 1]) * flipped[:, rows + row : rows + row + 1] * gain
            sides.append(normed.astype(bf16))
        if pair == 0:
            fetch.wait()
        out = mm(table_ref[...], jnp.concatenate(sides, axis=1)) * scale
        for side in range(2):
            o_ref[:, 2 * pair + side] = (
                out[:, side * lanes : (side + 1) * lanes].reshape(owners, -1, lanes).astype(bf16)
            )


def soften(values):
    return jnp.where(
        values > shrink_level,
        values - shrink_level,
        jnp.where(values < -shrink_level, values + shrink_level, 0.0),
    )


def block_matrix(w_ref, part):
    count, size = w_ref.shape[1], w_ref.shape[2]
    rows = []
    for block in range(count):
        cells = [jnp.zeros((size, size), f32)] * count
        cells[block] = w_ref[part, block]
        rows.append(jnp.concatenate(cells, axis=1))
    return jnp.concatenate(rows, axis=0)


def complex_matrix(w_ref):
    real, imag = block_matrix(w_ref, 0), block_matrix(w_ref, 1)
    return jnp.concatenate(
        [jnp.concatenate([real, imag], axis=1), jnp.concatenate([-imag, real], axis=1)], axis=0
    ).astype(bf16)


def bias_row(b_ref):
    parts, count = b_ref.shape[0], b_ref.shape[1]
    return jnp.concatenate(
        [b_ref[part, block : block + 1, :] for part in range(parts) for block in range(count)], axis=1
    )


def column_kernel(
    scale,
    x_ref,
    cos_hbm,
    sin_hbm,
    w1_ref,
    b1_ref,
    w2_ref,
    b2_ref,
    o_ref,
    wide_ref,
    real_ref,
    imag_ref,
    cos_ref,
    sin_ref,
    sems,
):
    fetches = [
        pltpu.make_async_copy(source, target, sems.at[place])
        for place, (source, target) in enumerate(((cos_hbm, cos_ref), (sin_hbm, sin_ref)))
    ]
    for fetch in fetches:
        fetch.start()
    weight_one, weight_two = complex_matrix(w1_ref), complex_matrix(w2_ref)
    bias_one, bias_two = bias_row(b1_ref), bias_row(b2_ref)
    height = cos_ref.shape[0]
    lanes = x_ref.shape[1]
    step = x_ref.shape[0] // height
    count = step // 2
    wide_ref[...] = x_ref[...].astype(f32)
    for part, target in ((0, real_ref), (1, imag_ref)):
        for k in range(count):
            target[:, k * lanes : (k + 1) * lanes] = wide_ref[
                pl.ds(part * count + k, height, stride=step), :
            ].astype(bf16)
    for fetch in fetches:
        fetch.wait()
    for half in range(count // 2):
        span = pl.ds(half * 2 * lanes, 2 * lanes)
        cos, sin = cos_ref[...], sin_ref[...]
        real, imag = real_ref[:, span], imag_ref[:, span]
        out_real = (mm(cos, real) + mm(sin, imag)) * scale
        out_imag = (mm(cos, imag) - mm(sin, real)) * scale
        next_real, next_imag = [], []
        for side in range(2):
            cut = slice(side * lanes, (side + 1) * lanes)
            both = jnp.concatenate([out_real[:, cut].astype(bf16), out_imag[:, cut].astype(bf16)], axis=1)
            first = jnp.maximum(mm(both, weight_one) + bias_one, 0.0).astype(bf16)
            second = soften(mm(first, weight_two) + bias_two).astype(bf16)
            next_real.append(second[:, :lanes])
            next_imag.append(second[:, lanes:])
        real, imag = jnp.concatenate(next_real, axis=1), jnp.concatenate(next_imag, axis=1)
        back_real = (mm(cos, real) - mm(sin, imag)) * scale
        back_imag = (mm(cos, imag) + mm(sin, real)) * scale
        for side in range(2):
            cut = slice(side * lanes, (side + 1) * lanes)
            k = half * 2 + side
            wide_ref[pl.ds(k, height, stride=step), :] = back_real[:, cut]
            wide_ref[pl.ds(count + k, height, stride=step), :] = back_imag[:, cut]
    o_ref[...] = wide_ref[...].astype(bf16)


def inverse_kernel(scale, me_ref, x_ref, table_hbm, t_ref, f_ref, gain_ref, *refs):
    *o_refs, table_ref, sem = refs
    fetch = pltpu.make_async_copy(table_hbm, table_ref, sem)
    fetch.start()
    ways = len(o_refs)
    rows, width, lanes = t_ref.shape
    group = rows // ways
    me = me_ref[0]
    gain = gain_ref[...]
    column = lax.broadcasted_iota(jnp.int32, f_ref.shape, 1)
    for shift in range(ways):
        owner = lax.rem(me + shift, ways)
        for pair in range(group // 2):
            first = owner * group + 2 * pair
            sides = [
                x_ref[:, first + side].astype(f32).reshape(-1, lanes).astype(bf16) for side in range(2)
            ]
            if shift == 0 and pair == 0:
                fetch.wait()
            out = mm(table_ref[...], jnp.concatenate(sides, axis=1)) * scale
            for side in range(2):
                row = first + side
                source = t_ref[row].astype(f32)
                center = jnp.sum(jnp.where(column == row, f_ref[...], 0.0), axis=1, keepdims=True)
                factor = jnp.sum(jnp.where(column == row + rows, f_ref[...], 0.0), axis=1, keepdims=True)
                normed = (source - center) * factor * gain
                o_refs[shift][pl.ds((2 * pair + side) * width, width), :] = (
                    (out[:, side * lanes : (side + 1) * lanes] + normed) + source
                ).astype(bf16)


def gelu(values):
    return 0.5 * values * (1.0 + lax.erf(values * math.sqrt(0.5)))


def mlp_kernel(tile, me_ref, x0, x1, x2, x3, wa_ref, wb_ref, gain_ref, s0, s1, s2, s3, y0, y1, y2, y3, x_ref, y_ref, b_ref):
    ways, tokens, lanes = x_ref.shape
    channels = ways * lanes
    me = me_ref[0]
    biases_out = (s0, s1, s2, s3)
    for shift, ref in enumerate((x0, x1, x2, x3)):
        x_ref[lax.rem(me + ways - shift, ways)] = ref[...]
        b_ref[pl.ds(lax.rem(me + ways - shift, ways), 1), :] = biases_out[shift][2, 0:1, 0:lanes]
    unit = jnp.ones((8, lanes), bf16)
    hidden_block = 512
    biases = []
    for ref in (wa_ref, wb_ref):
        for start in range(0, ref.shape[0], hidden_block):
            biases.append(mm_t(unit, ref[start : start + hidden_block, 2 * channels :])[0:1])

    def body(index, carry):
        span = pl.ds(pl.multiple_of(index * tile, tile), tile)
        mixed = [x_ref[block, span, :].astype(f32) for block in range(ways)]
        total = sum(mixed[1:], mixed[0])
        square = sum((m * m for m in mixed[1:]), mixed[0] * mixed[0])
        center = jnp.sum(total, axis=1, keepdims=True) / channels
        spread = jnp.sum(square, axis=1, keepdims=True) / channels - center * center
        inverse = lax.rsqrt(spread + norm_eps)
        normed = jnp.concatenate(
            [
                ((m - center) * inverse * gain_ref[:, b * lanes : (b + 1) * lanes]).astype(bf16)
                for b, m in enumerate(mixed)
            ],
            axis=1,
        )
        acc = None
        block = 0
        for ref in (wa_ref, wb_ref):
            for start in range(0, ref.shape[0], hidden_block):
                rows = pl.ds(start, hidden_block)
                hidden = gelu(mm_t(normed, ref[rows, :channels]) + biases[block]).astype(bf16)
                product = mm(hidden, ref[rows, channels : 2 * channels])
                acc = product if acc is None else acc + product
                block += 1
        for b in range(ways):
            cut = slice(b * lanes, (b + 1) * lanes)
            y_ref[b, span, :] = (mixed[b] + acc[:, cut] + b_ref[b : b + 1, :]).astype(bf16)
        return carry

    lax.fori_loop(0, tokens // tile, body, 0)
    for shift, ref in enumerate((y0, y1, y2, y3)):
        ref[...] = y_ref[lax.rem(me + shift, ways)]


def place_kernel(me_ref, x0, x1, x2, x3, o_ref):
    ways = o_ref.shape[0]
    for shift, ref in enumerate((x0, x1, x2, x3)):
        o_ref[lax.rem(me_ref[0] + ways - shift, ways)] = ref[...]


def piece_kernel(piece_ref, one_ref, bias_ref, two_ref, o_ref, flat_ref):
    units, columns = o_ref.shape
    channels = one_ref.shape[0]
    lanes = columns - 2 * channels
    piece = piece_ref[0]
    slab = pl.ds(pl.multiple_of(piece * units // lanes * lanes, lanes), lanes)
    row = lax.broadcasted_iota(jnp.int32, (lanes, lanes), 0)
    column = lax.broadcasted_iota(jnp.int32, (lanes, lanes), 1)
    unit = jnp.where(row == column, 1.0, 0.0).astype(bf16)
    flat_ref[:, 0:channels] = mm_t(unit, one_ref[:, slab])
    bias = jnp.where(row == column, jnp.broadcast_to(bias_ref[:, slab].astype(f32), (lanes, lanes)), 0.0)
    flat_ref[:, channels:] = bias
    within = pl.ds(pl.multiple_of(lax.rem(piece * units, lanes), units), units)
    o_ref[:, 0:channels] = flat_ref[within, 0:channels].astype(bf16)
    o_ref[:, channels : 2 * channels] = two_ref[pl.ds(pl.multiple_of(piece * units, units), units), :]
    o_ref[:, 2 * channels :] = flat_ref[within, channels:].astype(bf16)


def vmem(count):
    return [pl.BlockSpec(memory_space=pltpu.VMEM)] * count


smem = pl.BlockSpec(memory_space=pltpu.SMEM)
hbm = pl.BlockSpec(memory_space=pltpu.HBM)


def call(kernel, shapes, in_specs, scratch=(), flops=0, size=0):
    return pl.pallas_call(
        kernel,
        out_shape=shapes,
        in_specs=in_specs,
        out_specs=jax.tree.map(lambda _: pl.BlockSpec(memory_space=pltpu.VMEM), shapes),
        scratch_shapes=scratch,
        cost_estimate=pl.CostEstimate(flops=flops, bytes_accessed=size, transcendentals=0),
        compiler_params=pltpu.CompilerParams(vmem_limit_bytes=24 * 1024 * 1024),
    )


def shape(dims, dtype):
    return jax.ShapeDtypeStruct(dims, dtype)


def shifts(value_of, axis, ways):
    return [
        lax.ppermute(value_of(shift), axis, [(i, (i + shift) % ways) for i in range(ways)])
        for shift in range(1, ways)
    ]


def local(
    tokens,
    gain_in,
    spectral_w1,
    spectral_b1,
    spectral_w2,
    spectral_b2,
    gain_out,
    fc1_weight,
    fc1_bias,
    fc2_weight,
    fc2_bias,
):
    rows, width, lanes = tokens.shape
    ways = lax.axis_size("chan")
    owners = lax.axis_size("rows")
    height = rows * owners
    channels = lanes * ways
    per_owner = width // 2 // owners
    me = lax.axis_index("chan").astype(jnp.int32).reshape(1)
    forward, inverse, cos, sin = (jnp.asarray(t, bf16) for t in tables(height, width, per_owner))
    half_scale = 2.0 ** math.floor(math.log2(math.sqrt(width)))
    first_scale, second_scale = 1.0 / half_scale, half_scale / math.sqrt(width * height)

    stats = call(stats_kernel, shape((3, rows, width), f32), vmem(2))(
        tokens, fc2_bias.reshape(1, lanes)
    )
    others = shifts(lambda s: stats, "chan", ways)
    spectra, flipped = call(
        partial(forward_kernel, channels, first_scale),
        (shape((owners, rows, 2 * per_owner, lanes), bf16), shape((width, 2 * rows), f32)),
        vmem(6) + [hbm],
        scratch=[pltpu.VMEM(forward.shape, bf16), pltpu.SemaphoreType.DMA],
    )(tokens, stats, *others, gain_in.reshape(1, lanes), forward)
    columns = lax.all_to_all(spectra, "rows", split_axis=0, concat_axis=0)

    ring_x, per_x = 4, owners // 4
    place = lax.axis_index("rows").astype(jnp.int32)
    units = fc1_weight.shape[1] // (2 * ring_x)
    piece = ((place // per_x) * 2 + place % 2).reshape(1)
    mine = call(
        piece_kernel,
        shape((units, 2 * channels + lanes), bf16),
        [smem] + vmem(3),
        scratch=[pltpu.VMEM((lanes, channels + lanes), f32)],
    )(piece, fc1_weight, fc1_bias.reshape(1, -1), fc2_weight)
    stage = jnp.concatenate([mine] + shifts(lambda s: mine, "chan", ways), axis=0)
    parts = [stage]
    for shift in range(1, ring_x):
        parts.append(
            lax.ppermute(stage, "rows", [(i, (i + shift * per_x) % owners) for i in range(owners)])
        )
    near = jnp.concatenate(parts, axis=0)
    far = lax.ppermute(near, "rows", [(i, i ^ 1) for i in range(owners)])

    total = owners * rows * 2 * per_owner
    back = call(
        partial(column_kernel, second_scale),
        shape((total, lanes), bf16),
        vmem(1) + [hbm] * 2 + vmem(4),
        scratch=[
            pltpu.VMEM((total, lanes), f32),
            pltpu.VMEM((height, per_owner * lanes), bf16),
            pltpu.VMEM((height, per_owner * lanes), bf16),
            pltpu.VMEM(cos.shape, bf16),
            pltpu.VMEM(sin.shape, bf16),
            pltpu.SemaphoreType.DMA((2,)),
        ],
    )(
        columns.reshape(total, lanes),
        cos,
        sin,
        spectral_w1,
        spectral_b1,
        spectral_w2,
        spectral_b2,
    )
    returned = lax.all_to_all(
        back.reshape(owners, rows, 2 * per_owner, lanes), "rows", split_axis=0, concat_axis=0
    )
    share = rows // ways * width
    mixed = call(
        partial(inverse_kernel, first_scale),
        [shape((share, lanes), bf16)] * ways,
        [smem] + vmem(1) + [hbm] + vmem(3),
        scratch=[pltpu.VMEM(inverse.shape, bf16), pltpu.SemaphoreType.DMA],
    )(me, returned, inverse, tokens, flipped, gain_in.reshape(1, lanes))
    whole = [mixed[0]] + shifts(lambda s: mixed[s], "chan", ways)
    result = call(
        partial(mlp_kernel, 256),
        [shape((share, lanes), bf16)] * ways,
        [smem] + vmem(11),
        scratch=[
            pltpu.VMEM((ways, share, lanes), bf16),
            pltpu.VMEM((ways, share, lanes), bf16),
            pltpu.VMEM((ways, lanes), f32),
        ],
    )(me, *whole, near, far, gain_out.reshape(1, channels), stats, *others)
    parts = [result[0]] + shifts(lambda s: result[s], "chan", ways)
    final = call(place_kernel, shape((ways, share, lanes), bf16), [smem] + vmem(4))(me, *parts)
    return final.reshape(rows, width, lanes)


def solution(mesh):
    return jax.shard_map(
        local,
        mesh=mesh,
        in_specs=(
            P("rows", None, "chan"),
            P("chan"),
            P(None, "chan", None, None),
            P(None, "chan", None),
            P(None, "chan", None, None),
            P(None, "chan", None),
            P(),
            P(None, "chan"),
            P("chan"),
            P("chan", None),
            P("chan"),
        ),
        out_specs=P("rows", None, "chan"),
        check_vma=False,
    )
```

profile of v0, /device:TPU:1, one launch (start us, length us, event | category | flops | bytes accessed | tf_op | source)
XLA Modules:
  0.0 190.7 jit_solution(8398108634326803499)
XLA Ops:
  2.8 3.8 %collective-permute-start = (f32[3,8,512]{2,1,0:T(8,128)S(1)}, f32[3,8,512]{2,1,0:T(8,128)S(1)}, u32[]{:S(2)}, u32[]{:S(2)}) collective-permute-start(f32[3,8,512]{2,1,0:T(8,128)S(1)} %shard_map.145.s0_ref.s0), channel_id=1, source_target_pairs={{0,64},{64,128},{128,192},{192,0},{1,65},{65,129},{129,193},{193,1... | collective-permute-start | bytes 147464 | tf_op jit(solution)/shard_map/ppermute | solution.py:310
  6.6 5.1 %collective-permute-start.1 = (f32[3,8,512]{2,1,0:T(8,128)S(1)}, f32[3,8,512]{2,1,0:T(8,128)S(1)}, u32[]{:S(2)}, u32[]{:S(2)}) collective-permute-start(f32[3,8,512]{2,1,0:T(8,128)S(1)} %shard_map.145.s0_ref.s0), channel_id=1, source_target_pairs={{0,128},{64,192},{128,0},{192,64},{1,129},{65,193},{129,1},{193,65... | collective-permute-start | bytes 147464 | tf_op jit(solution)/shard_map/ppermute | solution.py:310
  11.8 2.4 %collective-permute-start.2 = (f32[3,8,512]{2,1,0:T(8,128)S(1)}, f32[3,8,512]{2,1,0:T(8,128)S(1)}, u32[]{:S(2)}, u32[]{:S(2)}) collective-permute-start(f32[3,8,512]{2,1,0:T(8,128)S(1)} %shard_map.145.s0_ref.s0), channel_id=1, source_target_pairs={{0,192},{64,0},{128,64},{192,128},{1,193},{65,1},{129,65},{193,129... | collective-permute-start | bytes 147464 | tf_op jit(solution)/shard_map/ppermute | solution.py:310
  14.1 3.2 %collective-permute-done.2.s3_ref.s3 = f32[3,8,512]{2,1,0:T(8,128)S(1)} collective-permute-done((f32[3,8,512]{2,1,0:T(8,128)S(1)}, f32[3,8,512]{2,1,0:T(8,128)S(1)}, u32[]{:S(2)}, u32[]{:S(2)}) %collective-permute-start.2) | collective-permute-done | bytes 49184 | tf_op jit(solution)/shard_map/ppermute | solution.py:310
  19.0 2.8 %shard_map.146 = (bf16[64,8,8,128]{3,2,1,0:T(8,128)(2,1)}, f32[512,16]{1,0:T(8,128)S(1)}) custom-call(bf16[8,512,128]{2,1,0:T(8,128)(2,1)S(1)} %copy-done, f32[3,8,512]{2,1,0:T(8,128)S(1)} %shard_map.145.s0_ref.s0, f32[3,8,512]{2,1,0:T(8,128)S(1)} %collective-permute-done.s1_ref.s1, f32[3,8,512]{2,1,0:T(8,128)S(1)} %collective-permute-done.1.s2_ref.s2, ...), custom_call_target="tpu_custom_call" | custom-call | tf_op jit(solution)/shard_map/pallas_call | solution.py:343
  21.8 8.9 %all-to-all-start = ((bf16[64,8,8,128]{3,2,1,0:T(8,128)(2,1)}), bf16[64,8,8,128]{3,2,1,0:T(8,128)(2,1)S(1)}, u32[]{:S(2)}, u32[]{:S(2)}) async-start(bf16[64,8,8,128]{3,2,1,0:T(8,128)(2,1)} %get-tuple-element.15), calls=%async_computation | async-start | bytes 2097152 | tf_op jit(solution)/shard_map/all_to_all | solution.py:349
  31.0 2.1 %collective-permute-start.6 = (bf16[64,1152]{1,0:T(8,128)(2,1)S(1)}, bf16[64,1152]{1,0:T(8,128)(2,1)S(1)}, u32[]{:S(2)}, u32[]{:S(2)}) collective-permute-start(bf16[64,1152]{1,0:T(8,128)(2,1)S(1)} %shard_map.149), channel_id=1, source_target_pairs={{0,64},{64,128},{128,192},{192,0},{1,65},{65,129},{129,193},{193,1... | collective-permute-start | bytes 442376 | tf_op jit(solution)/shard_map/ppermute | solution.py:310
  33.0 3.7 %collective-permute-start.7 = (bf16[64,1152]{1,0:T(8,128)(2,1)S(1)}, bf16[64,1152]{1,0:T(8,128)(2,1)S(1)}, u32[]{:S(2)}, u32[]{:S(2)}) collective-permute-start(bf16[64,1152]{1,0:T(8,128)(2,1)S(1)} %shard_map.149), channel_id=1, source_target_pairs={{0,128},{64,192},{128,0},{192,64},{1,129},{65,193},{129,1},{193,65... | collective-permute-start | bytes 442376 | tf_op jit(solution)/shard_map/ppermute | solution.py:310
  36.7 1.3 collective-permute-start.8
  38.7 13.8 %collective-permute-done.6 = bf16[64,1152]{1,0:T(8,128)(2,1)S(1)} collective-permute-done((bf16[64,1152]{1,0:T(8,128)(2,1)S(1)}, bf16[64,1152]{1,0:T(8,128)(2,1)S(1)}, u32[]{:S(2)}, u32[]{:S(2)}) %collective-permute-start.6) | collective-permute-done | bytes 147488 | tf_op jit(solution)/shard_map/ppermute | solution.py:310
  52.5 3.2 %collective-permute-done.7 = bf16[64,1152]{1,0:T(8,128)(2,1)S(1)} collective-permute-done((bf16[64,1152]{1,0:T(8,128)(2,1)S(1)}, bf16[64,1152]{1,0:T(8,128)(2,1)S(1)}, u32[]{:S(2)}, u32[]{:S(2)}) %collective-permute-start.7) | collective-permute-done | bytes 147488 | tf_op jit(solution)/shard_map/ppermute | solution.py:310
  55.8 1.4 collective-permute-start.9
  57.2 2.6 %collective-permute-start.10 = (bf16[256,1152]{1,0:T(8,128)(2,1)S(1)}, bf16[256,1152]{1,0:T(8,128)(2,1)S(1)}, u32[]{:S(2)}, u32[]{:S(2)}) collective-permute-start(bf16[256,1152]{1,0:T(8,128)(2,1)S(1)} %pad_maximum_fusion), channel_id=1, source_target_pairs={{0,32},{1,33},{2,34},{3,35},{4,36},{5,37},{6,38},{7,39},{8,40},{9,... | collective-permute-start | bytes 1769480 | tf_op jit(solution)/shard_map/ppermute | solution.py:365
  62.9 8.0 %collective-permute-done.9 = bf16[256,1152]{1,0:T(8,128)(2,1)S(1)} collective-permute-done((bf16[256,1152]{1,0:T(8,128)(2,1)S(1)}, bf16[256,1152]{1,0:T(8,128)(2,1)S(1)}, u32[]{:S(2)}, u32[]{:S(2)}) %collective-permute-start.9) | collective-permute-done | bytes 589856 | tf_op jit(solution)/shard_map/ppermute | solution.py:365
  71.8 12.8 %collective-permute-done.10 = bf16[256,1152]{1,0:T(8,128)(2,1)S(1)} collective-permute-done((bf16[256,1152]{1,0:T(8,128)(2,1)S(1)}, bf16[256,1152]{1,0:T(8,128)(2,1)S(1)}, u32[]{:S(2)}, u32[]{:S(2)}) %collective-permute-start.10) | collective-permute-done | bytes 589856 | tf_op jit(solution)/shard_map/ppermute | solution.py:365
  86.4 2.2 %collective-permute-start.12 = (bf16[1024,1152]{1,0:T(8,128)(2,1)}, bf16[1024,1152]{1,0:T(8,128)(2,1)}, u32[]{:S(2)}, u32[]{:S(2)}) collective-permute-start(bf16[1024,1152]{1,0:T(8,128)(2,1)} %constant_dynamic-update-slice_fusion.wa_ref), channel_id=1, source_target_pairs={{0,1},{1,0},{2,3},{3,2},{4,5},{5,4},{6,7},{7,6},{8,9},{9,8},{10,11... | collective-permute-start | bytes 7077896 | tf_op jit(solution)/shard_map/ppermute | solution.py:368
  92.8 5.7 %shard_map.147 = bf16[4096,128]{1,0:T(8,128)(2,1)} custom-call(bf16[4096,128]{1,0:T(8,128)(2,1)S(1)} %bitcast.8, bf16[512,512]{1,0:T(8,128)(2,1)S(1)} %copy-done.5, bf16[512,512]{1,0:T(8,128)(2,1)S(1)} %copy-done.6, f32[2,2,64,64]{3,2,1,0:T(8,128)S(1)} %copy-done.10, f32[2,2,64]{2,1,0:T(2,128)S(1)} %copy-done.13, f32[2,2,64,64]{3,2,1,0:T(8,128)S(1)} %copy-done.11, ...), custom_call_target="tpu_custom_call" | custom-call | tf_op jit(solution)/shard_map/pallas_call | solution.py:371
  98.5 8.5 %all-to-all-start.1 = ((bf16[64,8,8,128]{3,2,1,0:T(8,128)(2,1)}), bf16[64,8,8,128]{3,2,1,0:T(8,128)(2,1)S(1)}, u32[]{:S(2)}, u32[]{:S(2)}) async-start(bf16[64,8,8,128]{3,2,1,0:T(8,128)(2,1)} %bitcast.4), calls=%async_computation.1 | async-start | bytes 2097152 | tf_op jit(solution)/shard_map/all_to_all | solution.py:392
  107.0 17.9 %all-to-all-done.1.x_ref = bf16[64,8,8,128]{3,2,1,0:T(8,128)(2,1)S(1)} async-done(((bf16[64,8,8,128]{3,2,1,0:T(8,128)(2,1)}), bf16[64,8,8,128]{3,2,1,0:T(8,128)(2,1)S(1)}, u32[]{:S(2)}, u32[]{:S(2)}) %all-to-all-start.1) | async-done | bytes 1048608 | tf_op jit(solution)/shard_map/all_to_all | solution.py:392
  125.5 1.5 shard_map.148
  127.0 2.8 %collective-permute-start.3 = (bf16[1024,128]{1,0:T(8,128)(2,1)S(1)}, bf16[1024,128]{1,0:T(8,128)(2,1)S(1)}, u32[]{:S(2)}, u32[]{:S(2)}) collective-permute-start(bf16[1024,128]{1,0:T(8,128)(2,1)S(1)} %get-tuple-element.18), channel_id=1, source_target_pairs={{0,64},{64,128},{128,192},{192,0},{1,65},{65,129},{129,193},{193,1... | collective-permute-start | bytes 786440 | tf_op jit(solution)/shard_map/ppermute | solution.py:310
  129.8 1.7 collective-permute-start.4
  131.5 2.8 %collective-permute-start.5 = (bf16[1024,128]{1,0:T(8,128)(2,1)S(1)}, bf16[1024,128]{1,0:T(8,128)(2,1)S(1)}, u32[]{:S(2)}, u32[]{:S(2)}) collective-permute-start(bf16[1024,128]{1,0:T(8,128)(2,1)S(1)} %get-tuple-element.20), channel_id=1, source_target_pairs={{0,192},{64,0},{128,64},{192,128},{1,193},{65,1},{129,65},{193,129... | collective-permute-start | bytes 786440 | tf_op jit(solution)/shard_map/ppermute | solution.py:310
  134.3 8.7 %collective-permute-done.3.x1 = bf16[1024,128]{1,0:T(8,128)(2,1)S(1)} collective-permute-done((bf16[1024,128]{1,0:T(8,128)(2,1)S(1)}, bf16[1024,128]{1,0:T(8,128)(2,1)S(1)}, u32[]{:S(2)}, u32[]{:S(2)}) %collective-permute-start.3) | collective-permute-done | bytes 262176 | tf_op jit(solution)/shard_map/ppermute | solution.py:310
  143.1 7.5 %collective-permute-done.4.x2 = bf16[1024,128]{1,0:T(8,128)(2,1)S(1)} collective-permute-done((bf16[1024,128]{1,0:T(8,128)(2,1)S(1)}, bf16[1024,128]{1,0:T(8,128)(2,1)S(1)}, u32[]{:S(2)}, u32[]{:S(2)}) %collective-permute-start.4) | collective-permute-done | bytes 262176 | tf_op jit(solution)/shard_map/ppermute | solution.py:310
  150.5 5.9 %collective-permute-done.5.x3 = bf16[1024,128]{1,0:T(8,128)(2,1)S(1)} collective-permute-done((bf16[1024,128]{1,0:T(8,128)(2,1)S(1)}, bf16[1024,128]{1,0:T(8,128)(2,1)S(1)}, u32[]{:S(2)}, u32[]{:S(2)}) %collective-permute-start.5) | collective-permute-done | bytes 262176 | tf_op jit(solution)/shard_map/ppermute | solution.py:310
  156.4 9.5 %shard_map.150 = (bf16[1024,128]{1,0:T(8,128)(2,1)S(1)}, bf16[1024,128]{1,0:T(8,128)(2,1)S(1)}, bf16[1024,128]{1,0:T(8,128)(2,1)S(1)}, bf16[1024,128]{1,0:T(8,128)(2,1)S(1)}) custom-call(s32[1]{0:T(128)} %bitcast.me_ref, bf16[1024,128]{1,0:T(8,128)(2,1)S(1)} %get-tuple-element.17.x0, bf16[1024,128]{1,0:T(8,128)(2,1)S(1)} %collective-permute-done.3.x1, ...), custom_call_target="tpu_custom_call" | custom-call | tf_op jit(solution)/shard_map/pallas_call | solution.py:403
  165.9 2.7 %collective-permute-start.13 = (bf16[1024,128]{1,0:T(8,128)(2,1)S(1)}, bf16[1024,128]{1,0:T(8,128)(2,1)S(1)}, u32[]{:S(2)}, u32[]{:S(2)}) collective-permute-start(bf16[1024,128]{1,0:T(8,128)(2,1)S(1)} %get-tuple-element.22), channel_id=1, source_target_pairs={{0,64},{64,128},{128,192},{192,0},{1,65},{65,129},{129,193},{193,1... | collective-permute-start | bytes 786440 | tf_op jit(solution)/shard_map/ppermute | solution.py:310
  168.6 1.8 collective-permute-start.14
  170.3 2.8 %collective-permute-start.15 = (bf16[1024,128]{1,0:T(8,128)(2,1)S(1)}, bf16[1024,128]{1,0:T(8,128)(2,1)S(1)}, u32[]{:S(2)}, u32[]{:S(2)}) collective-permute-start(bf16[1024,128]{1,0:T(8,128)(2,1)S(1)} %get-tuple-element.24), channel_id=1, source_target_pairs={{0,192},{64,0},{128,64},{192,128},{1,193},{65,1},{129,65},{193,129... | collective-permute-start | bytes 786440 | tf_op jit(solution)/shard_map/ppermute | solution.py:310
  173.1 2.3 %collective-permute-done.13.x1 = bf16[1024,128]{1,0:T(8,128)(2,1)S(1)} collective-permute-done((bf16[1024,128]{1,0:T(8,128)(2,1)S(1)}, bf16[1024,128]{1,0:T(8,128)(2,1)S(1)}, u32[]{:S(2)}, u32[]{:S(2)}) %collective-permute-start.13) | collective-permute-done | bytes 262176 | tf_op jit(solution)/shard_map/ppermute | solution.py:310
  175.4 14.2 %collective-permute-done.14.x2 = bf16[1024,128]{1,0:T(8,128)(2,1)S(1)} collective-permute-done((bf16[1024,128]{1,0:T(8,128)(2,1)S(1)}, bf16[1024,128]{1,0:T(8,128)(2,1)S(1)}, u32[]{:S(2)}, u32[]{:S(2)}) %collective-permute-start.14) | collective-permute-done | bytes 262176 | tf_op jit(solution)/shard_map/ppermute | solution.py:310
  (58 shorter events, 17.1 us)
Async XLA Ops:
  0.0 1.2 copy-start
  1.9 28.8 %copy-start.18 = (bf16[512]{0:T(512)(128)(2,1)S(1)}, bf16[512]{0:T(512)(128)(2,1)}, u32[]{:S(2)}) copy-start(bf16[512]{0:T(512)(128)(2,1)} %param.23) | copy-start | bytes 3076
  1.9 28.9 %copy-start.2 = (bf16[512,512]{1,0:T(8,128)(2,1)S(1)}, bf16[512,512]{1,0:T(8,128)(2,1)}, u32[]{:S(2)}) copy-start(bf16[512,512]{1,0:T(8,128)(2,1)} %one_ref.1) | copy-start | bytes 1572868
  1.9 28.9 %copy-start.3 = (bf16[512,512]{1,0:T(8,128)(2,1)S(1)}, bf16[512,512]{1,0:T(8,128)(2,1)}, u32[]{:S(2)}) copy-start(bf16[512,512]{1,0:T(8,128)(2,1)} %two_ref.1) | copy-start | bytes 1572868
  2.8 11.3 %collective-permute-start = (f32[3,8,512]{2,1,0:T(8,128)S(1)}, f32[3,8,512]{2,1,0:T(8,128)S(1)}, u32[]{:S(2)}, u32[]{:S(2)}) collective-permute-start(f32[3,8,512]{2,1,0:T(8,128)S(1)} %shard_map.145.s0_ref.s0), channel_id=1, source_target_pairs={{0,64},{64,128},{128,192},{192,0},{1,65},{65,129},{129,193},{193,1... | collective-permute-start | bytes 147464 | tf_op jit(solution)/shard_map/ppermute | solution.py:310
  6.6 7.5 %collective-permute-start.1 = (f32[3,8,512]{2,1,0:T(8,128)S(1)}, f32[3,8,512]{2,1,0:T(8,128)S(1)}, u32[]{:S(2)}, u32[]{:S(2)}) collective-permute-start(f32[3,8,512]{2,1,0:T(8,128)S(1)} %shard_map.145.s0_ref.s0), channel_id=1, source_target_pairs={{0,128},{64,192},{128,0},{192,64},{1,129},{65,193},{129,1},{193,65... | collective-permute-start | bytes 147464 | tf_op jit(solution)/shard_map/ppermute | solution.py:310
  11.8 5.6 %collective-permute-start.2 = (f32[3,8,512]{2,1,0:T(8,128)S(1)}, f32[3,8,512]{2,1,0:T(8,128)S(1)}, u32[]{:S(2)}, u32[]{:S(2)}) collective-permute-start(f32[3,8,512]{2,1,0:T(8,128)S(1)} %shard_map.145.s0_ref.s0), channel_id=1, source_target_pairs={{0,192},{64,0},{128,64},{192,128},{1,193},{65,1},{129,65},{193,129... | collective-permute-start | bytes 147464 | tf_op jit(solution)/shard_map/ppermute | solution.py:310
  17.3 4.5 %copy-start.8 = (f32[3,8,512]{2,1,0:T(8,128)}, f32[3,8,512]{2,1,0:T(8,128)S(1)}, u32[]{:S(2)}) copy-start(f32[3,8,512]{2,1,0:T(8,128)S(1)} %collective-permute-done.2.s3_ref.s3) | copy-start | bytes 147460
  17.3 1.1 copy-start.7
  21.8 66.7 %all-to-all-start = ((bf16[64,8,8,128]{3,2,1,0:T(8,128)(2,1)}), bf16[64,8,8,128]{3,2,1,0:T(8,128)(2,1)S(1)}, u32[]{:S(2)}, u32[]{:S(2)}) async-start(bf16[64,8,8,128]{3,2,1,0:T(8,128)(2,1)} %get-tuple-element.15), calls=%async_computation | async-start | bytes 2097152 | tf_op jit(solution)/shard_map/all_to_all | solution.py:349
  31.0 21.6 %collective-permute-start.6 = (bf16[64,1152]{1,0:T(8,128)(2,1)S(1)}, bf16[64,1152]{1,0:T(8,128)(2,1)S(1)}, u32[]{:S(2)}, u32[]{:S(2)}) collective-permute-start(bf16[64,1152]{1,0:T(8,128)(2,1)S(1)} %shard_map.149), channel_id=1, source_target_pairs={{0,64},{64,128},{128,192},{192,0},{1,65},{65,129},{129,193},{193,1... | collective-permute-start | bytes 442376 | tf_op jit(solution)/shard_map/ppermute | solution.py:310
  33.0 22.7 %collective-permute-start.7 = (bf16[64,1152]{1,0:T(8,128)(2,1)S(1)}, bf16[64,1152]{1,0:T(8,128)(2,1)S(1)}, u32[]{:S(2)}, u32[]{:S(2)}) collective-permute-start(bf16[64,1152]{1,0:T(8,128)(2,1)S(1)} %shard_map.149), channel_id=1, source_target_pairs={{0,128},{64,192},{128,0},{192,64},{1,129},{65,193},{129,1},{193,65... | collective-permute-start | bytes 442376 | tf_op jit(solution)/shard_map/ppermute | solution.py:310
  36.7 19.1 %collective-permute-start.8 = (bf16[64,1152]{1,0:T(8,128)(2,1)S(1)}, bf16[64,1152]{1,0:T(8,128)(2,1)S(1)}, u32[]{:S(2)}, u32[]{:S(2)}) collective-permute-start(bf16[64,1152]{1,0:T(8,128)(2,1)S(1)} %shard_map.149), channel_id=1, source_target_pairs={{0,192},{64,0},{128,64},{192,128},{1,193},{65,1},{129,65},{193,129... | collective-permute-start | bytes 442376 | tf_op jit(solution)/shard_map/ppermute | solution.py:310
  55.8 32.7 %copy-start.5 = (bf16[512,512]{1,0:T(8,128)(2,1)S(1)}, bf16[512,512]{1,0:T(8,128)(2,1)}, u32[]{:S(2)}) copy-start(bf16[512,512]{1,0:T(8,128)(2,1)} %constant.46.clone.cos_hbm) | copy-start | bytes 1572868
  55.8 15.1 %collective-permute-start.9 = (bf16[256,1152]{1,0:T(8,128)(2,1)S(1)}, bf16[256,1152]{1,0:T(8,128)(2,1)S(1)}, u32[]{:S(2)}, u32[]{:S(2)}) collective-permute-start(bf16[256,1152]{1,0:T(8,128)(2,1)S(1)} %pad_maximum_fusion), channel_id=1, source_target_pairs={{0,16},{1,17},{2,18},{3,19},{4,20},{5,21},{6,22},{7,23},{8,24},{9,... | collective-permute-start | bytes 1769480 | tf_op jit(solution)/shard_map/ppermute | solution.py:365
  57.2 27.4 %collective-permute-start.10 = (bf16[256,1152]{1,0:T(8,128)(2,1)S(1)}, bf16[256,1152]{1,0:T(8,128)(2,1)S(1)}, u32[]{:S(2)}, u32[]{:S(2)}) collective-permute-start(bf16[256,1152]{1,0:T(8,128)(2,1)S(1)} %pad_maximum_fusion), channel_id=1, source_target_pairs={{0,32},{1,33},{2,34},{3,35},{4,36},{5,37},{6,38},{7,39},{8,40},{9,... | collective-permute-start | bytes 1769480 | tf_op jit(solution)/shard_map/ppermute | solution.py:365
  59.9 25.6 %collective-permute-start.11 = (bf16[256,1152]{1,0:T(8,128)(2,1)S(1)}, bf16[256,1152]{1,0:T(8,128)(2,1)S(1)}, u32[]{:S(2)}, u32[]{:S(2)}) collective-permute-start(bf16[256,1152]{1,0:T(8,128)(2,1)S(1)} %pad_maximum_fusion), channel_id=1, source_target_pairs={{0,48},{1,49},{2,50},{3,51},{4,52},{5,53},{6,54},{7,55},{8,56},{9,... | collective-permute-start | bytes 1769480 | tf_op jit(solution)/shard_map/ppermute | solution.py:365
  86.4 48.0 %collective-permute-start.12 = (bf16[1024,1152]{1,0:T(8,128)(2,1)}, bf16[1024,1152]{1,0:T(8,128)(2,1)}, u32[]{:S(2)}, u32[]{:S(2)}) collective-permute-start(bf16[1024,1152]{1,0:T(8,128)(2,1)} %constant_dynamic-update-slice_fusion.wa_ref), channel_id=1, source_target_pairs={{0,1},{1,0},{2,3},{3,2},{4,5},{5,4},{6,7},{7,6},{8,9},{9,8},{10,11... | collective-permute-start | bytes 7077896 | tf_op jit(solution)/shard_map/ppermute | solution.py:368
  88.5 1.0 copy-start.6
  89.6 0.9 copy-start.10
  90.5 0.9 copy-start.11
  92.7 32.1 %copy-start.1 = (bf16[8,512,128]{2,1,0:T(8,128)(2,1)S(1)}, bf16[8,512,128]{2,1,0:T(8,128)(2,1)}, u32[]{:S(2)}) copy-start(bf16[8,512,128]{2,1,0:T(8,128)(2,1)} %t_ref.1) | copy-start | bytes 3145732
  92.8 32.1 %copy-start.4 = (bf16[512,512]{1,0:T(8,128)(2,1)S(1)}, bf16[512,512]{1,0:T(8,128)(2,1)}, u32[]{:S(2)}) copy-start(bf16[512,512]{1,0:T(8,128)(2,1)} %constant.45.clone.table_hbm) | copy-start | bytes 1572868
  98.5 57.9 %copy-start.9 = (f32[3,8,512]{2,1,0:T(8,128)S(1)}, f32[3,8,512]{2,1,0:T(8,128)}, u32[]{:S(2)}) copy-start(f32[3,8,512]{2,1,0:T(8,128)} %copy-done.8) | copy-start | bytes 147460
  98.5 57.9 %copy-start.12 = (f32[512]{0:T(512)S(1)}, f32[512]{0:T(512)}, u32[]{:S(2)}) copy-start(f32[512]{0:T(512)} %param.21) | copy-start | bytes 6148
  98.5 26.4 %all-to-all-start.1 = ((bf16[64,8,8,128]{3,2,1,0:T(8,128)(2,1)}), bf16[64,8,8,128]{3,2,1,0:T(8,128)(2,1)S(1)}, u32[]{:S(2)}, u32[]{:S(2)}) async-start(bf16[64,8,8,128]{3,2,1,0:T(8,128)(2,1)} %bitcast.4), calls=%async_computation.1 | async-start | bytes 2097152 | tf_op jit(solution)/shard_map/all_to_all | solution.py:392
  127.0 16.0 %collective-permute-start.3 = (bf16[1024,128]{1,0:T(8,128)(2,1)S(1)}, bf16[1024,128]{1,0:T(8,128)(2,1)S(1)}, u32[]{:S(2)}, u32[]{:S(2)}) collective-permute-start(bf16[1024,128]{1,0:T(8,128)(2,1)S(1)} %get-tuple-element.18), channel_id=1, source_target_pairs={{0,64},{64,128},{128,192},{192,0},{1,65},{65,129},{129,193},{193,1... | collective-permute-start | bytes 786440 | tf_op jit(solution)/shard_map/ppermute | solution.py:310
  129.8 20.7 %collective-permute-start.4 = (bf16[1024,128]{1,0:T(8,128)(2,1)S(1)}, bf16[1024,128]{1,0:T(8,128)(2,1)S(1)}, u32[]{:S(2)}, u32[]{:S(2)}) collective-permute-start(bf16[1024,128]{1,0:T(8,128)(2,1)S(1)} %get-tuple-element.19), channel_id=1, source_target_pairs={{0,128},{64,192},{128,0},{192,64},{1,129},{65,193},{129,1},{193,65... | collective-permute-start | bytes 786440 | tf_op jit(solution)/shard_map/ppermute | solution.py:310
  131.5 24.9 %collective-permute-start.5 = (bf16[1024,128]{1,0:T(8,128)(2,1)S(1)}, bf16[1024,128]{1,0:T(8,128)(2,1)S(1)}, u32[]{:S(2)}, u32[]{:S(2)}) collective-permute-start(bf16[1024,128]{1,0:T(8,128)(2,1)S(1)} %get-tuple-element.20), channel_id=1, source_target_pairs={{0,192},{64,0},{128,64},{192,128},{1,193},{65,1},{129,65},{193,129... | collective-permute-start | bytes 786440 | tf_op jit(solution)/shard_map/ppermute | solution.py:310
  165.9 9.6 %collective-permute-start.13 = (bf16[1024,128]{1,0:T(8,128)(2,1)S(1)}, bf16[1024,128]{1,0:T(8,128)(2,1)S(1)}, u32[]{:S(2)}, u32[]{:S(2)}) collective-permute-start(bf16[1024,128]{1,0:T(8,128)(2,1)S(1)} %get-tuple-element.22), channel_id=1, source_target_pairs={{0,64},{64,128},{128,192},{192,0},{1,65},{65,129},{129,193},{193,1... | collective-permute-start | bytes 786440 | tf_op jit(solution)/shard_map/ppermute | solution.py:310
  168.6 21.0 %collective-permute-start.14 = (bf16[1024,128]{1,0:T(8,128)(2,1)S(1)}, bf16[1024,128]{1,0:T(8,128)(2,1)S(1)}, u32[]{:S(2)}, u32[]{:S(2)}) collective-permute-start(bf16[1024,128]{1,0:T(8,128)(2,1)S(1)} %get-tuple-element.23), channel_id=1, source_target_pairs={{0,128},{64,192},{128,0},{192,64},{1,129},{65,193},{129,1},{193,65... | collective-permute-start | bytes 786440 | tf_op jit(solution)/shard_map/ppermute | solution.py:310
  170.3 19.3 %collective-permute-start.15 = (bf16[1024,128]{1,0:T(8,128)(2,1)S(1)}, bf16[1024,128]{1,0:T(8,128)(2,1)S(1)}, u32[]{:S(2)}, u32[]{:S(2)}) collective-permute-start(bf16[1024,128]{1,0:T(8,128)(2,1)S(1)} %get-tuple-element.24), channel_id=1, source_target_pairs={{0,192},{64,0},{128,64},{192,128},{1,193},{65,1},{129,65},{193,129... | collective-permute-start | bytes 786440 | tf_op jit(solution)/shard_map/ppermute | solution.py:310
  (5 other events, 3.3 us)
where the time goes:
time: 193 us; the launch traced here: 191 us
  waiting for transfers between devices  97.5 us (51%)
  starting transfers between devices  57.6 us (30%)
  Pallas kernels  21.6 us (11%)
  local copies, waits for them, and re-layouts  13.8 us (7%)
    ppermute x12, waiting for transfers between devices, shifts(): lax.ppermute(value_of(shift), axis, [(i, (i + shift) % ways) for i in ran...  58.7 us
    ppermute x12, starting transfers between devices, shifts(): lax.ppermute(value_of(shift), axis, [(i, (i + shift) % ways) for i in ran...  33 us
    ppermute x3, waiting for transfers between devices, local(): lax.ppermute(stage, 'rows', [(i, (i + shift * per_x) % owners) for i in r...  20.8 us
    all_to_all x1, waiting for transfers between devices, local(): lax.all_to_all(back.reshape(owners, rows, 2 * per_owner, lanes), 'rows',...  17.9 us
    unnamed x44, local copies, waits for them, and re-layouts  12.9 us
    pallas_call x1, Pallas kernels, local(): call(partial(mlp_kernel, 256), [shape((share, lanes), bf16)] * ways, [sme...  9.47 us
    all_to_all x1, starting transfers between devices, local(): columns = lax.all_to_all(spectra, 'rows', split_axis=0, concat_axis=0)  8.86 us
    all_to_all x1, starting transfers between devices, local(): lax.all_to_all(back.reshape(owners, rows, 2 * per_owner, lanes), 'rows',...  8.48 us
  transfers between devices with their start and end apart: 18, of which 11 were waited for; matrix products, arithmetic and copies ran while one was open for 3% of the time, Pallas kernels for 4%

commit v1 on v0

--- a/solution.py
+++ b/solution.py
@@ -177,7 +177,7 @@
     *o_refs, table_ref, sem = refs
     fetch = pltpu.make_async_copy(table_hbm, table_ref, sem)
     fetch.start()
-    ways = len(o_refs)
+    ways = len(o_refs) // 2
     rows, width, lanes = t_ref.shape
     group = rows // ways
     me = me_ref[0]
@@ -199,7 +199,7 @@
                 center = jnp.sum(jnp.where(column == row, f_ref[...], 0.0), axis=1, keepdims=True)
                 factor = jnp.sum(jnp.where(column == row + rows, f_ref[...], 0.0), axis=1, keepdims=True)
                 normed = (source - center) * factor * gain
-                o_refs[shift][pl.ds((2 * pair + side) * width, width), :] = (
+                o_refs[side * ways + shift][pl.ds(pair * width, width), :] = (
                     (out[:, side * lanes : (side + 1) * lanes] + normed) + source
                 ).astype(bf16)
 
@@ -257,28 +257,49 @@
         ref[...] = y_ref[lax.rem(me + shift, ways)]
 
 
-def place_kernel(me_ref, x0, x1, x2, x3, o_ref):
+def place_kernel(me_ref, *refs):
+    *parts, o_ref = refs
     ways = o_ref.shape[0]
-    for shift, ref in enumerate((x0, x1, x2, x3)):
-        o_ref[lax.rem(me_ref[0] + ways - shift, ways)] = ref[...]
+    half = o_ref.shape[1] // 2
+    for place, part in enumerate(parts):
+        shift = place % ways
+        o_ref[lax.rem(me_ref[0] + ways - shift, ways), pl.ds(place // ways * half, half), :] = part[...]
 
 
 def piece_kernel(piece_ref, one_ref, bias_ref, two_ref, o_ref, flat_ref):
-    units, columns = o_ref.shape
     channels = one_ref.shape[0]
-    lanes = columns - 2 * channels
-    piece = piece_ref[0]
-    slab = pl.ds(pl.multiple_of(piece * units // lanes * lanes, lanes), lanes)
+    units = o_ref.shape[0] // 2
+    lanes = o_ref.shape[1] - 2 * channels
     row = lax.broadcasted_iota(jnp.int32, (lanes, lanes), 0)
     column = lax.broadcasted_iota(jnp.int32, (lanes, lanes), 1)
     unit = jnp.where(row == column, 1.0, 0.0).astype(bf16)
-    flat_ref[:, 0:channels] = mm_t(unit, one_ref[:, slab])
-    bias = jnp.where(row == column, jnp.broadcast_to(bias_ref[:, slab].astype(f32), (lanes, lanes)), 0.0)
-    flat_ref[:, channels:] = bias
-    within = pl.ds(pl.multiple_of(lax.rem(piece * units, lanes), units), units)
-    o_ref[:, 0:channels] = flat_ref[within, 0:channels].astype(bf16)
-    o_ref[:, channels : 2 * channels] = two_ref[pl.ds(pl.multiple_of(piece * units, units), units), :]
-    o_ref[:, 2 * channels :] = flat_ref[within, channels:].astype(bf16)
+    for half in range(2):
+        first = half * (one_ref.shape[1] // 2) + piece_ref[half] * units
+        slab = pl.ds(pl.multiple_of(first // lanes * lanes, lanes), lanes)
+        bias = jnp.broadcast_to(bias_ref[:, slab].astype(f32), (lanes, lanes))
+        flat_ref[:, 0:channels] = mm_t(unit, one_ref[:, slab])
+        flat_ref[:, channels:] = jnp.where(row == column, bias, 0.0)
+        within = pl.ds(pl.multiple_of(lax.rem(first, lanes), units), units)
+        target = pl.ds(half * units, units)
+        o_ref[target, 0:channels] = flat_ref[within, 0:channels].astype(bf16)
+        o_ref[target, channels : 2 * channels] = two_ref[pl.ds(pl.multiple_of(first, units), units), :]
+        o_ref[target, 2 * channels :] = flat_ref[within, channels:].astype(bf16)
+
+
+def split_kernel(*refs):
+    *parts, first_ref, second_ref = refs
+    size = parts[0].shape[0] // 2
+    for place, part in enumerate(parts):
+        for half, ref in enumerate((first_ref, second_ref)):
+            ref[place * size : (place + 1) * size, :] = part[half * size : (half + 1) * size, :]
+
+
+def join_kernel(*refs):
+    *parts, after_ref, o_ref = refs
+    start = 0
+    for part in parts:
+        o_ref[start : start + part.shape[0], :] = part[...]
+        start += part.shape[0]
 
 
 def vmem(count):
@@ -348,24 +369,30 @@
     )(tokens, stats, *others, gain_in.reshape(1, lanes), forward)
     columns = lax.all_to_all(spectra, "rows", split_axis=0, concat_axis=0)
 
-    ring_x, per_x = 4, owners // 4
+    ring_x, ring_y, per_x = 4, 4, owners // 4
     place = lax.axis_index("rows").astype(jnp.int32)
     units = fc1_weight.shape[1] // (2 * ring_x)
-    piece = ((place // per_x) * 2 + place % 2).reshape(1)
+    across, along, core = place // per_x, place // 2 % ring_y, place % 2
+    piece = jnp.stack([across * 2 + core, along * 2 + core])
     mine = call(
         piece_kernel,
         shape((units, 2 * channels + lanes), bf16),
         [smem] + vmem(3),
         scratch=[pltpu.VMEM((lanes, channels + lanes), f32)],
     )(piece, fc1_weight, fc1_bias.reshape(1, -1), fc2_weight)
-    stage = jnp.concatenate([mine] + shifts(lambda s: mine, "chan", ways), axis=0)
-    parts = [stage]
+    stage = [mine] + shifts(lambda s: mine, "chan", ways)
+    count = ways * units // 2
+    sides = call(
+        split_kernel, [shape((count, mine.shape[1]), bf16)] * 2, vmem(ways)
+    )(*stage)
+    parts = list(sides)
     for shift in range(1, ring_x):
-        parts.append(
-            lax.ppermute(stage, "rows", [(i, (i + shift * per_x) % owners) for i in range(owners)])
-        )
-    near = jnp.concatenate(parts, axis=0)
-    far = lax.ppermute(near, "rows", [(i, i ^ 1) for i in range(owners)])
+        ring = [
+            [(i, (i + shift * per_x) % owners) for i in range(owners)],
+            [(i, i + 2 * ((i // 2 % ring_y + shift) % ring_y - i // 2 % ring_y)) for i in range(owners)],
+        ]
+        for half in range(2):
+            parts.append(lax.ppermute(sides[half], "rows", ring[half]))
 
     total = owners * rows * 2 * per_owner
     back = call(
@@ -392,26 +419,42 @@
     returned = lax.all_to_all(
         back.reshape(owners, rows, 2 * per_owner, lanes), "rows", split_axis=0, concat_axis=0
     )
-    share = rows // ways * width
+    share = rows // ways * width // 2
     mixed = call(
         partial(inverse_kernel, first_scale),
-        [shape((share, lanes), bf16)] * ways,
+        [shape((share, lanes), bf16)] * (2 * ways),
         [smem] + vmem(1) + [hbm] + vmem(3),
         scratch=[pltpu.VMEM(inverse.shape, bf16), pltpu.SemaphoreType.DMA],
     )(me, returned, inverse, tokens, flipped, gain_in.reshape(1, lanes))
-    whole = [mixed[0]] + shifts(lambda s: mixed[s], "chan", ways)
-    result = call(
-        partial(mlp_kernel, 256),
-        [shape((share, lanes), bf16)] * ways,
-        [smem] + vmem(11),
-        scratch=[
-            pltpu.VMEM((ways, share, lanes), bf16),
-            pltpu.VMEM((ways, share, lanes), bf16),
-            pltpu.VMEM((ways, lanes), f32),
-        ],
-    )(me, *whole, near, far, gain_out.reshape(1, channels), stats, *others)
-    parts = [result[0]] + shifts(lambda s: result[s], "chan", ways)
-    final = call(place_kernel, shape((ways, share, lanes), bf16), [smem] + vmem(4))(me, *parts)
+    halves = [mixed[:ways], mixed[ways:]]
+    whole_a = [halves[0][0]] + shifts(lambda s: halves[0][s], "chan", ways)
+    near = call(
+        join_kernel,
+        shape((2 * ring_x * parts[0].shape[0], parts[0].shape[1]), bf16),
+        vmem(len(parts)) + [pl.BlockSpec(memory_space=pl.ANY)],
+    )(*parts, mixed[0])
+    far = lax.ppermute(near, "rows", [(i, i ^ 1) for i in range(owners)])
+    whole_b = [halves[1][0]] + shifts(lambda s: halves[1][s], "chan", ways)
+
+    def mlp(whole):
+        return call(
+            partial(mlp_kernel, 256),
+            [shape((share, lanes), bf16)] * ways,
+            [smem] + vmem(11),
+            scratch=[
+                pltpu.VMEM((ways, share, lanes), bf16),
+                pltpu.VMEM((ways, share, lanes), bf16),
+                pltpu.VMEM((ways, lanes), f32),
+            ],
+        )(me, *whole, near, far, gain_out.reshape(1, channels), stats, *others)
+
+    result_a = mlp(whole_a)
+    parts_a = [result_a[0]] + shifts(lambda s: result_a[s], "chan", ways)
+    result_b = mlp(whole_b)
+    parts_b = [result_b[0]] + shifts(lambda s: result_b[s], "chan", ways)
+    final = call(place_kernel, shape((ways, 2 * share, lanes), bf16), [smem] + vmem(2 * ways))(
+        me, *parts_a, *parts_b
+    )
     return final.reshape(rows, width, lanes)
 
 

time: 193 us -> 172 us (0.89)
  the two profiles are of different devices: /device:TPU:1 before, /device:TPU:38 now
where the time goes in v1:
time: 172 us
  waiting for transfers between devices  61.7 us (36%)
  starting transfers between devices  60 us (35%)
  blocking collectives  23.5 us (14%)
  Pallas kernels  20.7 us (12%)
  local copies, waits for them, and re-layouts  5.63 us (3%)
    ppermute x18, waiting for transfers between devices, shifts(): lax.ppermute(value_of(shift), axis, [(i, (i + shift) % ways) for i in ran...  50.1 us
    ppermute x18, starting transfers between devices, shifts(): lax.ppermute(value_of(shift), axis, [(i, (i + shift) % ways) for i in ran...  42.8 us
    all_to_all x1, blocking collectives, local(): columns = lax.all_to_all(spectra, 'rows', split_axis=0, concat_axis=0)  23.5 us
    ppermute x6, waiting for transfers between devices, local(): parts.append(lax.ppermute(sides[half], 'rows', ring[half]))  11.5 us
    ppermute x6, starting transfers between devices, local(): parts.append(lax.ppermute(sides[half], 'rows', ring[half]))  8.97 us
    all_to_all x1, starting transfers between devices, local(): lax.all_to_all(back.reshape(owners, rows, 2 * per_owner, lanes), 'rows',...  8.13 us
    pallas_call x2, Pallas kernels, mlp(): call(partial(mlp_kernel, 256), [shape((share, lanes), bf16)] * ways, [sme...  7.41 us
    pallas_call x1, Pallas kernels, local(): call(partial(column_kernel, second_scale), shape((total, lanes), bf16), v...  5.69 us
  transfers between devices with their start and end apart: 26, of which 9 were waited for; matrix products, arithmetic and copies ran while one was open for 0% of the time, Pallas kernels for 6%

profile of v1, /device:TPU:38, one launch (start us, length us, event | category | flops | bytes accessed | tf_op | source)
XLA Modules:
  0.0 172.0 jit_solution(954619323437412964)
XLA Ops:
  2.8 5.4 %collective-permute-start.2 = (f32[3,8,512]{2,1,0:T(8,128)S(1)}, f32[3,8,512]{2,1,0:T(8,128)S(1)}, u32[]{:S(2)}, u32[]{:S(2)}) collective-permute-start(f32[3,8,512]{2,1,0:T(8,128)S(1)} %shard_map.145.s0_ref.s0), channel_id=1, source_target_pairs={{0,192},{64,0},{128,64},{192,128},{1,193},{65,1},{129,65},{193,129... | collective-permute-start | bytes 147464 | tf_op jit(solution)/shard_map/ppermute | solution.py:331
  8.2 1.4 collective-permute-start.1
  9.7 2.4 %collective-permute-start = (f32[3,8,512]{2,1,0:T(8,128)S(1)}, f32[3,8,512]{2,1,0:T(8,128)S(1)}, u32[]{:S(2)}, u32[]{:S(2)}) collective-permute-start(f32[3,8,512]{2,1,0:T(8,128)S(1)} %shard_map.145.s0_ref.s0), channel_id=1, source_target_pairs={{0,64},{64,128},{128,192},{192,0},{1,65},{65,129},{129,193},{193,1... | collective-permute-start | bytes 147464 | tf_op jit(solution)/shard_map/ppermute | solution.py:331
  12.1 4.2 %collective-permute-done.1.s2_ref.s2 = f32[3,8,512]{2,1,0:T(8,128)S(1)} collective-permute-done((f32[3,8,512]{2,1,0:T(8,128)S(1)}, f32[3,8,512]{2,1,0:T(8,128)S(1)}, u32[]{:S(2)}, u32[]{:S(2)}) %collective-permute-start.1) | collective-permute-done | bytes 49184 | tf_op jit(solution)/shard_map/ppermute | solution.py:331
  18.8 1.8 %shard_map.146 = (bf16[64,8,8,128]{3,2,1,0:T(8,128)(2,1)S(1)}, f32[512,16]{1,0:T(8,128)S(1)}) custom-call(bf16[8,512,128]{2,1,0:T(8,128)(2,1)S(1)} %copy-done, f32[3,8,512]{2,1,0:T(8,128)S(1)} %shard_map.145.s0_ref.s0, f32[3,8,512]{2,1,0:T(8,128)S(1)} %collective-permute-done.s1_ref.s1, f32[3,8,512]{2,1,0:T(8,128)S(1)} %collective-permute-done.1.s2_ref.s2, ...), custom_call_target="tpu_custom_call" | custom-call | tf_op jit(solution)/shard_map/pallas_call | solution.py:364
  20.6 23.5 %all_to_all.10 = bf16[64,8,8,128]{3,2,1,0:T(8,128)(2,1)S(1)} all-to-all(bf16[64,8,8,128]{3,2,1,0:T(8,128)(2,1)S(1)} %get-tuple-element.25), channel_id=1, replica_groups=mesh['chan'=4,'rows'=64] {'rows'}, dimensions={0} | all-to-all | bytes 2097152 | tf_op jit(solution)/shard_map/all_to_all | solution.py:370
  44.2 5.7 %shard_map.147 = bf16[4096,128]{1,0:T(8,128)(2,1)} custom-call(bf16[4096,128]{1,0:T(8,128)(2,1)S(1)} %bitcast.9, bf16[512,512]{1,0:T(8,128)(2,1)S(1)} %copy-done.7, bf16[512,512]{1,0:T(8,128)(2,1)S(1)} %copy-done.6, f32[2,2,64,64]{3,2,1,0:T(8,128)S(1)} %copy-done.10, f32[2,2,64]{2,1,0:T(2,128)S(1)} %copy-done.13, f32[2,2,64,64]{3,2,1,0:T(8,128)S(1)} %copy-done.11, ...), custom_call_target="tpu_custom_call" | custom-call | tf_op jit(solution)/shard_map/pallas_call | solution.py:398
  50.0 8.1 %all-to-all-start.1 = ((bf16[64,8,8,128]{3,2,1,0:T(8,128)(2,1)}), bf16[64,8,8,128]{3,2,1,0:T(8,128)(2,1)S(1)}, u32[]{:S(2)}, u32[]{:S(2)}) async-start(bf16[64,8,8,128]{3,2,1,0:T(8,128)(2,1)} %bitcast.4), calls=%async_computation.1 | async-start | bytes 2097152 | tf_op jit(solution)/shard_map/all_to_all | solution.py:419
  59.0 2.1 %collective-permute-start.8 = (bf16[64,1152]{1,0:T(8,128)(2,1)S(1)}, bf16[64,1152]{1,0:T(8,128)(2,1)S(1)}, u32[]{:S(2)}, u32[]{:S(2)}) collective-permute-start(bf16[64,1152]{1,0:T(8,128)(2,1)S(1)} %shard_map.149.refs_0_), channel_id=1, source_target_pairs={{0,192},{64,0},{128,64},{192,128},{1,193},{65,1},{129,65},{193,129... | collective-permute-start | bytes 442376 | tf_op jit(solution)/shard_map/ppermute | solution.py:331
  61.1 2.1 %collective-permute-start.7 = (bf16[64,1152]{1,0:T(8,128)(2,1)S(1)}, bf16[64,1152]{1,0:T(8,128)(2,1)S(1)}, u32[]{:S(2)}, u32[]{:S(2)}) collective-permute-start(bf16[64,1152]{1,0:T(8,128)(2,1)S(1)} %shard_map.149.refs_0_), channel_id=1, source_target_pairs={{0,128},{64,192},{128,0},{192,64},{1,129},{65,193},{129,1},{193,65... | collective-permute-start | bytes 442376 | tf_op jit(solution)/shard_map/ppermute | solution.py:331
  63.2 2.8 %collective-permute-start.6 = (bf16[64,1152]{1,0:T(8,128)(2,1)S(1)}, bf16[64,1152]{1,0:T(8,128)(2,1)S(1)}, u32[]{:S(2)}, u32[]{:S(2)}) collective-permute-start(bf16[64,1152]{1,0:T(8,128)(2,1)S(1)} %shard_map.149.refs_0_), channel_id=1, source_target_pairs={{0,64},{64,128},{128,192},{192,0},{1,65},{65,129},{129,193},{193,1... | collective-permute-start | bytes 442376 | tf_op jit(solution)/shard_map/ppermute | solution.py:331
  66.0 13.7 %collective-permute-done.8.refs_3_ = bf16[64,1152]{1,0:T(8,128)(2,1)S(1)} collective-permute-done((bf16[64,1152]{1,0:T(8,128)(2,1)S(1)}, bf16[64,1152]{1,0:T(8,128)(2,1)S(1)}, u32[]{:S(2)}, u32[]{:S(2)}) %collective-permute-start.8) | collective-permute-done | bytes 147488 | tf_op jit(solution)/shard_map/ppermute | solution.py:331
  79.7 7.0 %collective-permute-done.7.refs_2_ = bf16[64,1152]{1,0:T(8,128)(2,1)S(1)} collective-permute-done((bf16[64,1152]{1,0:T(8,128)(2,1)S(1)}, bf16[64,1152]{1,0:T(8,128)(2,1)S(1)}, u32[]{:S(2)}, u32[]{:S(2)}) %collective-permute-start.7) | collective-permute-done | bytes 147488 | tf_op jit(solution)/shard_map/ppermute | solution.py:331
  88.6 2.1 %collective-permute-start.9 = (bf16[128,1152]{1,0:T(8,128)(2,1)S(1)}, bf16[128,1152]{1,0:T(8,128)(2,1)}, u32[]{:S(2)}, u32[]{:S(2)}) collective-permute-start(bf16[128,1152]{1,0:T(8,128)(2,1)S(1)} %get-tuple-element.31.refs_0_), channel_id=1, source_target_pairs={{0,16},{1,17},{2,18},{3,19},{4,20},{5,21},{6,22},{7,23},{8,24},{9,... | collective-permute-start | bytes 884744 | tf_op jit(solution)/shard_map/ppermute | solution.py:395
  90.7 2.7 %collective-permute-start.14 = (bf16[128,1152]{1,0:T(8,128)(2,1)S(1)}, bf16[128,1152]{1,0:T(8,128)(2,1)}, u32[]{:S(2)}, u32[]{:S(2)}) collective-permute-start(bf16[128,1152]{1,0:T(8,128)(2,1)S(1)} %get-tuple-element.32.refs_1_), channel_id=1, source_target_pairs={{0,6},{1,7},{2,0},{3,1},{4,2},{5,3},{6,4},{7,5},{8,14},{9,15},{10,... | collective-permute-start | bytes 884744 | tf_op jit(solution)/shard_map/ppermute | solution.py:395
  94.3 8.6 %collective-permute-done.13.refs_6_ = bf16[128,1152]{1,0:T(8,128)(2,1)S(1)} collective-permute-done((bf16[128,1152]{1,0:T(8,128)(2,1)S(1)}, bf16[128,1152]{1,0:T(8,128)(2,1)S(1)}, u32[]{:S(2)}, u32[]{:S(2)}) %collective-permute-start.13) | collective-permute-done | bytes 294944 | tf_op jit(solution)/shard_map/ppermute | solution.py:395
  102.8 1.5 collective-permute-start.10
  106.3 1.5 shard_map.148
  107.9 3.0 %collective-permute-done.10.refs_3_ = bf16[128,1152]{1,0:T(8,128)(2,1)} collective-permute-done((bf16[128,1152]{1,0:T(8,128)(2,1)S(1)}, bf16[128,1152]{1,0:T(8,128)(2,1)}, u32[]{:S(2)}, u32[]{:S(2)}) %collective-permute-start.10) | collective-permute-done | bytes 294944 | tf_op jit(solution)/shard_map/ppermute | solution.py:395
  110.9 1.5 shard_map.151.wa_ref
  112.6 2.1 %collective-permute-start.20 = (bf16[512,128]{1,0:T(8,128)(2,1)S(1)}, bf16[512,128]{1,0:T(8,128)(2,1)S(1)}, u32[]{:S(2)}, u32[]{:S(2)}) collective-permute-start(bf16[512,128]{1,0:T(8,128)(2,1)S(1)} %get-tuple-element.39), channel_id=1, source_target_pairs={{0,128},{64,192},{128,0},{192,64},{1,129},{65,193},{129,1},{193,65... | collective-permute-start | bytes 393224 | tf_op jit(solution)/shard_map/ppermute | solution.py:331
  114.7 4.0 %collective-permute-start.21 = (bf16[512,128]{1,0:T(8,128)(2,1)S(1)}, bf16[512,128]{1,0:T(8,128)(2,1)S(1)}, u32[]{:S(2)}, u32[]{:S(2)}) collective-permute-start(bf16[512,128]{1,0:T(8,128)(2,1)S(1)} %get-tuple-element.40), channel_id=1, source_target_pairs={{0,192},{64,0},{128,64},{192,128},{1,193},{65,1},{129,65},{193,129... | collective-permute-start | bytes 393224 | tf_op jit(solution)/shard_map/ppermute | solution.py:331
  119.1 18.2 %collective-permute-done.19.x1 = bf16[512,128]{1,0:T(8,128)(2,1)S(1)} collective-permute-done((bf16[512,128]{1,0:T(8,128)(2,1)S(1)}, bf16[512,128]{1,0:T(8,128)(2,1)S(1)}, u32[]{:S(2)}, u32[]{:S(2)}) %collective-permute-start.19) | collective-permute-done | bytes 131104 | tf_op jit(solution)/shard_map/ppermute | solution.py:331
  137.3 1.2 collective-permute-start.5
  138.5 3.7 %shard_map.153 = (bf16[512,128]{1,0:T(8,128)(2,1)S(1)}, bf16[512,128]{1,0:T(8,128)(2,1)S(1)}, bf16[512,128]{1,0:T(8,128)(2,1)S(1)}, bf16[512,128]{1,0:T(8,128)(2,1)S(1)}) custom-call(s32[1]{0:T(128)} %bitcast.me_ref, bf16[512,128]{1,0:T(8,128)(2,1)S(1)} %get-tuple-element.37.x0, bf16[512,128]{1,0:T(8,128)(2,1)S(1)} %collective-permute-done.19.x1, ...), custom_call_target="tpu_custom_call" | custom-call | tf_op jit(solution)/shard_map/pallas_call | solution.py:440
  142.2 1.8 %collective-permute-start.22 = (bf16[512,128]{1,0:T(8,128)(2,1)S(1)}, bf16[512,128]{1,0:T(8,128)(2,1)S(1)}, u32[]{:S(2)}, u32[]{:S(2)}) collective-permute-start(bf16[512,128]{1,0:T(8,128)(2,1)S(1)} %get-tuple-element.42), channel_id=1, source_target_pairs={{0,64},{64,128},{128,192},{192,0},{1,65},{65,129},{129,193},{193,1... | collective-permute-start | bytes 393224 | tf_op jit(solution)/shard_map/ppermute | solution.py:331
  144.0 5.9 %collective-permute-start.23 = (bf16[512,128]{1,0:T(8,128)(2,1)S(1)}, bf16[512,128]{1,0:T(8,128)(2,1)S(1)}, u32[]{:S(2)}, u32[]{:S(2)}) collective-permute-start(bf16[512,128]{1,0:T(8,128)(2,1)S(1)} %get-tuple-element.43), channel_id=1, source_target_pairs={{0,128},{64,192},{128,0},{192,64},{1,129},{65,193},{129,1},{193,65... | collective-permute-start | bytes 393224 | tf_op jit(solution)/shard_map/ppermute | solution.py:331
  149.9 1.2 collective-permute-start.24
  151.2 3.7 %shard_map.152 = (bf16[512,128]{1,0:T(8,128)(2,1)S(1)}, bf16[512,128]{1,0:T(8,128)(2,1)S(1)}, bf16[512,128]{1,0:T(8,128)(2,1)S(1)}, bf16[512,128]{1,0:T(8,128)(2,1)S(1)}) custom-call(s32[1]{0:T(128)} %bitcast.me_ref, bf16[512,128]{1,0:T(8,128)(2,1)S(1)} %get-tuple-element.27.refs_8_.x0, bf16[512,128]{1,0:T(8,128)(2,1)S(1)} %collective-permute-done.3.x1, ...), custom_call_target="tpu_custom_call" | custom-call | tf_op jit(solution)/shard_map/pallas_call | solution.py:440
  154.9 6.2 %collective-permute-start.16 = (bf16[512,128]{1,0:T(8,128)(2,1)S(1)}, bf16[512,128]{1,0:T(8,128)(2,1)S(1)}, u32[]{:S(2)}, u32[]{:S(2)}) collective-permute-start(bf16[512,128]{1,0:T(8,128)(2,1)S(1)} %get-tuple-element.34), channel_id=1, source_target_pairs={{0,64},{64,128},{128,192},{192,0},{1,65},{65,129},{129,193},{193,1... | collective-permute-start | bytes 393224 | tf_op jit(solution)/shard_map/ppermute | solution.py:331
  161.1 3.7 %collective-permute-start.18 = (bf16[512,128]{1,0:T(8,128)(2,1)S(1)}, bf16[512,128]{1,0:T(8,128)(2,1)S(1)}, u32[]{:S(2)}, u32[]{:S(2)}) collective-permute-start(bf16[512,128]{1,0:T(8,128)(2,1)S(1)} %get-tuple-element.36), channel_id=1, source_target_pairs={{0,192},{64,0},{128,64},{192,128},{1,193},{65,1},{129,65},{193,129... | collective-permute-start | bytes 393224 | tf_op jit(solution)/shard_map/ppermute | solution.py:331
  164.8 5.6 %collective-permute-done.17.refs_2_ = bf16[512,128]{1,0:T(8,128)(2,1)S(1)} collective-permute-done((bf16[512,128]{1,0:T(8,128)(2,1)S(1)}, bf16[512,128]{1,0:T(8,128)(2,1)S(1)}, u32[]{:S(2)}, u32[]{:S(2)}) %collective-permute-start.17) | collective-permute-done | bytes 131104 | tf_op jit(solution)/shard_map/ppermute | solution.py:331
  (71 shorter events, 13.2 us)
Async XLA Ops:
  1.9 42.3 %copy-start.6 = (bf16[512,512]{1,0:T(8,128)(2,1)S(1)}, bf16[512,512]{1,0:T(8,128)(2,1)}, u32[]{:S(2)}) copy-start(bf16[512,512]{1,0:T(8,128)(2,1)} %constant.64.clone.sin_hbm) | copy-start | bytes 1572868
  1.9 42.3 %copy-start.7 = (bf16[512,512]{1,0:T(8,128)(2,1)S(1)}, bf16[512,512]{1,0:T(8,128)(2,1)}, u32[]{:S(2)}) copy-start(bf16[512,512]{1,0:T(8,128)(2,1)} %constant.63.clone.cos_hbm) | copy-start | bytes 1572868
  1.9 42.3 %copy-start.13 = (f32[2,2,64]{2,1,0:T(2,128)S(1)}, f32[2,2,64]{2,1,0:T(2,128)}, u32[]{:S(2)}) copy-start(f32[2,2,64]{2,1,0:T(2,128)} %b1_ref.1) | copy-start | bytes 3076
  1.9 42.3 %copy-start.14 = (f32[2,2,64]{2,1,0:T(2,128)S(1)}, f32[2,2,64]{2,1,0:T(2,128)}, u32[]{:S(2)}) copy-start(f32[2,2,64]{2,1,0:T(2,128)} %b2_ref.1) | copy-start | bytes 3076
  2.8 9.2 %collective-permute-start.2 = (f32[3,8,512]{2,1,0:T(8,128)S(1)}, f32[3,8,512]{2,1,0:T(8,128)S(1)}, u32[]{:S(2)}, u32[]{:S(2)}) collective-permute-start(f32[3,8,512]{2,1,0:T(8,128)S(1)} %shard_map.145.s0_ref.s0), channel_id=1, source_target_pairs={{0,192},{64,0},{128,64},{192,128},{1,193},{65,1},{129,65},{193,129... | collective-permute-start | bytes 147464 | tf_op jit(solution)/shard_map/ppermute | solution.py:331
  8.2 8.0 %collective-permute-start.1 = (f32[3,8,512]{2,1,0:T(8,128)S(1)}, f32[3,8,512]{2,1,0:T(8,128)S(1)}, u32[]{:S(2)}, u32[]{:S(2)}) collective-permute-start(f32[3,8,512]{2,1,0:T(8,128)S(1)} %shard_map.145.s0_ref.s0), channel_id=1, source_target_pairs={{0,128},{64,192},{128,0},{192,64},{1,129},{65,193},{129,1},{193,65... | collective-permute-start | bytes 147464 | tf_op jit(solution)/shard_map/ppermute | solution.py:331
  9.7 7.4 %collective-permute-start = (f32[3,8,512]{2,1,0:T(8,128)S(1)}, f32[3,8,512]{2,1,0:T(8,128)S(1)}, u32[]{:S(2)}, u32[]{:S(2)}) collective-permute-start(f32[3,8,512]{2,1,0:T(8,128)S(1)} %shard_map.145.s0_ref.s0), channel_id=1, source_target_pairs={{0,64},{64,128},{128,192},{192,0},{1,65},{65,129},{129,193},{193,1... | collective-permute-start | bytes 147464 | tf_op jit(solution)/shard_map/ppermute | solution.py:331
  49.9 54.4 %copy-start.1 = (bf16[8,512,128]{2,1,0:T(8,128)(2,1)S(1)}, bf16[8,512,128]{2,1,0:T(8,128)(2,1)}, u32[]{:S(2)}) copy-start(bf16[8,512,128]{2,1,0:T(8,128)(2,1)} %t_ref.1) | copy-start | bytes 3145732
  49.9 54.4 %copy-start.16 = (f32[128]{0:T(128)S(1)}, f32[128]{0:T(128)}, u32[]{:S(2)}) copy-start(f32[128]{0:T(128)} %param.16) | copy-start | bytes 1540
  50.0 54.4 %all-to-all-start.1 = ((bf16[64,8,8,128]{3,2,1,0:T(8,128)(2,1)}), bf16[64,8,8,128]{3,2,1,0:T(8,128)(2,1)S(1)}, u32[]{:S(2)}, u32[]{:S(2)}) async-start(bf16[64,8,8,128]{3,2,1,0:T(8,128)(2,1)} %bitcast.4), calls=%async_computation.1 | async-start | bytes 2097152 | tf_op jit(solution)/shard_map/all_to_all | solution.py:419
  59.0 20.7 %collective-permute-start.8 = (bf16[64,1152]{1,0:T(8,128)(2,1)S(1)}, bf16[64,1152]{1,0:T(8,128)(2,1)S(1)}, u32[]{:S(2)}, u32[]{:S(2)}) collective-permute-start(bf16[64,1152]{1,0:T(8,128)(2,1)S(1)} %shard_map.149.refs_0_), channel_id=1, source_target_pairs={{0,192},{64,0},{128,64},{192,128},{1,193},{65,1},{129,65},{193,129... | collective-permute-start | bytes 442376 | tf_op jit(solution)/shard_map/ppermute | solution.py:331
  61.1 25.6 %collective-permute-start.7 = (bf16[64,1152]{1,0:T(8,128)(2,1)S(1)}, bf16[64,1152]{1,0:T(8,128)(2,1)S(1)}, u32[]{:S(2)}, u32[]{:S(2)}) collective-permute-start(bf16[64,1152]{1,0:T(8,128)(2,1)S(1)} %shard_map.149.refs_0_), channel_id=1, source_target_pairs={{0,128},{64,192},{128,0},{192,64},{1,129},{65,193},{129,1},{193,65... | collective-permute-start | bytes 442376 | tf_op jit(solution)/shard_map/ppermute | solution.py:331
  63.2 23.6 %collective-permute-start.6 = (bf16[64,1152]{1,0:T(8,128)(2,1)S(1)}, bf16[64,1152]{1,0:T(8,128)(2,1)S(1)}, u32[]{:S(2)}, u32[]{:S(2)}) collective-permute-start(bf16[64,1152]{1,0:T(8,128)(2,1)S(1)} %shard_map.149.refs_0_), channel_id=1, source_target_pairs={{0,64},{64,128},{128,192},{192,0},{1,65},{65,129},{129,193},{193,1... | collective-permute-start | bytes 442376 | tf_op jit(solution)/shard_map/ppermute | solution.py:331
  86.8 16.1 %collective-permute-start.13 = (bf16[128,1152]{1,0:T(8,128)(2,1)S(1)}, bf16[128,1152]{1,0:T(8,128)(2,1)S(1)}, u32[]{:S(2)}, u32[]{:S(2)}) collective-permute-start(bf16[128,1152]{1,0:T(8,128)(2,1)S(1)} %get-tuple-element.31.refs_0_), channel_id=1, source_target_pairs={{0,48},{1,49},{2,50},{3,51},{4,52},{5,53},{6,54},{7,55},{8,56},{9,... | collective-permute-start | bytes 884744 | tf_op jit(solution)/shard_map/ppermute | solution.py:395
  87.6 20.3 %collective-permute-start.11 = (bf16[128,1152]{1,0:T(8,128)(2,1)S(1)}, bf16[128,1152]{1,0:T(8,128)(2,1)}, u32[]{:S(2)}, u32[]{:S(2)}) collective-permute-start(bf16[128,1152]{1,0:T(8,128)(2,1)S(1)} %get-tuple-element.31.refs_0_), channel_id=1, source_target_pairs={{0,32},{1,33},{2,34},{3,35},{4,36},{5,37},{6,38},{7,39},{8,40},{9,... | collective-permute-start | bytes 884744 | tf_op jit(solution)/shard_map/ppermute | solution.py:395
  88.6 19.3 %collective-permute-start.9 = (bf16[128,1152]{1,0:T(8,128)(2,1)S(1)}, bf16[128,1152]{1,0:T(8,128)(2,1)}, u32[]{:S(2)}, u32[]{:S(2)}) collective-permute-start(bf16[128,1152]{1,0:T(8,128)(2,1)S(1)} %get-tuple-element.31.refs_0_), channel_id=1, source_target_pairs={{0,16},{1,17},{2,18},{3,19},{4,20},{5,21},{6,22},{7,23},{8,24},{9,... | collective-permute-start | bytes 884744 | tf_op jit(solution)/shard_map/ppermute | solution.py:395
  90.7 17.2 %collective-permute-start.14 = (bf16[128,1152]{1,0:T(8,128)(2,1)S(1)}, bf16[128,1152]{1,0:T(8,128)(2,1)}, u32[]{:S(2)}, u32[]{:S(2)}) collective-permute-start(bf16[128,1152]{1,0:T(8,128)(2,1)S(1)} %get-tuple-element.32.refs_1_), channel_id=1, source_target_pairs={{0,6},{1,7},{2,0},{3,1},{4,2},{5,3},{6,4},{7,5},{8,14},{9,15},{10,... | collective-permute-start | bytes 884744 | tf_op jit(solution)/shard_map/ppermute | solution.py:395
  93.5 14.5 %collective-permute-start.12 = (bf16[128,1152]{1,0:T(8,128)(2,1)S(1)}, bf16[128,1152]{1,0:T(8,128)(2,1)}, u32[]{:S(2)}, u32[]{:S(2)}) collective-permute-start(bf16[128,1152]{1,0:T(8,128)(2,1)S(1)} %get-tuple-element.32.refs_1_), channel_id=1, source_target_pairs={{0,4},{1,5},{2,6},{3,7},{4,0},{5,1},{6,2},{7,3},{8,12},{9,13},{10,... | collective-permute-start | bytes 884744 | tf_op jit(solution)/shard_map/ppermute | solution.py:395
  102.8 8.0 %collective-permute-start.10 = (bf16[128,1152]{1,0:T(8,128)(2,1)S(1)}, bf16[128,1152]{1,0:T(8,128)(2,1)}, u32[]{:S(2)}, u32[]{:S(2)}) collective-permute-start(bf16[128,1152]{1,0:T(8,128)(2,1)S(1)} %get-tuple-element.32.refs_1_), channel_id=1, source_target_pairs={{0,2},{1,3},{2,4},{3,5},{4,6},{5,7},{6,0},{7,1},{8,10},{9,11},{10,... | collective-permute-start | bytes 884744 | tf_op jit(solution)/shard_map/ppermute | solution.py:395
  112.4 26.1 %collective-permute-start.15 = (bf16[1024,1152]{1,0:T(8,128)(2,1)S(1)}, bf16[1024,1152]{1,0:T(8,128)(2,1)S(1)}, u32[]{:S(2)}, u32[]{:S(2)}) collective-permute-start(bf16[1024,1152]{1,0:T(8,128)(2,1)S(1)} %shard_map.151.wa_ref), channel_id=1, source_target_pairs={{0,1},{1,0},{2,3},{3,2},{4,5},{5,4},{6,7},{7,6},{8,9},{9,8},{10,11... | collective-permute-start | bytes 7077896 | tf_op jit(solution)/shard_map/ppermute | solution.py:436
  112.5 24.8 %collective-permute-start.19 = (bf16[512,128]{1,0:T(8,128)(2,1)S(1)}, bf16[512,128]{1,0:T(8,128)(2,1)S(1)}, u32[]{:S(2)}, u32[]{:S(2)}) collective-permute-start(bf16[512,128]{1,0:T(8,128)(2,1)S(1)} %get-tuple-element.38), channel_id=1, source_target_pairs={{0,64},{64,128},{128,192},{192,0},{1,65},{65,129},{129,193},{193,1... | collective-permute-start | bytes 393224 | tf_op jit(solution)/shard_map/ppermute | solution.py:331
  112.6 24.7 %collective-permute-start.20 = (bf16[512,128]{1,0:T(8,128)(2,1)S(1)}, bf16[512,128]{1,0:T(8,128)(2,1)S(1)}, u32[]{:S(2)}, u32[]{:S(2)}) collective-permute-start(bf16[512,128]{1,0:T(8,128)(2,1)S(1)} %get-tuple-element.39), channel_id=1, source_target_pairs={{0,128},{64,192},{128,0},{192,64},{1,129},{65,193},{129,1},{193,65... | collective-permute-start | bytes 393224 | tf_op jit(solution)/shard_map/ppermute | solution.py:331
  114.7 23.9 %collective-permute-start.21 = (bf16[512,128]{1,0:T(8,128)(2,1)S(1)}, bf16[512,128]{1,0:T(8,128)(2,1)S(1)}, u32[]{:S(2)}, u32[]{:S(2)}) collective-permute-start(bf16[512,128]{1,0:T(8,128)(2,1)S(1)} %get-tuple-element.40), channel_id=1, source_target_pairs={{0,192},{64,0},{128,64},{192,128},{1,193},{65,1},{129,65},{193,129... | collective-permute-start | bytes 393224 | tf_op jit(solution)/shard_map/ppermute | solution.py:331
  118.7 31.2 %collective-permute-start.3 = (bf16[512,128]{1,0:T(8,128)(2,1)S(1)}, bf16[512,128]{1,0:T(8,128)(2,1)S(1)}, u32[]{:S(2)}, u32[]{:S(2)}) collective-permute-start(bf16[512,128]{1,0:T(8,128)(2,1)S(1)} %get-tuple-element.28), channel_id=1, source_target_pairs={{0,64},{64,128},{128,192},{192,0},{1,65},{65,129},{129,193},{193,1... | collective-permute-start | bytes 393224 | tf_op jit(solution)/shard_map/ppermute | solution.py:331
  137.3 13.9 %collective-permute-start.4 = (bf16[512,128]{1,0:T(8,128)(2,1)S(1)}, bf16[512,128]{1,0:T(8,128)(2,1)S(1)}, u32[]{:S(2)}, u32[]{:S(2)}) collective-permute-start(bf16[512,128]{1,0:T(8,128)(2,1)S(1)} %get-tuple-element.29), channel_id=1, source_target_pairs={{0,128},{64,192},{128,0},{192,64},{1,129},{65,193},{129,1},{193,65... | collective-permute-start | bytes 393224 | tf_op jit(solution)/shard_map/ppermute | solution.py:331
  137.3 13.9 %collective-permute-start.5 = (bf16[512,128]{1,0:T(8,128)(2,1)S(1)}, bf16[512,128]{1,0:T(8,128)(2,1)S(1)}, u32[]{:S(2)}, u32[]{:S(2)}) collective-permute-start(bf16[512,128]{1,0:T(8,128)(2,1)S(1)} %get-tuple-element.30), channel_id=1, source_target_pairs={{0,192},{64,0},{128,64},{192,128},{1,193},{65,1},{129,65},{193,129... | collective-permute-start | bytes 393224 | tf_op jit(solution)/shard_map/ppermute | solution.py:331
  142.2 18.9 %collective-permute-start.22 = (bf16[512,128]{1,0:T(8,128)(2,1)S(1)}, bf16[512,128]{1,0:T(8,128)(2,1)S(1)}, u32[]{:S(2)}, u32[]{:S(2)}) collective-permute-start(bf16[512,128]{1,0:T(8,128)(2,1)S(1)} %get-tuple-element.42), channel_id=1, source_target_pairs={{0,64},{64,128},{128,192},{192,0},{1,65},{65,129},{129,193},{193,1... | collective-permute-start | bytes 393224 | tf_op jit(solution)/shard_map/ppermute | solution.py:331
  144.0 20.8 %collective-permute-start.23 = (bf16[512,128]{1,0:T(8,128)(2,1)S(1)}, bf16[512,128]{1,0:T(8,128)(2,1)S(1)}, u32[]{:S(2)}, u32[]{:S(2)}) collective-permute-start(bf16[512,128]{1,0:T(8,128)(2,1)S(1)} %get-tuple-element.43), channel_id=1, source_target_pairs={{0,128},{64,192},{128,0},{192,64},{1,129},{65,193},{129,1},{193,65... | collective-permute-start | bytes 393224 | tf_op jit(solution)/shard_map/ppermute | solution.py:331
  149.9 14.9 %collective-permute-start.24 = (bf16[512,128]{1,0:T(8,128)(2,1)S(1)}, bf16[512,128]{1,0:T(8,128)(2,1)S(1)}, u32[]{:S(2)}, u32[]{:S(2)}) collective-permute-start(bf16[512,128]{1,0:T(8,128)(2,1)S(1)} %get-tuple-element.44), channel_id=1, source_target_pairs={{0,192},{64,0},{128,64},{192,128},{1,193},{65,1},{129,65},{193,129... | collective-permute-start | bytes 393224 | tf_op jit(solution)/shard_map/ppermute | solution.py:331
  154.9 9.9 %collective-permute-start.16 = (bf16[512,128]{1,0:T(8,128)(2,1)S(1)}, bf16[512,128]{1,0:T(8,128)(2,1)S(1)}, u32[]{:S(2)}, u32[]{:S(2)}) collective-permute-start(bf16[512,128]{1,0:T(8,128)(2,1)S(1)} %get-tuple-element.34), channel_id=1, source_target_pairs={{0,64},{64,128},{128,192},{192,0},{1,65},{65,129},{129,193},{193,1... | collective-permute-start | bytes 393224 | tf_op jit(solution)/shard_map/ppermute | solution.py:331
  161.1 9.3 %collective-permute-start.17 = (bf16[512,128]{1,0:T(8,128)(2,1)S(1)}, bf16[512,128]{1,0:T(8,128)(2,1)S(1)}, u32[]{:S(2)}, u32[]{:S(2)}) collective-permute-start(bf16[512,128]{1,0:T(8,128)(2,1)S(1)} %get-tuple-element.35), channel_id=1, source_target_pairs={{0,128},{64,192},{128,0},{192,64},{1,129},{65,193},{129,1},{193,65... | collective-permute-start | bytes 393224 | tf_op jit(solution)/shard_map/ppermute | solution.py:331
  161.1 9.8 %collective-permute-start.18 = (bf16[512,128]{1,0:T(8,128)(2,1)S(1)}, bf16[512,128]{1,0:T(8,128)(2,1)S(1)}, u32[]{:S(2)}, u32[]{:S(2)}) collective-permute-start(bf16[512,128]{1,0:T(8,128)(2,1)S(1)} %get-tuple-element.36), channel_id=1, source_target_pairs={{0,192},{64,0},{128,64},{192,128},{1,193},{65,1},{129,65},{193,129... | collective-permute-start | bytes 393224 | tf_op jit(solution)/shard_map/ppermute | solution.py:331
  (13 other events, 149.5 us)

commit v2 on v1

v2 whole, which is shorter than its diff:
```python
import math
from functools import partial

import jax
import jax.numpy as jnp
import numpy as np
from jax import lax
from jax.experimental import pallas as pl
from jax.experimental.pallas import tpu as pltpu
from jax.sharding import PartitionSpec as P

norm_eps = 1e-05
shrink_level = 0.01
bf16 = jnp.bfloat16
f32 = jnp.float32


def tables(rows, width, per_owner):
    owners = width // 2 // per_owner
    place = np.arange(width)
    freq = np.arange(width // 2).reshape(owners, 1, per_owner)
    freq = np.broadcast_to(freq, (owners, 2, per_owner)).reshape(-1)
    part = np.broadcast_to(np.arange(2).reshape(1, 2, 1), (owners, 2, per_owner)).reshape(-1)
    angle = 2.0 * np.pi / width * ((freq[:, None] * place[None, :]) % width)
    forward = np.where(part[:, None] == 0, np.cos(angle), -np.sin(angle))
    grid = np.arange(rows)
    turn = 2.0 * np.pi / rows * ((grid[:, None] * grid[None, :]) % rows)
    return forward, np.cos(turn), np.sin(turn)


def mm(left, right):
    return jnp.dot(left, right, preferred_element_type=f32)


def mm_t(left, right):
    return lax.dot_general(left, right, (((1,), (1,)), ((), ())), preferred_element_type=f32)


def stats_kernel(x_ref, o_ref):
    rows, _, lanes = x_ref.shape
    ones = jnp.ones((8, lanes), bf16)

    def body(row, carry):
        x = x_ref[row]
        wide = x.astype(f32)
        square = wide * wide
        high = square.astype(bf16)
        low = (square - high.astype(f32)).astype(bf16)
        o_ref[0, pl.ds(row, 1), :] = mm_t(ones, x)[0:1]
        o_ref[1, pl.ds(row, 1), :] = (mm_t(ones, high) + mm_t(ones, low))[0:1]
        return carry

    lax.fori_loop(0, rows, body, 0, unroll=2)


def add_kernel(left_ref, right_ref, o_ref):
    o_ref[...] = left_ref[...] + right_ref[...]


def warm_kernel(*refs):
    count = len(refs) // 2
    for source, target in zip(refs[:count], refs[count:]):
        target[...] = source[...]


def moments(left_ref, right_ref, channels):
    center = (left_ref[0] + right_ref[0]) / channels
    spread = (left_ref[1] + right_ref[1]) / channels - center * center
    return jnp.transpose(jnp.concatenate([center, lax.rsqrt(spread + norm_eps)], axis=0))


def normed_row(source, flipped, row, rows, gain):
    column = lax.broadcasted_iota(jnp.int32, flipped.shape, 1)
    center = jnp.sum(jnp.where(column == row, flipped, 0.0), axis=1, keepdims=True)
    factor = jnp.sum(jnp.where(column == row + rows, flipped, 0.0), axis=1, keepdims=True)
    return (source - center) * factor * gain


def forward_kernel(channels, scale, x_ref, left_ref, right_ref, gain_ref, table_ref, o_ref, f_ref):
    rows, _, lanes = x_ref.shape
    owners = o_ref.shape[0]
    f_ref[...] = moments(left_ref, right_ref, channels)

    def body(pair, carry):
        sides = [
            normed_row(x_ref[row].astype(f32), f_ref[...], row, rows, gain_ref[...]).astype(bf16)
            for row in (2 * pair, 2 * pair + 1)
        ]
        out = mm(table_ref[...], jnp.concatenate(sides, axis=1)) * scale
        for side in range(2):
            o_ref[:, 2 * pair + side] = (
                out[:, side * lanes : (side + 1) * lanes].reshape(owners, -1, lanes).astype(bf16)
            )
        return carry

    lax.fori_loop(0, rows // 2, body, 0)


def residual_kernel(channels, x_ref, left_ref, right_ref, gain_ref, o_ref, f_ref):
    rows = x_ref.shape[0]
    f_ref[...] = moments(left_ref, right_ref, channels)

    def body(row, carry):
        source = x_ref[row].astype(f32)
        o_ref[row] = normed_row(source, f_ref[...], row, rows, gain_ref[...]) + source
        return carry

    lax.fori_loop(0, rows, body, 0)


def flip_kernel(per_owner, lanes, table_ref, i_ref):
    for start in range(0, table_ref.shape[0], lanes):
        place = lax.broadcasted_iota(jnp.int32, (lanes, 1), 0) + start
        weight = jnp.where((place == 0) | (place == per_owner), 1.0, 2.0)
        part = table_ref[start : start + lanes, :].astype(f32) * weight
        i_ref[:, start : start + lanes] = jnp.transpose(part).astype(bf16)


def soften(values):
    return jnp.where(
        values > shrink_level,
        values - shrink_level,
        jnp.where(values < -shrink_level, values + shrink_level, 0.0),
    )


def block_matrix(w_ref, part):
    count, size = w_ref.shape[1], w_ref.shape[2]
    rows = []
    for block in range(count):
        cells = [jnp.zeros((size, size), f32)] * count
        cells[block] = w_ref[part, block]
        rows.append(jnp.concatenate(cells, axis=1))
    return jnp.concatenate(rows, axis=0)


def complex_matrix(w_ref):
    real, imag = block_matrix(w_ref, 0), block_matrix(w_ref, 1)
    return jnp.concatenate(
        [jnp.concatenate([real, imag], axis=1), jnp.concatenate([-imag, real], axis=1)], axis=0
    ).astype(bf16)


def bias_row(b_ref):
    parts, count = b_ref.shape[0], b_ref.shape[1]
    return jnp.concatenate(
        [b_ref[part, block : block + 1, :] for part in range(parts) for block in range(count)], axis=1
    )


def column_kernel(
    scale, x_ref, table_ref, w_ref, o_ref, wide_ref, real_ref, imag_ref
):
    size = w_ref.shape[1]
    tail = w_ref[2 * size :, :].astype(f32)
    bias_one, bias_two = tail[0:1] + tail[1:2], tail[2:3] + tail[3:4]
    height = table_ref.shape[1]
    lanes = x_ref.shape[1]
    step = x_ref.shape[0] // height
    count = step // 2
    wide_ref[...] = x_ref[...].astype(f32)
    for part, target in ((0, real_ref), (1, imag_ref)):
        for k in range(count):
            target[:, k * lanes : (k + 1) * lanes] = wide_ref[
                pl.ds(part * count + k, height, stride=step), :
            ].astype(bf16)

    def body(half, carry):
        span = pl.ds(pl.multiple_of(half * 2 * lanes, 2 * lanes), 2 * lanes)
        cos, sin = table_ref[0:height, :], table_ref[height:, :]
        real, imag = real_ref[:, span], imag_ref[:, span]
        out_real = (mm(cos, real) + mm(sin, imag)) * scale
        out_imag = (mm(cos, imag) - mm(sin, real)) * scale
        next_real, next_imag = [], []
        for side in range(2):
            cut = slice(side * lanes, (side + 1) * lanes)
            both = jnp.concatenate([out_real[:, cut].astype(bf16), out_imag[:, cut].astype(bf16)], axis=1)
            first = jnp.maximum(mm(both, w_ref[0:size, :]) + bias_one, 0.0).astype(bf16)
            second = soften(mm(first, w_ref[size : 2 * size, :]) + bias_two).astype(bf16)
            next_real.append(second[:, :lanes])
            next_imag.append(second[:, lanes:])
        real, imag = jnp.concatenate(next_real, axis=1), jnp.concatenate(next_imag, axis=1)
        back_real = (mm(cos, real) - mm(sin, imag)) * scale
        back_imag = (mm(cos, imag) + mm(sin, real)) * scale
        for side in range(2):
            cut = slice(side * lanes, (side + 1) * lanes)
            k = half * 2 + side
            wide_ref[pl.ds(k, height, stride=step), :] = back_real[:, cut]
            wide_ref[pl.ds(count + k, height, stride=step), :] = back_imag[:, cut]
        return carry

    lax.fori_loop(0, count // 2, body, 0)
    o_ref[...] = wide_ref[...].astype(bf16)


def inverse_kernel(scale, me_ref, x_ref, table_ref, r_ref, *refs):
    *o_refs, m_ref = refs
    ways = len(o_refs) // 2
    rows, _, lanes = r_ref.shape

    def body(pair, carry):
        sides = [
            x_ref[:, 2 * pair + side].astype(f32).reshape(-1, lanes).astype(bf16) for side in range(2)
        ]
        out = mm(table_ref[...], jnp.concatenate(sides, axis=1)) * scale
        for side in range(2):
            m_ref[side, pair] = (out[:, side * lanes : (side + 1) * lanes] + r_ref[2 * pair + side]).astype(bf16)
        return carry

    lax.fori_loop(0, rows // 2, body, 0)
    for shift in range(ways):
        for side in range(2):
            o_refs[side * ways + shift][...] = m_ref[side, lax.rem(me_ref[0] + shift, ways)]


def gelu(values):
    return 0.5 * values * (1.0 + lax.erf(values * math.sqrt(0.5)))


def mlp_kernel(
    tile, me_ref, x0, x1, x2, x3, wa_ref, wb_ref, gain_ref, bias_ref, y0, y1, y2, y3, x_ref, y_ref, n_ref, a_ref
):
    ways, tokens, lanes = x_ref.shape
    channels = ways * lanes
    me = me_ref[0]
    for shift, ref in enumerate((x0, x1, x2, x3)):
        x_ref[lax.rem(me + ways - shift, ways)] = ref[...]
    unit = jnp.ones((8, lanes), bf16)
    hidden_block = 512

    def body(index, carry):
        span = pl.ds(pl.multiple_of(index * tile, tile), tile)
        mixed = [x_ref[block, span, :].astype(f32) for block in range(ways)]
        total = sum(mixed[1:], mixed[0])
        square = sum((m * m for m in mixed[1:]), mixed[0] * mixed[0])
        center = jnp.sum(total, axis=1, keepdims=True) / channels
        spread = jnp.sum(square, axis=1, keepdims=True) / channels - center * center
        inverse = lax.rsqrt(spread + norm_eps)
        for b, m in enumerate(mixed):
            cut = slice(b * lanes, (b + 1) * lanes)
            n_ref[:, cut] = ((m - center) * inverse * gain_ref[:, cut]).astype(bf16)
            a_ref[:, cut] = m + bias_ref[b : b + 1, :]

        def block(place, inner):
            rows = pl.ds(pl.multiple_of(place * hidden_block, hidden_block), hidden_block)
            product = None
            for ref in (wa_ref, wb_ref):
                bias = mm_t(unit, ref[rows, 2 * channels :])[0:1]
                hidden = gelu(mm_t(n_ref[...], ref[rows, :channels]) + bias).astype(bf16)
                part = mm(hidden, ref[rows, channels : 2 * channels])
                product = part if product is None else product + part
            a_ref[...] += product
            return inner

        lax.fori_loop(0, wa_ref.shape[0] // hidden_block, block, 0)
        for b in range(ways):
            y_ref[b, span, :] = a_ref[:, b * lanes : (b + 1) * lanes].astype(bf16)
        return carry

    lax.fori_loop(0, tokens // tile, body, 0)
    for shift, ref in enumerate((y0, y1, y2, y3)):
        ref[...] = y_ref[lax.rem(me + shift, ways)]


def place_kernel(me_ref, *refs):
    *parts, o_ref = refs
    ways = o_ref.shape[0]
    half = o_ref.shape[1] // 2
    for place, part in enumerate(parts):
        shift = place % ways
        o_ref[lax.rem(me_ref[0] + ways - shift, ways), pl.ds(place // ways * half, half), :] = part[...]


def piece_kernel(
    piece_ref, one_ref, bias_ref, two_ref, out_ref, o_ref, flat_ref
):
    channels = one_ref.shape[0]
    lanes = o_ref.shape[1] - 2 * channels
    units = (o_ref.shape[0] - 16) // 2
    row = lax.broadcasted_iota(jnp.int32, (lanes, lanes), 0)
    column = lax.broadcasted_iota(jnp.int32, (lanes, lanes), 1)
    unit = jnp.where(row == column, 1.0, 0.0).astype(bf16)
    for half in range(2):
        first = half * (one_ref.shape[1] // 2) + piece_ref[half] * units
        slab = pl.ds(pl.multiple_of(first // lanes * lanes, lanes), lanes)
        bias = jnp.broadcast_to(bias_ref[:, slab].astype(f32), (lanes, lanes))
        flat_ref[:, 0:channels] = mm_t(unit, one_ref[:, slab])
        flat_ref[:, channels:] = jnp.where(row == column, bias, 0.0)
        within = pl.ds(pl.multiple_of(lax.rem(first, lanes), units), units)
        target = pl.ds(half * units, units)
        o_ref[target, 0:channels] = flat_ref[within, 0:channels].astype(bf16)
        o_ref[target, channels : 2 * channels] = two_ref[pl.ds(pl.multiple_of(first, units), units), :]
        o_ref[target, 2 * channels :] = flat_ref[within, channels:].astype(bf16)
    tail = pl.ds(2 * units, 16)
    o_ref[tail, :] = jnp.zeros((16, o_ref.shape[1]), bf16)
    o_ref[tail, 0:lanes] = jnp.broadcast_to(out_ref[...].astype(f32), (16, lanes)).astype(bf16)


def prep_kernel(w1_ref, b1_ref, w2_ref, b2_ref, o_ref):
    size = o_ref.shape[1]
    o_ref[0:size, :] = complex_matrix(w1_ref)
    o_ref[size : 2 * size, :] = complex_matrix(w2_ref)
    rows = []
    for ref in (b1_ref, b2_ref):
        bias = bias_row(ref)
        high = bias.astype(bf16).astype(f32)
        rows += [high, bias - high]
    rows.append(jnp.zeros((12, size), f32))
    o_ref[2 * size :, :] = jnp.concatenate(rows, axis=0).astype(bf16)


def split_kernel(me_ref, *refs):
    *parts, first_ref, second_ref, bias_ref = refs
    ways = len(parts)
    lanes = bias_ref.shape[1]
    size = first_ref.shape[0] // ways
    for place, part in enumerate(parts):
        for half, ref in enumerate((first_ref, second_ref)):
            ref[place * size : (place + 1) * size, :] = part[half * size : (half + 1) * size, :]
        row = part[2 * size : 2 * size + 16, 0:lanes].astype(f32)[0:1]
        bias_ref[pl.ds(lax.rem(me_ref[0] + ways - place, ways), 1), :] = row


def join_kernel(*refs):
    *parts, after_ref, o_ref = refs
    start = 0
    for part in parts:
        o_ref[start : start + part.shape[0], :] = part[...]
        start += part.shape[0]


def vmem(count):
    return [pl.BlockSpec(memory_space=pltpu.VMEM)] * count


smem = pl.BlockSpec(memory_space=pltpu.SMEM)


def call(kernel, shapes, in_specs, scratch=(), flops=0, size=0):
    return pl.pallas_call(
        kernel,
        out_shape=shapes,
        in_specs=in_specs,
        out_specs=jax.tree.map(lambda _: pl.BlockSpec(memory_space=pltpu.VMEM), shapes),
        scratch_shapes=scratch,
        cost_estimate=pl.CostEstimate(flops=flops, bytes_accessed=size, transcendentals=0),
        compiler_params=pltpu.CompilerParams(vmem_limit_bytes=24 * 1024 * 1024),
    )


def shape(dims, dtype):
    return jax.ShapeDtypeStruct(dims, dtype)


def shifts(value_of, axis, ways):
    return [
        lax.ppermute(value_of(shift), axis, [(i, (i + shift) % ways) for i in range(ways)])
        for shift in range(1, ways)
    ]


def local(
    tokens,
    gain_in,
    spectral_w1,
    spectral_b1,
    spectral_w2,
    spectral_b2,
    gain_out,
    fc1_weight,
    fc1_bias,
    fc2_weight,
    fc2_bias,
):
    rows, width, lanes = tokens.shape
    ways = lax.axis_size("chan")
    owners = lax.axis_size("rows")
    height = rows * owners
    channels = lanes * ways
    per_owner = width // 2 // owners
    me = lax.axis_index("chan").astype(jnp.int32).reshape(1)
    forward, cos, sin = tables(height, width, per_owner)
    forward = jnp.asarray(forward, bf16)
    turns = jnp.asarray(np.concatenate([cos, sin], axis=0), bf16)
    half_scale = 2.0 ** math.floor(math.log2(math.sqrt(width)))
    first_scale, second_scale = 1.0 / half_scale, half_scale / math.sqrt(width * height)

    stats = call(stats_kernel, shape((2, rows, width), f32), vmem(1))(tokens)
    other = lax.ppermute(stats, "chan", [(i, i ^ 1) for i in range(ways)])
    left = call(add_kernel, shape(stats.shape, f32), vmem(2))(stats, other)
    right = lax.ppermute(left, "chan", [(i, i ^ 2) for i in range(ways)])
    table, gain = call(
        warm_kernel, [shape(forward.shape, bf16), shape((1, lanes), f32)], vmem(2)
    )(forward, gain_in.reshape(1, lanes))
    spectra = call(
        partial(forward_kernel, channels, first_scale),
        shape((owners, rows, 2 * per_owner, lanes), bf16),
        vmem(5),
        scratch=[pltpu.VMEM((width, 2 * rows), f32)],
    )(tokens, left, right, gain, table)
    columns = lax.all_to_all(spectra, "rows", split_axis=0, concat_axis=0)

    ring_x, ring_y, per_x = 4, 4, owners // 4
    place = lax.axis_index("rows").astype(jnp.int32)
    units = fc1_weight.shape[1] // (2 * ring_x)
    across, along, core = place // per_x, place // 2 % ring_y, place % 2
    piece = jnp.stack([across * 2 + core, along * 2 + core])
    mine = call(
        piece_kernel,
        shape((units + 16, 2 * channels + lanes), bf16),
        [smem] + vmem(4),
        scratch=[pltpu.VMEM((lanes, channels + lanes), f32)],
    )(piece, fc1_weight, fc1_bias.reshape(1, -1), fc2_weight, fc2_bias.reshape(1, lanes))
    wide = 2 * lanes
    spectral = call(prep_kernel, shape((2 * wide + 16, wide), bf16), vmem(4))(
        spectral_w1, spectral_b1, spectral_w2, spectral_b2
    )
    circle = call(warm_kernel, [shape(turns.shape, bf16)], vmem(1))(turns)[0]
    stage = [mine] + shifts(lambda s: mine, "chan", ways)
    count = ways * units // 2
    *sides, out_bias = call(
        split_kernel,
        [shape((count, mine.shape[1]), bf16)] * 2 + [shape((8, lanes), f32)],
        [smem] + vmem(ways),
    )(me, *stage)
    parts = list(sides)
    for shift in range(1, ring_x):
        ring = [
            [(i, (i + shift * per_x) % owners) for i in range(owners)],
            [(i, i + 2 * ((i // 2 % ring_y + shift) % ring_y - i // 2 % ring_y)) for i in range(owners)],
        ]
        for half in range(2):
            parts.append(lax.ppermute(sides[half], "rows", ring[half]))

    total = owners * rows * 2 * per_owner
    back = call(
        partial(column_kernel, second_scale),
        shape((total, lanes), bf16),
        vmem(3),
        scratch=[
            pltpu.VMEM((total, lanes), f32),
            pltpu.VMEM((height, per_owner * lanes), bf16),
            pltpu.VMEM((height, per_owner * lanes), bf16),
        ],
    )(columns.reshape(total, lanes), circle, spectral)
    returned = lax.all_to_all(
        back.reshape(owners, rows, 2 * per_owner, lanes), "rows", split_axis=0, concat_axis=0
    )
    resid = call(
        partial(residual_kernel, channels),
        shape((rows, width, lanes), f32),
        vmem(4),
        scratch=[pltpu.VMEM((width, 2 * rows), f32)],
    )(tokens, left, right, gain_in.reshape(1, lanes))
    inverse = call(partial(flip_kernel, per_owner, lanes), shape((width, width), bf16), vmem(1))(forward)
    share = rows // ways * width // 2
    mixed = call(
        partial(inverse_kernel, first_scale),
        [shape((share, lanes), bf16)] * (2 * ways),
        [smem] + vmem(3),
        scratch=[pltpu.VMEM((2, ways, width, lanes), bf16)],
    )(me, returned, inverse, resid)
    halves = [mixed[:ways], mixed[ways:]]
    whole_a = [halves[0][0]] + shifts(lambda s: halves[0][s], "chan", ways)
    near = call(
        join_kernel,
        shape((2 * ring_x * parts[0].shape[0], parts[0].shape[1]), bf16),
        vmem(len(parts)) + [pl.BlockSpec(memory_space=pl.ANY)],
    )(*parts, mixed[0])
    far = lax.ppermute(near, "rows", [(i, i ^ 1) for i in range(owners)])
    whole_b = [halves[1][0]] + shifts(lambda s: halves[1][s], "chan", ways)

    def mlp(whole):
        return call(
            partial(mlp_kernel, 256),
            [shape((share, lanes), bf16)] * ways,
            [smem] + vmem(8),
            scratch=[
                pltpu.VMEM((ways, share, lanes), bf16),
                pltpu.VMEM((ways, share, lanes), bf16),
                pltpu.VMEM((256, channels), bf16),
                pltpu.VMEM((256, channels), f32),
            ],
        )(me, *whole, near, far, gain_out.reshape(1, channels), out_bias)

    result_a = mlp(whole_a)
    parts_a = [result_a[0]] + shifts(lambda s: result_a[s], "chan", ways)
    result_b = mlp(whole_b)
    parts_b = [result_b[0]] + shifts(lambda s: result_b[s], "chan", ways)
    final = call(place_kernel, shape((ways, 2 * share, lanes), bf16), [smem] + vmem(2 * ways))(
        me, *parts_a, *parts_b
    )
    return final.reshape(rows, width, lanes)


def solution(mesh):
    return jax.shard_map(
        local,
        mesh=mesh,
        in_specs=(
            P("rows", None, "chan"),
            P("chan"),
            P(None, "chan", None, None),
            P(None, "chan", None),
            P(None, "chan", None, None),
            P(None, "chan", None),
            P(),
            P(None, "chan"),
            P("chan"),
            P("chan", None),
            P("chan"),
        ),
        out_specs=P("rows", None, "chan"),
        check_vma=False,
    )
```

time: 172 us -> 176 us (1.023)
  the two profiles are of different devices: /device:TPU:38 before, /device:TPU:4 now
where the time goes in v2:
time: 176 us; the launch traced here: 175 us
  starting transfers between devices  74.6 us (42%)
  waiting for transfers between devices  62.2 us (35%)
  Pallas kernels  29.6 us (17%)
  local copies, waits for them, and re-layouts  8.58 us (5%)
    ppermute x15, waiting for transfers between devices, shifts(): lax.ppermute(value_of(shift), axis, [(i, (i + shift) % ways) for i in ran...  40.5 us
    ppermute x15, starting transfers between devices, shifts(): lax.ppermute(value_of(shift), axis, [(i, (i + shift) % ways) for i in ran...  37.5 us
    all_to_all x1, waiting for transfers between devices, local(): columns = lax.all_to_all(spectra, 'rows', split_axis=0, concat_axis=0)  12.2 us
    ppermute x6, starting transfers between devices, local(): parts.append(lax.ppermute(sides[half], 'rows', ring[half]))  9.87 us
    pallas_call x2, Pallas kernels, mlp(): call(partial(mlp_kernel, 256), [shape((share, lanes), bf16)] * ways, [sme...  9.26 us
    all_to_all x1, starting transfers between devices, local(): columns = lax.all_to_all(spectra, 'rows', split_axis=0, concat_axis=0)  9.03 us
    unnamed x40, local copies, waits for them, and re-layouts  8.57 us
    all_to_all x1, starting transfers between devices, local(): lax.all_to_all(back.reshape(owners, rows, 2 * per_owner, lanes), 'rows',...  7.91 us
  transfers between devices with their start and end apart: 26, of which 11 were waited for; matrix products, arithmetic and copies ran while one was open for 0% of the time, Pallas kernels for 9%

profile of v2, /device:TPU:4, one launch (start us, length us, event | category | flops | bytes accessed | tf_op | source)
XLA Modules:
  0.0 175.3 jit_solution(8189807300000218892)
XLA Ops:
  2.5 3.3 %collective-permute-start = (f32[2,8,512]{2,1,0:T(8,128)S(1)}, f32[2,8,512]{2,1,0:T(8,128)S(1)}, u32[]{:S(2)}, u32[]{:S(2)}) collective-permute-start(f32[2,8,512]{2,1,0:T(8,128)S(1)} %shard_map.127.left_ref), channel_id=1, source_target_pairs={{0,64},{64,0},{128,192},{192,128},{1,65},{65,1},{129,193},{193,129... | collective-permute-start | bytes 98312 | tf_op jit(solution)/shard_map/ppermute | solution.py:389
  5.8 1.9 %collective-permute-done.right_ref = f32[2,8,512]{2,1,0:T(8,128)S(1)} collective-permute-done((f32[2,8,512]{2,1,0:T(8,128)S(1)}, f32[2,8,512]{2,1,0:T(8,128)S(1)}, u32[]{:S(2)}, u32[]{:S(2)}) %collective-permute-start) | collective-permute-done | bytes 32800 | tf_op jit(solution)/shard_map/ppermute | solution.py:389
  7.7 6.8 %collective-permute-start.1 = (f32[2,8,512]{2,1,0:T(8,128)S(1)}, f32[2,8,512]{2,1,0:T(8,128)S(1)}, u32[]{:S(2)}, u32[]{:S(2)}) collective-permute-start(f32[2,8,512]{2,1,0:T(8,128)S(1)} %shard_map.128.left_ref), channel_id=1, source_target_pairs={{0,128},{64,192},{128,0},{192,64},{1,129},{65,193},{129,1},{193,65... | collective-permute-start | bytes 98312 | tf_op jit(solution)/shard_map/ppermute | solution.py:391
  16.4 3.6 %shard_map.130 = bf16[64,8,8,128]{3,2,1,0:T(8,128)(2,1)} custom-call(bf16[8,512,128]{2,1,0:T(8,128)(2,1)S(1)} %copy-done.1, f32[2,8,512]{2,1,0:T(8,128)S(1)} %shard_map.128.left_ref, f32[2,8,512]{2,1,0:T(8,128)S(1)} %collective-permute-done.1.right_ref, f32[1,128]{1,0:T(1,128)S(1)} %get-tuple-element.26.gain_ref, ...), custom_call_target="tpu_custom_call" | custom-call | tf_op jit(solution)/shard_map/pallas_call | solution.py:395
  20.0 9.0 %all-to-all-start = ((bf16[64,8,8,128]{3,2,1,0:T(8,128)(2,1)}), bf16[64,8,8,128]{3,2,1,0:T(8,128)(2,1)S(1)}, u32[]{:S(2)}, u32[]{:S(2)}) async-start(bf16[64,8,8,128]{3,2,1,0:T(8,128)(2,1)} %shard_map.130), calls=%async_computation | async-start | bytes 2097152 | tf_op jit(solution)/shard_map/all_to_all | solution.py:401
  32.3 12.2 %all-to-all-done = bf16[64,8,8,128]{3,2,1,0:T(8,128)(2,1)S(1)} async-done(((bf16[64,8,8,128]{3,2,1,0:T(8,128)(2,1)}), bf16[64,8,8,128]{3,2,1,0:T(8,128)(2,1)S(1)}, u32[]{:S(2)}, u32[]{:S(2)}) %all-to-all-start) | async-done | bytes 1048608 | tf_op jit(solution)/shard_map/all_to_all | solution.py:401
  44.5 6.2 %shard_map.133 = bf16[4096,128]{1,0:T(8,128)(2,1)} custom-call(bf16[4096,128]{1,0:T(8,128)(2,1)S(1)} %bitcast.9, bf16[1024,512]{1,0:T(8,128)(2,1)S(1)} %shard_map.131.table_ref, bf16[528,256]{1,0:T(8,128)(2,1)S(1)} %shard_map.132.w_ref), custom_call_target="tpu_custom_call" | custom-call | tf_op jit(solution)/shard_map/pallas_call | solution.py:436
  50.7 7.9 %all-to-all-start.1 = ((bf16[64,8,8,128]{3,2,1,0:T(8,128)(2,1)}), bf16[64,8,8,128]{3,2,1,0:T(8,128)(2,1)}, u32[]{:S(2)}, u32[]{:S(2)}) async-start(bf16[64,8,8,128]{3,2,1,0:T(8,128)(2,1)} %bitcast.3), calls=%async_computation.1 | async-start | bytes 2097152 | tf_op jit(solution)/shard_map/all_to_all | solution.py:446
  59.6 2.6 %collective-permute-start.5 = (bf16[80,1152]{1,0:T(8,128)(2,1)S(1)}, bf16[80,1152]{1,0:T(8,128)(2,1)S(1)}, u32[]{:S(2)}, u32[]{:S(2)}) collective-permute-start(bf16[80,1152]{1,0:T(8,128)(2,1)S(1)} %shard_map.137.refs_0_), channel_id=1, source_target_pairs={{0,64},{64,128},{128,192},{192,0},{1,65},{65,129},{129,193},{193,1... | collective-permute-start | bytes 552968 | tf_op jit(solution)/shard_map/ppermute | solution.py:357
  62.2 4.5 %collective-permute-start.6 = (bf16[80,1152]{1,0:T(8,128)(2,1)S(1)}, bf16[80,1152]{1,0:T(8,128)(2,1)S(1)}, u32[]{:S(2)}, u32[]{:S(2)}) collective-permute-start(bf16[80,1152]{1,0:T(8,128)(2,1)S(1)} %shard_map.137.refs_0_), channel_id=1, source_target_pairs={{0,128},{64,192},{128,0},{192,64},{1,129},{65,193},{129,1},{193,65... | collective-permute-start | bytes 552968 | tf_op jit(solution)/shard_map/ppermute | solution.py:357
  66.7 2.7 %collective-permute-start.7 = (bf16[80,1152]{1,0:T(8,128)(2,1)S(1)}, bf16[80,1152]{1,0:T(8,128)(2,1)S(1)}, u32[]{:S(2)}, u32[]{:S(2)}) collective-permute-start(bf16[80,1152]{1,0:T(8,128)(2,1)S(1)} %shard_map.137.refs_0_), channel_id=1, source_target_pairs={{0,192},{64,0},{128,64},{192,128},{1,193},{65,1},{129,65},{193,129... | collective-permute-start | bytes 552968 | tf_op jit(solution)/shard_map/ppermute | solution.py:357
  69.4 14.5 %collective-permute-done.5.refs_1_ = bf16[80,1152]{1,0:T(8,128)(2,1)S(1)} collective-permute-done((bf16[80,1152]{1,0:T(8,128)(2,1)S(1)}, bf16[80,1152]{1,0:T(8,128)(2,1)S(1)}, u32[]{:S(2)}, u32[]{:S(2)}) %collective-permute-start.5) | collective-permute-done | bytes 184352 | tf_op jit(solution)/shard_map/ppermute | solution.py:357
  83.8 4.7 %collective-permute-done.6.refs_2_ = bf16[80,1152]{1,0:T(8,128)(2,1)S(1)} collective-permute-done((bf16[80,1152]{1,0:T(8,128)(2,1)S(1)}, bf16[80,1152]{1,0:T(8,128)(2,1)S(1)}, u32[]{:S(2)}, u32[]{:S(2)}) %collective-permute-start.6) | collective-permute-done | bytes 184352 | tf_op jit(solution)/shard_map/ppermute | solution.py:357
  92.8 2.7 %collective-permute-start.11 = (bf16[128,1152]{1,0:T(8,128)(2,1)}, bf16[128,1152]{1,0:T(8,128)(2,1)}, u32[]{:S(2)}, u32[]{:S(2)}) collective-permute-start(bf16[128,1152]{1,0:T(8,128)(2,1)} %get-tuple-element.33.refs_1_), channel_id=1, source_target_pairs={{0,4},{1,5},{2,6},{3,7},{4,0},{5,1},{6,2},{7,3},{8,12},{9,13},{10,... | collective-permute-start | bytes 884744 | tf_op jit(solution)/shard_map/ppermute | solution.py:433
  96.6 7.5 %collective-permute-done.8.refs_2_ = bf16[128,1152]{1,0:T(8,128)(2,1)S(1)} collective-permute-done((bf16[128,1152]{1,0:T(8,128)(2,1)}, bf16[128,1152]{1,0:T(8,128)(2,1)S(1)}, u32[]{:S(2)}, u32[]{:S(2)}) %collective-permute-start.8) | collective-permute-done | bytes 294944 | tf_op jit(solution)/shard_map/ppermute | solution.py:433
  104.8 2.7 %collective-permute-start.13 = (bf16[128,1152]{1,0:T(8,128)(2,1)}, bf16[128,1152]{1,0:T(8,128)(2,1)}, u32[]{:S(2)}, u32[]{:S(2)}) collective-permute-start(bf16[128,1152]{1,0:T(8,128)(2,1)} %get-tuple-element.33.refs_1_), channel_id=1, source_target_pairs={{0,6},{1,7},{2,0},{3,1},{4,2},{5,3},{6,4},{7,5},{8,14},{9,15},{10,... | collective-permute-start | bytes 884744 | tf_op jit(solution)/shard_map/ppermute | solution.py:433
  108.5 1.9 %shard_map.135.r_ref = f32[8,512,128]{2,1,0:T(8,128)S(1)} custom-call(bf16[8,512,128]{2,1,0:T(8,128)(2,1)S(1)} %copy-done.1, f32[2,8,512]{2,1,0:T(8,128)S(1)} %shard_map.128.left_ref, f32[2,8,512]{2,1,0:T(8,128)S(1)} %collective-permute-done.1.right_ref, f32[1,128]{1,0:T(1,128)S(1)} %bitcast.13), custom_call_target="tpu_custom_call" | custom-call | tf_op jit(solution)/shard_map/pallas_call | solution.py:449
  111.5 2.6 %shard_map.136 = (bf16[512,128]{1,0:T(8,128)(2,1)S(1)}, bf16[512,128]{1,0:T(8,128)(2,1)S(1)}, bf16[512,128]{1,0:T(8,128)(2,1)S(1)}, bf16[512,128]{1,0:T(8,128)(2...) custom-call(s32[1]{0:T(128)} %bitcast.me_ref, ...), custom_call_target="tpu_custom_call" | custom-call | tf_op jit(solution)/shard_map/pallas_call | solution.py:457
  114.1 1.7 shard_map.139.wa_ref
  115.9 5.2 %collective-permute-start.2 = (bf16[512,128]{1,0:T(8,128)(2,1)S(1)}, bf16[512,128]{1,0:T(8,128)(2,1)S(1)}, u32[]{:S(2)}, u32[]{:S(2)}) collective-permute-start(bf16[512,128]{1,0:T(8,128)(2,1)S(1)} %get-tuple-element.29), channel_id=1, source_target_pairs={{0,64},{64,128},{128,192},{192,0},{1,65},{65,129},{129,193},{193,1... | collective-permute-start | bytes 393224 | tf_op jit(solution)/shard_map/ppermute | solution.py:357
  122.6 2.2 %collective-permute-start.4 = (bf16[512,128]{1,0:T(8,128)(2,1)S(1)}, bf16[512,128]{1,0:T(8,128)(2,1)S(1)}, u32[]{:S(2)}, u32[]{:S(2)}) collective-permute-start(bf16[512,128]{1,0:T(8,128)(2,1)S(1)} %get-tuple-element.31), channel_id=1, source_target_pairs={{0,192},{64,0},{128,64},{192,128},{1,193},{65,1},{129,65},{193,129... | collective-permute-start | bytes 393224 | tf_op jit(solution)/shard_map/ppermute | solution.py:357
  125.5 3.3 %collective-permute-done.2.x1 = bf16[512,128]{1,0:T(8,128)(2,1)S(1)} collective-permute-done((bf16[512,128]{1,0:T(8,128)(2,1)S(1)}, bf16[512,128]{1,0:T(8,128)(2,1)S(1)}, u32[]{:S(2)}, u32[]{:S(2)}) %collective-permute-start.2) | collective-permute-done | bytes 131104 | tf_op jit(solution)/shard_map/ppermute | solution.py:357
  128.8 2.4 %collective-permute-start.19 = (bf16[512,128]{1,0:T(8,128)(2,1)S(1)}, bf16[512,128]{1,0:T(8,128)(2,1)S(1)}, u32[]{:S(2)}, u32[]{:S(2)}) collective-permute-start(bf16[512,128]{1,0:T(8,128)(2,1)S(1)} %get-tuple-element.41), channel_id=1, source_target_pairs={{0,128},{64,192},{128,0},{192,64},{1,129},{65,193},{129,1},{193,65... | collective-permute-start | bytes 393224 | tf_op jit(solution)/shard_map/ppermute | solution.py:357
  131.2 4.9 %collective-permute-done.3.x2 = bf16[512,128]{1,0:T(8,128)(2,1)S(1)} collective-permute-done((bf16[512,128]{1,0:T(8,128)(2,1)S(1)}, bf16[512,128]{1,0:T(8,128)(2,1)S(1)}, u32[]{:S(2)}, u32[]{:S(2)}) %collective-permute-start.3) | collective-permute-done | bytes 131104 | tf_op jit(solution)/shard_map/ppermute | solution.py:357
  136.3 7.6 %collective-permute-done.4.x3 = bf16[512,128]{1,0:T(8,128)(2,1)S(1)} collective-permute-done((bf16[512,128]{1,0:T(8,128)(2,1)S(1)}, bf16[512,128]{1,0:T(8,128)(2,1)S(1)}, u32[]{:S(2)}, u32[]{:S(2)}) %collective-permute-start.4) | collective-permute-done | bytes 131104 | tf_op jit(solution)/shard_map/ppermute | solution.py:357
  143.9 4.6 %shard_map.140 = (bf16[512,128]{1,0:T(8,128)(2,1)S(1)}, bf16[512,128]{1,0:T(8,128)(2,1)S(1)}, bf16[512,128]{1,0:T(8,128)(2,1)S(1)}, bf16[512,128]{1,0:T(8,128)(2,1)S(1)}) custom-call(s32[1]{0:T(128)} %bitcast.me_ref, bf16[512,128]{1,0:T(8,128)(2,1)S(1)} %get-tuple-element.28.refs_8_.x0, bf16[512,128]{1,0:T(8,128)(2,1)S(1)} %collective-permute-done.2.x1, ...), custom_call_target="tpu_custom_call" | custom-call | tf_op jit(solution)/shard_map/pallas_call | solution.py:474
  148.5 3.7 %collective-permute-start.15 = (bf16[512,128]{1,0:T(8,128)(2,1)S(1)}, bf16[512,128]{1,0:T(8,128)(2,1)S(1)}, u32[]{:S(2)}, u32[]{:S(2)}) collective-permute-start(bf16[512,128]{1,0:T(8,128)(2,1)S(1)} %get-tuple-element.36), channel_id=1, source_target_pairs={{0,64},{64,128},{128,192},{192,0},{1,65},{65,129},{129,193},{193,1... | collective-permute-start | bytes 393224 | tf_op jit(solution)/shard_map/ppermute | solution.py:357
  152.8 3.6 %collective-permute-start.17 = (bf16[512,128]{1,0:T(8,128)(2,1)S(1)}, bf16[512,128]{1,0:T(8,128)(2,1)S(1)}, u32[]{:S(2)}, u32[]{:S(2)}) collective-permute-start(bf16[512,128]{1,0:T(8,128)(2,1)S(1)} %get-tuple-element.38), channel_id=1, source_target_pairs={{0,192},{64,0},{128,64},{192,128},{1,193},{65,1},{129,65},{193,129... | collective-permute-start | bytes 393224 | tf_op jit(solution)/shard_map/ppermute | solution.py:357
  156.4 4.6 %shard_map.141 = (bf16[512,128]{1,0:T(8,128)(2,1)S(1)}, bf16[512,128]{1,0:T(8,128)(2,1)S(1)}, bf16[512,128]{1,0:T(8,128)(2,1)S(1)}, bf16[512,128]{1,0:T(8,128)(2,1)S(1)}) custom-call(s32[1]{0:T(128)} %bitcast.me_ref, bf16[512,128]{1,0:T(8,128)(2,1)S(1)} %get-tuple-element.39.x0, bf16[512,128]{1,0:T(8,128)(2,1)S(1)} %collective-permute-done.18.x1, ...), custom_call_target="tpu_custom_call" | custom-call | tf_op jit(solution)/shard_map/pallas_call | solution.py:474
  161.1 4.7 %collective-permute-start.22 = (bf16[512,128]{1,0:T(8,128)(2,1)S(1)}, bf16[512,128]{1,0:T(8,128)(2,1)S(1)}, u32[]{:S(2)}, u32[]{:S(2)}) collective-permute-start(bf16[512,128]{1,0:T(8,128)(2,1)S(1)} %get-tuple-element.45), channel_id=1, source_target_pairs={{0,128},{64,192},{128,0},{192,64},{1,129},{65,193},{129,1},{193,65... | collective-permute-start | bytes 393224 | tf_op jit(solution)/shard_map/ppermute | solution.py:357
  165.8 3.0 %collective-permute-start.23 = (bf16[512,128]{1,0:T(8,128)(2,1)S(1)}, bf16[512,128]{1,0:T(8,128)(2,1)S(1)}, u32[]{:S(2)}, u32[]{:S(2)}) collective-permute-start(bf16[512,128]{1,0:T(8,128)(2,1)S(1)} %get-tuple-element.46), channel_id=1, source_target_pairs={{0,192},{64,0},{128,64},{192,128},{1,193},{65,1},{129,65},{193,129... | collective-permute-start | bytes 393224 | tf_op jit(solution)/shard_map/ppermute | solution.py:357
  169.8 4.4 %collective-permute-done.22.refs_6_ = bf16[512,128]{1,0:T(8,128)(2,1)S(1)} collective-permute-done((bf16[512,128]{1,0:T(8,128)(2,1)S(1)}, bf16[512,128]{1,0:T(8,128)(2,1)S(1)}, u32[]{:S(2)}, u32[]{:S(2)}) %collective-permute-start.22) | collective-permute-done | bytes 131104 | tf_op jit(solution)/shard_map/ppermute | solution.py:357
  (78 shorter events, 21.8 us)
Async XLA Ops:
  1.2 15.2 %copy-start.1 = (bf16[8,512,128]{2,1,0:T(8,128)(2,1)S(1)}, bf16[8,512,128]{2,1,0:T(8,128)(2,1)}, u32[]{:S(2)}) copy-start(bf16[8,512,128]{2,1,0:T(8,128)(2,1)} %x_ref.5) | copy-start | bytes 3145732
  2.5 5.2 %collective-permute-start = (f32[2,8,512]{2,1,0:T(8,128)S(1)}, f32[2,8,512]{2,1,0:T(8,128)S(1)}, u32[]{:S(2)}, u32[]{:S(2)}) collective-permute-start(f32[2,8,512]{2,1,0:T(8,128)S(1)} %shard_map.127.left_ref), channel_id=1, source_target_pairs={{0,64},{64,0},{128,192},{192,128},{1,65},{65,1},{129,193},{193,129... | collective-permute-start | bytes 98312 | tf_op jit(solution)/shard_map/ppermute | solution.py:389
  7.7 8.7 %collective-permute-start.1 = (f32[2,8,512]{2,1,0:T(8,128)S(1)}, f32[2,8,512]{2,1,0:T(8,128)S(1)}, u32[]{:S(2)}, u32[]{:S(2)}) collective-permute-start(f32[2,8,512]{2,1,0:T(8,128)S(1)} %shard_map.128.left_ref), channel_id=1, source_target_pairs={{0,128},{64,192},{128,0},{192,64},{1,129},{65,193},{129,1},{193,65... | collective-permute-start | bytes 98312 | tf_op jit(solution)/shard_map/ppermute | solution.py:391
  20.0 24.4 %all-to-all-start = ((bf16[64,8,8,128]{3,2,1,0:T(8,128)(2,1)}), bf16[64,8,8,128]{3,2,1,0:T(8,128)(2,1)S(1)}, u32[]{:S(2)}, u32[]{:S(2)}) async-start(bf16[64,8,8,128]{3,2,1,0:T(8,128)(2,1)} %shard_map.130), calls=%async_computation | async-start | bytes 2097152 | tf_op jit(solution)/shard_map/all_to_all | solution.py:401
  44.5 14.2 %copy-start.19 = (bf16[512]{0:T(512)(128)(2,1)S(1)}, bf16[512]{0:T(512)(128)(2,1)}, u32[]{:S(2)}) copy-start(bf16[512]{0:T(512)(128)(2,1)} %param.21) | copy-start | bytes 3076
  44.5 14.3 %copy-start.18 = (bf16[128]{0:T(256)(128)(2,1)S(1)}, bf16[128]{0:T(256)(128)(2,1)}, u32[]{:S(2)}) copy-start(bf16[128]{0:T(256)(128)(2,1)} %param.23) | copy-start | bytes 772
  50.7 56.8 %copy-start.3 = (bf16[512,512]{1,0:T(8,128)(2,1)S(1)}, bf16[512,512]{1,0:T(8,128)(2,1)}, u32[]{:S(2)}) copy-start(bf16[512,512]{1,0:T(8,128)(2,1)} %constant.57.clone.refs_0_.table_ref) | copy-start | bytes 1572868
  50.7 57.8 %copy-start.17 = (f32[128]{0:T(128)S(1)}, f32[128]{0:T(128)}, u32[]{:S(2)}) copy-start(f32[128]{0:T(128)} %param.14) | copy-start | bytes 1540
  50.7 59.7 %all-to-all-start.1 = ((bf16[64,8,8,128]{3,2,1,0:T(8,128)(2,1)}), bf16[64,8,8,128]{3,2,1,0:T(8,128)(2,1)}, u32[]{:S(2)}, u32[]{:S(2)}) async-start(bf16[64,8,8,128]{3,2,1,0:T(8,128)(2,1)} %bitcast.3), calls=%async_computation.1 | async-start | bytes 2097152 | tf_op jit(solution)/shard_map/all_to_all | solution.py:446
  59.6 24.3 %collective-permute-start.5 = (bf16[80,1152]{1,0:T(8,128)(2,1)S(1)}, bf16[80,1152]{1,0:T(8,128)(2,1)S(1)}, u32[]{:S(2)}, u32[]{:S(2)}) collective-permute-start(bf16[80,1152]{1,0:T(8,128)(2,1)S(1)} %shard_map.137.refs_0_), channel_id=1, source_target_pairs={{0,64},{64,128},{128,192},{192,0},{1,65},{65,129},{129,193},{193,1... | collective-permute-start | bytes 552968 | tf_op jit(solution)/shard_map/ppermute | solution.py:357
  62.2 26.3 %collective-permute-start.6 = (bf16[80,1152]{1,0:T(8,128)(2,1)S(1)}, bf16[80,1152]{1,0:T(8,128)(2,1)S(1)}, u32[]{:S(2)}, u32[]{:S(2)}) collective-permute-start(bf16[80,1152]{1,0:T(8,128)(2,1)S(1)} %shard_map.137.refs_0_), channel_id=1, source_target_pairs={{0,128},{64,192},{128,0},{192,64},{1,129},{65,193},{129,1},{193,65... | collective-permute-start | bytes 552968 | tf_op jit(solution)/shard_map/ppermute | solution.py:357
  66.7 21.8 %collective-permute-start.7 = (bf16[80,1152]{1,0:T(8,128)(2,1)S(1)}, bf16[80,1152]{1,0:T(8,128)(2,1)S(1)}, u32[]{:S(2)}, u32[]{:S(2)}) collective-permute-start(bf16[80,1152]{1,0:T(8,128)(2,1)S(1)} %shard_map.137.refs_0_), channel_id=1, source_target_pairs={{0,192},{64,0},{128,64},{192,128},{1,193},{65,1},{129,65},{193,129... | collective-permute-start | bytes 552968 | tf_op jit(solution)/shard_map/ppermute | solution.py:357
  89.4 14.6 %collective-permute-start.8 = (bf16[128,1152]{1,0:T(8,128)(2,1)}, bf16[128,1152]{1,0:T(8,128)(2,1)S(1)}, u32[]{:S(2)}, u32[]{:S(2)}) collective-permute-start(bf16[128,1152]{1,0:T(8,128)(2,1)} %get-tuple-element.32.refs_0_), channel_id=1, source_target_pairs={{0,16},{1,17},{2,18},{3,19},{4,20},{5,21},{6,22},{7,23},{8,24},{9,... | collective-permute-start | bytes 884744 | tf_op jit(solution)/shard_map/ppermute | solution.py:433
  90.7 23.4 %collective-permute-start.10 = (bf16[128,1152]{1,0:T(8,128)(2,1)}, bf16[128,1152]{1,0:T(8,128)(2,1)}, u32[]{:S(2)}, u32[]{:S(2)}) collective-permute-start(bf16[128,1152]{1,0:T(8,128)(2,1)} %get-tuple-element.32.refs_0_), channel_id=1, source_target_pairs={{0,32},{1,33},{2,34},{3,35},{4,36},{5,37},{6,38},{7,39},{8,40},{9,... | collective-permute-start | bytes 884744 | tf_op jit(solution)/shard_map/ppermute | solution.py:433
  91.3 22.7 %collective-permute-start.9 = (bf16[128,1152]{1,0:T(8,128)(2,1)}, bf16[128,1152]{1,0:T(8,128)(2,1)}, u32[]{:S(2)}, u32[]{:S(2)}) collective-permute-start(bf16[128,1152]{1,0:T(8,128)(2,1)} %get-tuple-element.33.refs_1_), channel_id=1, source_target_pairs={{0,2},{1,3},{2,4},{3,5},{4,6},{5,7},{6,0},{7,1},{8,10},{9,11},{10,... | collective-permute-start | bytes 884744 | tf_op jit(solution)/shard_map/ppermute | solution.py:433
  92.8 21.3 %collective-permute-start.11 = (bf16[128,1152]{1,0:T(8,128)(2,1)}, bf16[128,1152]{1,0:T(8,128)(2,1)}, u32[]{:S(2)}, u32[]{:S(2)}) collective-permute-start(bf16[128,1152]{1,0:T(8,128)(2,1)} %get-tuple-element.33.refs_1_), channel_id=1, source_target_pairs={{0,4},{1,5},{2,6},{3,7},{4,0},{5,1},{6,2},{7,3},{8,12},{9,13},{10,... | collective-permute-start | bytes 884744 | tf_op jit(solution)/shard_map/ppermute | solution.py:433
  95.5 18.6 %collective-permute-start.12 = (bf16[128,1152]{1,0:T(8,128)(2,1)}, bf16[128,1152]{1,0:T(8,128)(2,1)}, u32[]{:S(2)}, u32[]{:S(2)}) collective-permute-start(bf16[128,1152]{1,0:T(8,128)(2,1)} %get-tuple-element.32.refs_0_), channel_id=1, source_target_pairs={{0,48},{1,49},{2,50},{3,51},{4,52},{5,53},{6,54},{7,55},{8,56},{9,... | collective-permute-start | bytes 884744 | tf_op jit(solution)/shard_map/ppermute | solution.py:433
  104.8 9.3 %collective-permute-start.13 = (bf16[128,1152]{1,0:T(8,128)(2,1)}, bf16[128,1152]{1,0:T(8,128)(2,1)}, u32[]{:S(2)}, u32[]{:S(2)}) collective-permute-start(bf16[128,1152]{1,0:T(8,128)(2,1)} %get-tuple-element.33.refs_1_), channel_id=1, source_target_pairs={{0,6},{1,7},{2,0},{3,1},{4,2},{5,3},{6,4},{7,5},{8,14},{9,15},{10,... | collective-permute-start | bytes 884744 | tf_op jit(solution)/shard_map/ppermute | solution.py:433
  114.1 29.8 %copy-start.13 = (f32[512]{0:T(512)S(1)}, f32[512]{0:T(512)}, u32[]{:S(2)}) copy-start(f32[512]{0:T(512)} %param.19) | copy-start | bytes 6148
  115.8 28.1 %collective-permute-start.14 = (bf16[1024,1152]{1,0:T(8,128)(2,1)S(1)}, bf16[1024,1152]{1,0:T(8,128)(2,1)S(1)}, u32[]{:S(2)}, u32[]{:S(2)}) collective-permute-start(bf16[1024,1152]{1,0:T(8,128)(2,1)S(1)} %shard_map.139.wa_ref), channel_id=1, source_target_pairs={{0,1},{1,0},{2,3},{3,2},{4,5},{5,4},{6,7},{7,6},{8,9},{9,8},{10,11... | collective-permute-start | bytes 7077896 | tf_op jit(solution)/shard_map/ppermute | solution.py:470
  115.9 12.9 %collective-permute-start.2 = (bf16[512,128]{1,0:T(8,128)(2,1)S(1)}, bf16[512,128]{1,0:T(8,128)(2,1)S(1)}, u32[]{:S(2)}, u32[]{:S(2)}) collective-permute-start(bf16[512,128]{1,0:T(8,128)(2,1)S(1)} %get-tuple-element.29), channel_id=1, source_target_pairs={{0,64},{64,128},{128,192},{192,0},{1,65},{65,129},{129,193},{193,1... | collective-permute-start | bytes 393224 | tf_op jit(solution)/shard_map/ppermute | solution.py:357
  121.1 15.0 %collective-permute-start.3 = (bf16[512,128]{1,0:T(8,128)(2,1)S(1)}, bf16[512,128]{1,0:T(8,128)(2,1)S(1)}, u32[]{:S(2)}, u32[]{:S(2)}) collective-permute-start(bf16[512,128]{1,0:T(8,128)(2,1)S(1)} %get-tuple-element.30), channel_id=1, source_target_pairs={{0,128},{64,192},{128,0},{192,64},{1,129},{65,193},{129,1},{193,65... | collective-permute-start | bytes 393224 | tf_op jit(solution)/shard_map/ppermute | solution.py:357
  122.6 21.3 %collective-permute-start.4 = (bf16[512,128]{1,0:T(8,128)(2,1)S(1)}, bf16[512,128]{1,0:T(8,128)(2,1)S(1)}, u32[]{:S(2)}, u32[]{:S(2)}) collective-permute-start(bf16[512,128]{1,0:T(8,128)(2,1)S(1)} %get-tuple-element.31), channel_id=1, source_target_pairs={{0,192},{64,0},{128,64},{192,128},{1,193},{65,1},{129,65},{193,129... | collective-permute-start | bytes 393224 | tf_op jit(solution)/shard_map/ppermute | solution.py:357
  124.8 28.0 %collective-permute-start.18 = (bf16[512,128]{1,0:T(8,128)(2,1)S(1)}, bf16[512,128]{1,0:T(8,128)(2,1)S(1)}, u32[]{:S(2)}, u32[]{:S(2)}) collective-permute-start(bf16[512,128]{1,0:T(8,128)(2,1)S(1)} %get-tuple-element.40), channel_id=1, source_target_pairs={{0,64},{64,128},{128,192},{192,0},{1,65},{65,129},{129,193},{193,1... | collective-permute-start | bytes 393224 | tf_op jit(solution)/shard_map/ppermute | solution.py:357
  128.8 27.6 %collective-permute-start.19 = (bf16[512,128]{1,0:T(8,128)(2,1)S(1)}, bf16[512,128]{1,0:T(8,128)(2,1)S(1)}, u32[]{:S(2)}, u32[]{:S(2)}) collective-permute-start(bf16[512,128]{1,0:T(8,128)(2,1)S(1)} %get-tuple-element.41), channel_id=1, source_target_pairs={{0,128},{64,192},{128,0},{192,64},{1,129},{65,193},{129,1},{193,65... | collective-permute-start | bytes 393224 | tf_op jit(solution)/shard_map/ppermute | solution.py:357
  136.1 20.2 %collective-permute-start.20 = (bf16[512,128]{1,0:T(8,128)(2,1)S(1)}, bf16[512,128]{1,0:T(8,128)(2,1)S(1)}, u32[]{:S(2)}, u32[]{:S(2)}) collective-permute-start(bf16[512,128]{1,0:T(8,128)(2,1)S(1)} %get-tuple-element.42), channel_id=1, source_target_pairs={{0,192},{64,0},{128,64},{192,128},{1,193},{65,1},{129,65},{193,129... | collective-permute-start | bytes 393224 | tf_op jit(solution)/shard_map/ppermute | solution.py:357
  148.5 17.2 %collective-permute-start.15 = (bf16[512,128]{1,0:T(8,128)(2,1)S(1)}, bf16[512,128]{1,0:T(8,128)(2,1)S(1)}, u32[]{:S(2)}, u32[]{:S(2)}) collective-permute-start(bf16[512,128]{1,0:T(8,128)(2,1)S(1)} %get-tuple-element.36), channel_id=1, source_target_pairs={{0,64},{64,128},{128,192},{192,0},{1,65},{65,129},{129,193},{193,1... | collective-permute-start | bytes 393224 | tf_op jit(solution)/shard_map/ppermute | solution.py:357
  152.2 16.6 %collective-permute-start.16 = (bf16[512,128]{1,0:T(8,128)(2,1)S(1)}, bf16[512,128]{1,0:T(8,128)(2,1)S(1)}, u32[]{:S(2)}, u32[]{:S(2)}) collective-permute-start(bf16[512,128]{1,0:T(8,128)(2,1)S(1)} %get-tuple-element.37), channel_id=1, source_target_pairs={{0,128},{64,192},{128,0},{192,64},{1,129},{65,193},{129,1},{193,65... | collective-permute-start | bytes 393224 | tf_op jit(solution)/shard_map/ppermute | solution.py:357
  152.8 16.0 %collective-permute-start.17 = (bf16[512,128]{1,0:T(8,128)(2,1)S(1)}, bf16[512,128]{1,0:T(8,128)(2,1)S(1)}, u32[]{:S(2)}, u32[]{:S(2)}) collective-permute-start(bf16[512,128]{1,0:T(8,128)(2,1)S(1)} %get-tuple-element.38), channel_id=1, source_target_pairs={{0,192},{64,0},{128,64},{192,128},{1,193},{65,1},{129,65},{193,129... | collective-permute-start | bytes 393224 | tf_op jit(solution)/shard_map/ppermute | solution.py:357
  161.0 8.8 %collective-permute-start.21 = (bf16[512,128]{1,0:T(8,128)(2,1)S(1)}, bf16[512,128]{1,0:T(8,128)(2,1)S(1)}, u32[]{:S(2)}, u32[]{:S(2)}) collective-permute-start(bf16[512,128]{1,0:T(8,128)(2,1)S(1)} %get-tuple-element.44), channel_id=1, source_target_pairs={{0,64},{64,128},{128,192},{192,0},{1,65},{65,129},{129,193},{193,1... | collective-permute-start | bytes 393224 | tf_op jit(solution)/shard_map/ppermute | solution.py:357
  161.1 13.1 %collective-permute-start.22 = (bf16[512,128]{1,0:T(8,128)(2,1)S(1)}, bf16[512,128]{1,0:T(8,128)(2,1)S(1)}, u32[]{:S(2)}, u32[]{:S(2)}) collective-permute-start(bf16[512,128]{1,0:T(8,128)(2,1)S(1)} %get-tuple-element.45), channel_id=1, source_target_pairs={{0,128},{64,192},{128,0},{192,64},{1,129},{65,193},{129,1},{193,65... | collective-permute-start | bytes 393224 | tf_op jit(solution)/shard_map/ppermute | solution.py:357
  165.8 8.5 %collective-permute-start.23 = (bf16[512,128]{1,0:T(8,128)(2,1)S(1)}, bf16[512,128]{1,0:T(8,128)(2,1)S(1)}, u32[]{:S(2)}, u32[]{:S(2)}) collective-permute-start(bf16[512,128]{1,0:T(8,128)(2,1)S(1)} %get-tuple-element.46), channel_id=1, source_target_pairs={{0,192},{64,0},{128,64},{192,128},{1,193},{65,1},{129,65},{193,129... | collective-permute-start | bytes 393224 | tf_op jit(solution)/shard_map/ppermute | solution.py:357
  (14 other events, 48.0 us)

commit v3 on v2

--- a/solution.py
+++ b/solution.py
@@ -40,17 +40,14 @@
     rows, _, lanes = x_ref.shape
     ones = jnp.ones((8, lanes), bf16)
 
-    def body(row, carry):
+    for row in range(rows):
         x = x_ref[row]
         wide = x.astype(f32)
         square = wide * wide
         high = square.astype(bf16)
         low = (square - high.astype(f32)).astype(bf16)
-        o_ref[0, pl.ds(row, 1), :] = mm_t(ones, x)[0:1]
-        o_ref[1, pl.ds(row, 1), :] = (mm_t(ones, high) + mm_t(ones, low))[0:1]
-        return carry
-
-    lax.fori_loop(0, rows, body, 0, unroll=2)
+        o_ref[0, row : row + 1, :] = mm_t(ones, x)[0:1]
+        o_ref[1, row : row + 1, :] = (mm_t(ones, high) + mm_t(ones, low))[0:1]
 
 
 def add_kernel(left_ref, right_ref, o_ref):
@@ -70,20 +67,17 @@
 
 
 def normed_row(source, flipped, row, rows, gain):
-    column = lax.broadcasted_iota(jnp.int32, flipped.shape, 1)
-    center = jnp.sum(jnp.where(column == row, flipped, 0.0), axis=1, keepdims=True)
-    factor = jnp.sum(jnp.where(column == row + rows, flipped, 0.0), axis=1, keepdims=True)
-    return (source - center) * factor * gain
-
-
-def forward_kernel(channels, scale, x_ref, left_ref, right_ref, gain_ref, table_ref, o_ref, f_ref):
+    return (source - flipped[:, row : row + 1]) * flipped[:, rows + row : rows + row + 1] * gain
+
+
+def forward_kernel(channels, scale, x_ref, left_ref, right_ref, gain_ref, table_ref, o_ref):
     rows, _, lanes = x_ref.shape
     owners = o_ref.shape[0]
-    f_ref[...] = moments(left_ref, right_ref, channels)
-
-    def body(pair, carry):
+    flipped = moments(left_ref, right_ref, channels)
+    gain = gain_ref[...]
+    for pair in range(rows // 2):
         sides = [
-            normed_row(x_ref[row].astype(f32), f_ref[...], row, rows, gain_ref[...]).astype(bf16)
+            normed_row(x_ref[row].astype(f32), flipped, row, rows, gain).astype(bf16)
             for row in (2 * pair, 2 * pair + 1)
         ]
         out = mm(table_ref[...], jnp.concatenate(sides, axis=1)) * scale
@@ -91,21 +85,14 @@
             o_ref[:, 2 * pair + side] = (
                 out[:, side * lanes : (side + 1) * lanes].reshape(owners, -1, lanes).astype(bf16)
             )
-        return carry
-
-    lax.fori_loop(0, rows // 2, body, 0)
-
-
-def residual_kernel(channels, x_ref, left_ref, right_ref, gain_ref, o_ref, f_ref):
+
+
+def residual_kernel(channels, x_ref, left_ref, right_ref, gain_ref, o_ref):
     rows = x_ref.shape[0]
-    f_ref[...] = moments(left_ref, right_ref, channels)
-
-    def body(row, carry):
+    flipped = moments(left_ref, right_ref, channels)
+    for row in range(rows):
         source = x_ref[row].astype(f32)
-        o_ref[row] = normed_row(source, f_ref[...], row, rows, gain_ref[...]) + source
-        return carry
-
-    lax.fori_loop(0, rows, body, 0)
+        o_ref[row] = normed_row(source, flipped, row, rows, gain_ref[...]) + source
 
 
 def flip_kernel(per_owner, lanes, table_ref, i_ref):
@@ -165,8 +152,8 @@
                 pl.ds(part * count + k, height, stride=step), :
             ].astype(bf16)
 
-    def body(half, carry):
-        span = pl.ds(pl.multiple_of(half * 2 * lanes, 2 * lanes), 2 * lanes)
+    for half in range(count // 2):
+        span = pl.ds(half * 2 * lanes, 2 * lanes)
         cos, sin = table_ref[0:height, :], table_ref[height:, :]
         real, imag = real_ref[:, span], imag_ref[:, span]
         out_real = (mm(cos, real) + mm(sin, imag)) * scale
@@ -187,46 +174,50 @@
             k = half * 2 + side
             wide_ref[pl.ds(k, height, stride=step), :] = back_real[:, cut]
             wide_ref[pl.ds(count + k, height, stride=step), :] = back_imag[:, cut]
-        return carry
-
-    lax.fori_loop(0, count // 2, body, 0)
     o_ref[...] = wide_ref[...].astype(bf16)
 
 
-def inverse_kernel(scale, me_ref, x_ref, table_ref, r_ref, *refs):
-    *o_refs, m_ref = refs
+def inverse_kernel(scale, me_ref, x_ref, table_ref, r_ref, *o_refs):
     ways = len(o_refs) // 2
-    rows, _, lanes = r_ref.shape
-
-    def body(pair, carry):
+    _, _, lanes = r_ref.shape
+    for shift in range(ways):
+        owner = lax.rem(me_ref[0] + shift, ways)
         sides = [
-            x_ref[:, 2 * pair + side].astype(f32).reshape(-1, lanes).astype(bf16) for side in range(2)
+            x_ref[:, 2 * owner + side].astype(f32).reshape(-1, lanes).astype(bf16) for side in range(2)
         ]
         out = mm(table_ref[...], jnp.concatenate(sides, axis=1)) * scale
         for side in range(2):
-            m_ref[side, pair] = (out[:, side * lanes : (side + 1) * lanes] + r_ref[2 * pair + side]).astype(bf16)
-        return carry
-
-    lax.fori_loop(0, rows // 2, body, 0)
-    for shift in range(ways):
-        for side in range(2):
-            o_refs[side * ways + shift][...] = m_ref[side, lax.rem(me_ref[0] + shift, ways)]
+            o_refs[side * ways + shift][...] = (
+                out[:, side * lanes : (side + 1) * lanes] + r_ref[2 * owner + side]
+            ).astype(bf16)
 
 
 def gelu(values):
     return 0.5 * values * (1.0 + lax.erf(values * math.sqrt(0.5)))
 
 
+def eye(rows, columns):
+    row = lax.broadcasted_iota(jnp.int32, (rows, columns), 0)
+    column = lax.broadcasted_iota(jnp.int32, (rows, columns), 1)
+    return jnp.where(row == column, 1.0, 0.0)
+
+
 def mlp_kernel(
-    tile, me_ref, x0, x1, x2, x3, wa_ref, wb_ref, gain_ref, bias_ref, y0, y1, y2, y3, x_ref, y_ref, n_ref, a_ref
+    tile, me_ref, x0, x1, x2, x3, wa_ref, wb_ref, gain_ref, bias_ref, y0, y1, y2, y3, x_ref, y_ref
 ):
     ways, tokens, lanes = x_ref.shape
     channels = ways * lanes
     me = me_ref[0]
     for shift, ref in enumerate((x0, x1, x2, x3)):
         x_ref[lax.rem(me + ways - shift, ways)] = ref[...]
-    unit = jnp.ones((8, lanes), bf16)
+    unit = eye(8, lanes).astype(bf16)
     hidden_block = 512
+    blocks = [
+        (ref, pl.ds(start, hidden_block))
+        for ref in (wa_ref, wb_ref)
+        for start in range(0, ref.shape[0], hidden_block)
+    ]
+    biases = [mm_t(unit, ref[span, 2 * channels :])[0:1] for ref, span in blocks]
 
     def body(index, carry):
         span = pl.ds(pl.multiple_of(index * tile, tile), tile)
@@ -236,25 +227,21 @@
         center = jnp.sum(total, axis=1, keepdims=True) / channels
         spread = jnp.sum(square, axis=1, keepdims=True) / channels - center * center
         inverse = lax.rsqrt(spread + norm_eps)
-        for b, m in enumerate(mixed):
+        normed = jnp.concatenate(
+            [
+                ((m - center) * inverse * gain_ref[:, b * lanes : (b + 1) * lanes]).astype(bf16)
+                for b, m in enumerate(mixed)
+            ],
+            axis=1,
+        )
+        acc = None
+        for (ref, rows), bias in zip(blocks, biases):
+            hidden = gelu(mm_t(normed, ref[rows, :channels]) + bias).astype(bf16)
+            product = mm(hidden, ref[rows, channels : 2 * channels])
+            acc = product if acc is None else acc + product
+        for b in range(ways):
             cut = slice(b * lanes, (b + 1) * lanes)
-            n_ref[:, cut] = ((m - center) * inverse * gain_ref[:, cut]).astype(bf16)
-            a_ref[:, cut] = m + bias_ref[b : b + 1, :]
-
-        def block(place, inner):
-            rows = pl.ds(pl.multiple_of(place * hidden_block, hidden_block), hidden_block)
-            product = None
-            for ref in (wa_ref, wb_ref):
-                bias = mm_t(unit, ref[rows, 2 * channels :])[0:1]
-                hidden = gelu(mm_t(n_ref[...], ref[rows, :channels]) + bias).astype(bf16)
-                part = mm(hidden, ref[rows, channels : 2 * channels])
-                product = part if product is None else product + part
-            a_ref[...] += product
-            return inner
-
-        lax.fori_loop(0, wa_ref.shape[0] // hidden_block, block, 0)
-        for b in range(ways):
-            y_ref[b, span, :] = a_ref[:, b * lanes : (b + 1) * lanes].astype(bf16)
+            y_ref[b, span, :] = (mixed[b] + acc[:, cut] + bias_ref[b : b + 1, :]).astype(bf16)
         return carry
 
     lax.fori_loop(0, tokens // tile, body, 0)
@@ -271,29 +258,27 @@
         o_ref[lax.rem(me_ref[0] + ways - shift, ways), pl.ds(place // ways * half, half), :] = part[...]
 
 
-def piece_kernel(
-    piece_ref, one_ref, bias_ref, two_ref, out_ref, o_ref, flat_ref
-):
+def piece_kernel(piece_ref, one_ref, bias_ref, two_ref, out_ref, o_ref, flat_ref):
     channels = one_ref.shape[0]
     lanes = o_ref.shape[1] - 2 * channels
-    units = (o_ref.shape[0] - 16) // 2
-    row = lax.broadcasted_iota(jnp.int32, (lanes, lanes), 0)
-    column = lax.broadcasted_iota(jnp.int32, (lanes, lanes), 1)
-    unit = jnp.where(row == column, 1.0, 0.0).astype(bf16)
+    units = o_ref.shape[0] // 2
+    square = eye(lanes, lanes)
+    place = lax.broadcasted_iota(jnp.int32, (units, lanes), 1)
+    extra = jnp.sum(square * out_ref[...].astype(f32), axis=1, keepdims=True)
     for half in range(2):
         first = half * (one_ref.shape[1] // 2) + piece_ref[half] * units
         slab = pl.ds(pl.multiple_of(first // lanes * lanes, lanes), lanes)
-        bias = jnp.broadcast_to(bias_ref[:, slab].astype(f32), (lanes, lanes))
-        flat_ref[:, 0:channels] = mm_t(unit, one_ref[:, slab])
-        flat_ref[:, channels:] = jnp.where(row == column, bias, 0.0)
+        flat_ref[:, 0:channels] = mm_t(square.astype(bf16), one_ref[:, slab])
+        flat_ref[:, channels:] = square * bias_ref[:, slab].astype(f32)
         within = pl.ds(pl.multiple_of(lax.rem(first, lanes), units), units)
         target = pl.ds(half * units, units)
         o_ref[target, 0:channels] = flat_ref[within, 0:channels].astype(bf16)
         o_ref[target, channels : 2 * channels] = two_ref[pl.ds(pl.multiple_of(first, units), units), :]
-        o_ref[target, 2 * channels :] = flat_ref[within, channels:].astype(bf16)
-    tail = pl.ds(2 * units, 16)
-    o_ref[tail, :] = jnp.zeros((16, o_ref.shape[1]), bf16)
-    o_ref[tail, 0:lanes] = jnp.broadcast_to(out_ref[...].astype(f32), (16, lanes)).astype(bf16)
+        bias = jnp.sum(flat_ref[within, channels:], axis=1, keepdims=True)
+        near = extra[half * units : (half + 1) * units]
+        far = extra[(2 + half) * units : (3 + half) * units]
+        values = jnp.where(place == 0, bias, jnp.where(place == 1, near, jnp.where(place == 2, far, 0.0)))
+        o_ref[target, 2 * channels :] = values.astype(bf16)
 
 
 def prep_kernel(w1_ref, b1_ref, w2_ref, b2_ref, o_ref):
@@ -317,12 +302,13 @@
     for place, part in enumerate(parts):
         for half, ref in enumerate((first_ref, second_ref)):
             ref[place * size : (place + 1) * size, :] = part[half * size : (half + 1) * size, :]
-        row = part[2 * size : 2 * size + 16, 0:lanes].astype(f32)[0:1]
+        found = mm_t(eye(8, lanes).astype(bf16), part[:, part.shape[1] - lanes :])
+        row = jnp.concatenate([found[1:2], found[2:3]], axis=1)
         bias_ref[pl.ds(lax.rem(me_ref[0] + ways - place, ways), 1), :] = row
 
 
 def join_kernel(*refs):
-    *parts, after_ref, o_ref = refs
+    *parts, o_ref = refs
     start = 0
     for part in parts:
         o_ref[start : start + part.shape[0], :] = part[...]
@@ -396,7 +382,6 @@
         partial(forward_kernel, channels, first_scale),
         shape((owners, rows, 2 * per_owner, lanes), bf16),
         vmem(5),
-        scratch=[pltpu.VMEM((width, 2 * rows), f32)],
     )(tokens, left, right, gain, table)
     columns = lax.all_to_all(spectra, "rows", split_axis=0, concat_axis=0)
 
@@ -407,7 +392,7 @@
     piece = jnp.stack([across * 2 + core, along * 2 + core])
     mine = call(
         piece_kernel,
-        shape((units + 16, 2 * channels + lanes), bf16),
+        shape((units, 2 * channels + lanes), bf16),
         [smem] + vmem(4),
         scratch=[pltpu.VMEM((lanes, channels + lanes), f32)],
     )(piece, fc1_weight, fc1_bias.reshape(1, -1), fc2_weight, fc2_bias.reshape(1, lanes))
@@ -450,7 +435,6 @@
         partial(residual_kernel, channels),
         shape((rows, width, lanes), f32),
         vmem(4),
-        scratch=[pltpu.VMEM((width, 2 * rows), f32)],
     )(tokens, left, right, gain_in.reshape(1, lanes))
     inverse = call(partial(flip_kernel, per_owner, lanes), shape((width, width), bf16), vmem(1))(forward)
     share = rows // ways * width // 2
@@ -458,15 +442,14 @@
         partial(inverse_kernel, first_scale),
         [shape((share, lanes), bf16)] * (2 * ways),
         [smem] + vmem(3),
-        scratch=[pltpu.VMEM((2, ways, width, lanes), bf16)],
     )(me, returned, inverse, resid)
     halves = [mixed[:ways], mixed[ways:]]
     whole_a = [halves[0][0]] + shifts(lambda s: halves[0][s], "chan", ways)
     near = call(
         join_kernel,
         shape((2 * ring_x * parts[0].shape[0], parts[0].shape[1]), bf16),
-        vmem(len(parts)) + [pl.BlockSpec(memory_space=pl.ANY)],
-    )(*parts, mixed[0])
+        vmem(len(parts)),
+    )(*parts)
     far = lax.ppermute(near, "rows", [(i, i ^ 1) for i in range(owners)])
     whole_b = [halves[1][0]] + shifts(lambda s: halves[1][s], "chan", ways)
 
@@ -478,8 +461,6 @@
             scratch=[
                 pltpu.VMEM((ways, share, lanes), bf16),
                 pltpu.VMEM((ways, share, lanes), bf16),
-                pltpu.VMEM((256, channels), bf16),
-                pltpu.VMEM((256, channels), f32),
             ],
         )(me, *whole, near, far, gain_out.reshape(1, channels), out_bias)
 

time: 176 us -> 182 us (1.034)
  the two profiles are of different devices: /device:TPU:4 before, /device:TPU:1 now
where the time goes in v3:
time: 182 us; the launch traced here: 181 us
  starting transfers between devices  79.2 us (44%)
  waiting for transfers between devices  62 us (34%)
  Pallas kernels  25.8 us (14%)
  local copies, waits for them, and re-layouts  13.6 us (7%)
    ppermute x15, waiting for transfers between devices, shifts(): lax.ppermute(value_of(shift), axis, [(i, (i + shift) % ways) for i in ran...  39.4 us
    ppermute x15, starting transfers between devices, shifts(): lax.ppermute(value_of(shift), axis, [(i, (i + shift) % ways) for i in ran...  34.2 us
    unnamed x50, local copies, waits for them, and re-layouts  13.6 us
    all_to_all x1, waiting for transfers between devices, local(): lax.all_to_all(back.reshape(owners, rows, 2 * per_owner, lanes), 'rows',...  13.1 us
    ppermute x6, starting transfers between devices, local(): parts.append(lax.ppermute(sides[half], 'rows', ring[half]))  10.9 us
    all_to_all x1, starting transfers between devices, local(): columns = lax.all_to_all(spectra, 'rows', split_axis=0, concat_axis=0)  10.7 us
    pallas_call x2, Pallas kernels, mlp(): call(partial(mlp_kernel, 256), [shape((share, lanes), bf16)] * ways, [sme...  10.6 us
    all_to_all x1, starting transfers between devices, local(): lax.all_to_all(back.reshape(owners, rows, 2 * per_owner, lanes), 'rows',...  10.2 us
  transfers between devices with their start and end apart: 26, of which 11 were waited for; matrix products, arithmetic and copies ran while one was open for 0% of the time, Pallas kernels for 12%

profile of v3, /device:TPU:1, one launch (start us, length us, event | category | flops | bytes accessed | tf_op | source)
XLA Modules:
  0.0 181.0 jit_solution(17305174952148771793)
XLA Ops:
  2.1 3.8 %collective-permute-start = (f32[2,8,512]{2,1,0:T(8,128)S(1)}, f32[2,8,512]{2,1,0:T(8,128)S(1)}, u32[]{:S(2)}, u32[]{:S(2)}) collective-permute-start(f32[2,8,512]{2,1,0:T(8,128)S(1)} %shard_map.127.left_ref), channel_id=1, source_target_pairs={{0,64},{64,0},{128,192},{192,128},{1,65},{65,1},{129,193},{193,129... | collective-permute-start | bytes 98312 | tf_op jit(solution)/shard_map/ppermute | solution.py:375
  7.3 6.3 %collective-permute-start.1 = (f32[2,8,512]{2,1,0:T(8,128)S(1)}, f32[2,8,512]{2,1,0:T(8,128)S(1)}, u32[]{:S(2)}, u32[]{:S(2)}) collective-permute-start(f32[2,8,512]{2,1,0:T(8,128)S(1)} %shard_map.128.left_ref), channel_id=1, source_target_pairs={{0,128},{64,192},{128,0},{192,64},{1,129},{65,193},{129,1},{193,65... | collective-permute-start | bytes 98312 | tf_op jit(solution)/shard_map/ppermute | solution.py:377
  15.4 2.7 %shard_map.130 = bf16[64,8,8,128]{3,2,1,0:T(8,128)(2,1)} custom-call(bf16[8,512,128]{2,1,0:T(8,128)(2,1)S(1)} %copy-done.1, f32[2,8,512]{2,1,0:T(8,128)S(1)} %shard_map.128.left_ref, f32[2,8,512]{2,1,0:T(8,128)S(1)} %collective-permute-done.1.right_ref, f32[1,128]{1,0:T(1,128)S(1)} %get-tuple-element.26.gain_ref, ...), custom_call_target="tpu_custom_call" | custom-call | tf_op jit(solution)/shard_map/pallas_call | solution.py:381
  18.1 10.7 %all-to-all-start = ((bf16[64,8,8,128]{3,2,1,0:T(8,128)(2,1)}), bf16[64,8,8,128]{3,2,1,0:T(8,128)(2,1)}, u32[]{:S(2)}, u32[]{:S(2)}) async-start(bf16[64,8,8,128]{3,2,1,0:T(8,128)(2,1)} %shard_map.130), calls=%async_computation | async-start | bytes 2097152 | tf_op jit(solution)/shard_map/all_to_all | solution.py:386
  29.8 2.3 %collective-permute-start.5 = (bf16[64,1152]{1,0:T(8,128)(2,1)S(1)}, bf16[64,1152]{1,0:T(8,128)(2,1)S(1)}, u32[]{:S(2)}, u32[]{:S(2)}) collective-permute-start(bf16[64,1152]{1,0:T(8,128)(2,1)S(1)} %shard_map.137.refs_0_), channel_id=1, source_target_pairs={{0,64},{64,128},{128,192},{192,0},{1,65},{65,129},{129,193},{193,1... | collective-permute-start | bytes 442376 | tf_op jit(solution)/shard_map/ppermute | solution.py:343
  32.1 4.2 %collective-permute-start.6 = (bf16[64,1152]{1,0:T(8,128)(2,1)S(1)}, bf16[64,1152]{1,0:T(8,128)(2,1)S(1)}, u32[]{:S(2)}, u32[]{:S(2)}) collective-permute-start(bf16[64,1152]{1,0:T(8,128)(2,1)S(1)} %shard_map.137.refs_0_), channel_id=1, source_target_pairs={{0,128},{64,192},{128,0},{192,64},{1,129},{65,193},{129,1},{193,65... | collective-permute-start | bytes 442376 | tf_op jit(solution)/shard_map/ppermute | solution.py:343
  36.4 2.4 %collective-permute-start.7 = (bf16[64,1152]{1,0:T(8,128)(2,1)S(1)}, bf16[64,1152]{1,0:T(8,128)(2,1)S(1)}, u32[]{:S(2)}, u32[]{:S(2)}) collective-permute-start(bf16[64,1152]{1,0:T(8,128)(2,1)S(1)} %shard_map.137.refs_0_), channel_id=1, source_target_pairs={{0,192},{64,0},{128,64},{192,128},{1,193},{65,1},{129,65},{193,129... | collective-permute-start | bytes 442376 | tf_op jit(solution)/shard_map/ppermute | solution.py:343
  38.7 12.4 %collective-permute-done.5.refs_1_ = bf16[64,1152]{1,0:T(8,128)(2,1)S(1)} collective-permute-done((bf16[64,1152]{1,0:T(8,128)(2,1)S(1)}, bf16[64,1152]{1,0:T(8,128)(2,1)S(1)}, u32[]{:S(2)}, u32[]{:S(2)}) %collective-permute-start.5) | collective-permute-done | bytes 147488 | tf_op jit(solution)/shard_map/ppermute | solution.py:343
  51.1 4.3 %collective-permute-done.6.refs_2_ = bf16[64,1152]{1,0:T(8,128)(2,1)S(1)} collective-permute-done((bf16[64,1152]{1,0:T(8,128)(2,1)S(1)}, bf16[64,1152]{1,0:T(8,128)(2,1)S(1)}, u32[]{:S(2)}, u32[]{:S(2)}) %collective-permute-start.6) | collective-permute-done | bytes 147488 | tf_op jit(solution)/shard_map/ppermute | solution.py:343
  57.0 2.6 %collective-permute-start.10 = (bf16[128,1152]{1,0:T(8,128)(2,1)S(1)}, bf16[128,1152]{1,0:T(8,128)(2,1)S(1)}, u32[]{:S(2)}, u32[]{:S(2)}) collective-permute-start(bf16[128,1152]{1,0:T(8,128)(2,1)S(1)} %get-tuple-element.32.refs_0_), channel_id=1, source_target_pairs={{0,32},{1,33},{2,34},{3,35},{4,36},{5,37},{6,38},{7,39},{8,40},{9,... | collective-permute-start | bytes 884744 | tf_op jit(solution)/shard_map/ppermute | solution.py:418
  60.9 2.4 %collective-permute-start.11 = (bf16[128,1152]{1,0:T(8,128)(2,1)S(1)}, bf16[128,1152]{1,0:T(8,128)(2,1)S(1)}, u32[]{:S(2)}, u32[]{:S(2)}) collective-permute-start(bf16[128,1152]{1,0:T(8,128)(2,1)S(1)} %get-tuple-element.33.refs_1_), channel_id=1, source_target_pairs={{0,4},{1,5},{2,6},{3,7},{4,0},{5,1},{6,2},{7,3},{8,12},{9,13},{10,... | collective-permute-start | bytes 884744 | tf_op jit(solution)/shard_map/ppermute | solution.py:418
  64.4 2.2 %collective-permute-start.13 = (bf16[128,1152]{1,0:T(8,128)(2,1)S(1)}, bf16[128,1152]{1,0:T(8,128)(2,1)S(1)}, u32[]{:S(2)}, u32[]{:S(2)}) collective-permute-start(bf16[128,1152]{1,0:T(8,128)(2,1)S(1)} %get-tuple-element.33.refs_1_), channel_id=1, source_target_pairs={{0,6},{1,7},{2,0},{3,1},{4,2},{5,3},{6,4},{7,5},{8,14},{9,15},{10,... | collective-permute-start | bytes 884744 | tf_op jit(solution)/shard_map/ppermute | solution.py:418
  67.5 4.1 %collective-permute-done.10.refs_4_ = bf16[128,1152]{1,0:T(8,128)(2,1)S(1)} collective-permute-done((bf16[128,1152]{1,0:T(8,128)(2,1)S(1)}, bf16[128,1152]{1,0:T(8,128)(2,1)S(1)}, u32[]{:S(2)}, u32[]{:S(2)}) %collective-permute-start.10) | collective-permute-done | bytes 294944 | tf_op jit(solution)/shard_map/ppermute | solution.py:418
  71.6 3.2 %collective-permute-done.11.refs_5_ = bf16[128,1152]{1,0:T(8,128)(2,1)S(1)} collective-permute-done((bf16[128,1152]{1,0:T(8,128)(2,1)S(1)}, bf16[128,1152]{1,0:T(8,128)(2,1)S(1)}, u32[]{:S(2)}, u32[]{:S(2)}) %collective-permute-start.11) | collective-permute-done | bytes 294944 | tf_op jit(solution)/shard_map/ppermute | solution.py:418
  75.0 3.0 %collective-permute-start.14 = (bf16[1024,1152]{1,0:T(8,128)(2,1)S(1)}, bf16[1024,1152]{1,0:T(8,128)(2,1)}, u32[]{:S(2)}, u32[]{:S(2)}) collective-permute-start(bf16[1024,1152]{1,0:T(8,128)(2,1)S(1)} %shard_map.139.wa_ref), channel_id=1, source_target_pairs={{0,1},{1,0},{2,3},{3,2},{4,5},{5,4},{6,7},{7,6},{8,9},{9,8},{10,11... | collective-permute-start | bytes 7077896 | tf_op jit(solution)/shard_map/ppermute | solution.py:453
  82.1 5.5 %shard_map.133 = bf16[4096,128]{1,0:T(8,128)(2,1)S(1)} custom-call(bf16[4096,128]{1,0:T(8,128)(2,1)} %bitcast.2.x_ref, bf16[1024,512]{1,0:T(8,128)(2,1)S(1)} %copy-done.6, bf16[528,256]{1,0:T(8,128)(2,1)S(1)} %copy-done.12), custom_call_target="tpu_custom_call" | custom-call | tf_op jit(solution)/shard_map/pallas_call | solution.py:421
  88.6 10.2 %all-to-all-start.1 = ((bf16[64,8,8,128]{3,2,1,0:T(8,128)(2,1)}), bf16[64,8,8,128]{3,2,1,0:T(8,128)(2,1)}, u32[]{:S(2)}, u32[]{:S(2)}) async-start(bf16[64,8,8,128]{3,2,1,0:T(8,128)(2,1)} %bitcast.9), calls=%async_computation.1 | async-start | bytes 2097152 | tf_op jit(solution)/shard_map/all_to_all | solution.py:431
  103.5 13.1 %all-to-all-done.1.x_ref = bf16[64,8,8,128]{3,2,1,0:T(8,128)(2,1)} async-done(((bf16[64,8,8,128]{3,2,1,0:T(8,128)(2,1)}), bf16[64,8,8,128]{3,2,1,0:T(8,128)(2,1)}, u32[]{:S(2)}, u32[]{:S(2)}) %all-to-all-start.1) | async-done | bytes 1048608 | tf_op jit(solution)/shard_map/all_to_all | solution.py:431
  116.7 1.6 copy-done.3
  119.3 2.0 %shard_map.136 = (bf16[512,128]{1,0:T(8,128)(2,1)S(1)}, bf16[512,128]{1,0:T(8,128)(2,1)S(1)}, bf16[512,128]{1,0:T(8,128)(2,1)S(1)}, bf16[512,128]{1,0:T(8,128)(2...) custom-call(s32[1]{0:T(128)} %bitcast.me_ref, ...), custom_call_target="tpu_custom_call" | custom-call | tf_op jit(solution)/shard_map/pallas_call | solution.py:441
  121.3 3.4 %collective-permute-start.2 = (bf16[512,128]{1,0:T(8,128)(2,1)S(1)}, bf16[512,128]{1,0:T(8,128)(2,1)S(1)}, u32[]{:S(2)}, u32[]{:S(2)}) collective-permute-start(bf16[512,128]{1,0:T(8,128)(2,1)S(1)} %get-tuple-element.29), channel_id=1, source_target_pairs={{0,64},{64,128},{128,192},{192,0},{1,65},{65,129},{129,193},{193,1... | collective-permute-start | bytes 393224 | tf_op jit(solution)/shard_map/ppermute | solution.py:343
  125.8 3.4 %collective-permute-start.4 = (bf16[512,128]{1,0:T(8,128)(2,1)S(1)}, bf16[512,128]{1,0:T(8,128)(2,1)S(1)}, u32[]{:S(2)}, u32[]{:S(2)}) collective-permute-start(bf16[512,128]{1,0:T(8,128)(2,1)S(1)} %get-tuple-element.31), channel_id=1, source_target_pairs={{0,192},{64,0},{128,64},{192,128},{1,193},{65,1},{129,65},{193,129... | collective-permute-start | bytes 393224 | tf_op jit(solution)/shard_map/ppermute | solution.py:343
  129.1 3.2 %collective-permute-start.19 = (bf16[512,128]{1,0:T(8,128)(2,1)S(1)}, bf16[512,128]{1,0:T(8,128)(2,1)S(1)}, u32[]{:S(2)}, u32[]{:S(2)}) collective-permute-start(bf16[512,128]{1,0:T(8,128)(2,1)S(1)} %get-tuple-element.41), channel_id=1, source_target_pairs={{0,128},{64,192},{128,0},{192,64},{1,129},{65,193},{129,1},{193,65... | collective-permute-start | bytes 393224 | tf_op jit(solution)/shard_map/ppermute | solution.py:343
  133.9 1.9 %collective-permute-done.3.x2 = bf16[512,128]{1,0:T(8,128)(2,1)S(1)} collective-permute-done((bf16[512,128]{1,0:T(8,128)(2,1)S(1)}, bf16[512,128]{1,0:T(8,128)(2,1)S(1)}, u32[]{:S(2)}, u32[]{:S(2)}) %collective-permute-start.3) | collective-permute-done | bytes 131104 | tf_op jit(solution)/shard_map/ppermute | solution.py:343
  135.8 12.0 %collective-permute-done.4.x3 = bf16[512,128]{1,0:T(8,128)(2,1)S(1)} collective-permute-done((bf16[512,128]{1,0:T(8,128)(2,1)S(1)}, bf16[512,128]{1,0:T(8,128)(2,1)S(1)}, u32[]{:S(2)}, u32[]{:S(2)}) %collective-permute-start.4) | collective-permute-done | bytes 131104 | tf_op jit(solution)/shard_map/ppermute | solution.py:343
  147.8 5.3 %shard_map.140 = (bf16[512,128]{1,0:T(8,128)(2,1)S(1)}, bf16[512,128]{1,0:T(8,128)(2,1)S(1)}, bf16[512,128]{1,0:T(8,128)(2,1)S(1)}, bf16[512,128]{1,0:T(8,128)(2,1)S(1)}) custom-call(s32[1]{0:T(128)} %bitcast.me_ref, bf16[512,128]{1,0:T(8,128)(2,1)S(1)} %get-tuple-element.28.x0, bf16[512,128]{1,0:T(8,128)(2,1)S(1)} %collective-permute-done.2.x1, ...), custom_call_target="tpu_custom_call" | custom-call | tf_op jit(solution)/shard_map/pallas_call | solution.py:457
  153.1 3.3 %collective-permute-start.15 = (bf16[512,128]{1,0:T(8,128)(2,1)S(1)}, bf16[512,128]{1,0:T(8,128)(2,1)S(1)}, u32[]{:S(2)}, u32[]{:S(2)}) collective-permute-start(bf16[512,128]{1,0:T(8,128)(2,1)S(1)} %get-tuple-element.36), channel_id=1, source_target_pairs={{0,64},{64,128},{128,192},{192,0},{1,65},{65,129},{129,193},{193,1... | collective-permute-start | bytes 393224 | tf_op jit(solution)/shard_map/ppermute | solution.py:343
  157.7 3.2 %collective-permute-start.17 = (bf16[512,128]{1,0:T(8,128)(2,1)S(1)}, bf16[512,128]{1,0:T(8,128)(2,1)S(1)}, u32[]{:S(2)}, u32[]{:S(2)}) collective-permute-start(bf16[512,128]{1,0:T(8,128)(2,1)S(1)} %get-tuple-element.38), channel_id=1, source_target_pairs={{0,192},{64,0},{128,64},{192,128},{1,193},{65,1},{129,65},{193,129... | collective-permute-start | bytes 393224 | tf_op jit(solution)/shard_map/ppermute | solution.py:343
  160.9 5.3 %shard_map.141 = (bf16[512,128]{1,0:T(8,128)(2,1)S(1)}, bf16[512,128]{1,0:T(8,128)(2,1)S(1)}, bf16[512,128]{1,0:T(8,128)(2,1)S(1)}, bf16[512,128]{1,0:T(8,128)(2,1)S(1)}) custom-call(s32[1]{0:T(128)} %bitcast.me_ref, bf16[512,128]{1,0:T(8,128)(2,1)S(1)} %get-tuple-element.39.x0, bf16[512,128]{1,0:T(8,128)(2,1)S(1)} %collective-permute-done.18.x1, ...), custom_call_target="tpu_custom_call" | custom-call | tf_op jit(solution)/shard_map/pallas_call | solution.py:457
  166.4 3.3 %collective-permute-start.22 = (bf16[512,128]{1,0:T(8,128)(2,1)S(1)}, bf16[512,128]{1,0:T(8,128)(2,1)S(1)}, u32[]{:S(2)}, u32[]{:S(2)}) collective-permute-start(bf16[512,128]{1,0:T(8,128)(2,1)S(1)} %get-tuple-element.45), channel_id=1, source_target_pairs={{0,128},{64,192},{128,0},{192,64},{1,129},{65,193},{129,1},{193,65... | collective-permute-start | bytes 393224 | tf_op jit(solution)/shard_map/ppermute | solution.py:343
  169.6 1.5 collective-permute-start.23
  172.6 7.4 %collective-permute-done.22.refs_6_ = bf16[512,128]{1,0:T(8,128)(2,1)S(1)} collective-permute-done((bf16[512,128]{1,0:T(8,128)(2,1)S(1)}, bf16[512,128]{1,0:T(8,128)(2,1)S(1)}, u32[]{:S(2)}, u32[]{:S(2)}) %collective-permute-start.22) | collective-permute-done | bytes 131104 | tf_op jit(solution)/shard_map/ppermute | solution.py:343
  (88 shorter events, 28.3 us)
Async XLA Ops:
  2.1 5.2 %collective-permute-start = (f32[2,8,512]{2,1,0:T(8,128)S(1)}, f32[2,8,512]{2,1,0:T(8,128)S(1)}, u32[]{:S(2)}, u32[]{:S(2)}) collective-permute-start(f32[2,8,512]{2,1,0:T(8,128)S(1)} %shard_map.127.left_ref), channel_id=1, source_target_pairs={{0,64},{64,0},{128,192},{192,128},{1,65},{65,1},{129,193},{193,129... | collective-permute-start | bytes 98312 | tf_op jit(solution)/shard_map/ppermute | solution.py:375
  7.3 8.0 %collective-permute-start.1 = (f32[2,8,512]{2,1,0:T(8,128)S(1)}, f32[2,8,512]{2,1,0:T(8,128)S(1)}, u32[]{:S(2)}, u32[]{:S(2)}) collective-permute-start(f32[2,8,512]{2,1,0:T(8,128)S(1)} %shard_map.128.left_ref), channel_id=1, source_target_pairs={{0,128},{64,192},{128,0},{192,64},{1,129},{65,193},{129,1},{193,65... | collective-permute-start | bytes 98312 | tf_op jit(solution)/shard_map/ppermute | solution.py:377
  18.1 61.8 %all-to-all-start = ((bf16[64,8,8,128]{3,2,1,0:T(8,128)(2,1)}), bf16[64,8,8,128]{3,2,1,0:T(8,128)(2,1)}, u32[]{:S(2)}, u32[]{:S(2)}) async-start(bf16[64,8,8,128]{3,2,1,0:T(8,128)(2,1)} %shard_map.130), calls=%async_computation | async-start | bytes 2097152 | tf_op jit(solution)/shard_map/all_to_all | solution.py:386
  29.8 21.3 %collective-permute-start.5 = (bf16[64,1152]{1,0:T(8,128)(2,1)S(1)}, bf16[64,1152]{1,0:T(8,128)(2,1)S(1)}, u32[]{:S(2)}, u32[]{:S(2)}) collective-permute-start(bf16[64,1152]{1,0:T(8,128)(2,1)S(1)} %shard_map.137.refs_0_), channel_id=1, source_target_pairs={{0,64},{64,128},{128,192},{192,0},{1,65},{65,129},{129,193},{193,1... | collective-permute-start | bytes 442376 | tf_op jit(solution)/shard_map/ppermute | solution.py:343
  32.1 23.3 %collective-permute-start.6 = (bf16[64,1152]{1,0:T(8,128)(2,1)S(1)}, bf16[64,1152]{1,0:T(8,128)(2,1)S(1)}, u32[]{:S(2)}, u32[]{:S(2)}) collective-permute-start(bf16[64,1152]{1,0:T(8,128)(2,1)S(1)} %shard_map.137.refs_0_), channel_id=1, source_target_pairs={{0,128},{64,192},{128,0},{192,64},{1,129},{65,193},{129,1},{193,65... | collective-permute-start | bytes 442376 | tf_op jit(solution)/shard_map/ppermute | solution.py:343
  36.4 19.0 %collective-permute-start.7 = (bf16[64,1152]{1,0:T(8,128)(2,1)S(1)}, bf16[64,1152]{1,0:T(8,128)(2,1)S(1)}, u32[]{:S(2)}, u32[]{:S(2)}) collective-permute-start(bf16[64,1152]{1,0:T(8,128)(2,1)S(1)} %shard_map.137.refs_0_), channel_id=1, source_target_pairs={{0,192},{64,0},{128,64},{192,128},{1,193},{65,1},{129,65},{193,129... | collective-permute-start | bytes 442376 | tf_op jit(solution)/shard_map/ppermute | solution.py:343
  55.6 8.8 %collective-permute-start.8 = (bf16[128,1152]{1,0:T(8,128)(2,1)S(1)}, bf16[128,1152]{1,0:T(8,128)(2,1)S(1)}, u32[]{:S(2)}, u32[]{:S(2)}) collective-permute-start(bf16[128,1152]{1,0:T(8,128)(2,1)S(1)} %get-tuple-element.32.refs_0_), channel_id=1, source_target_pairs={{0,16},{1,17},{2,18},{3,19},{4,20},{5,21},{6,22},{7,23},{8,24},{9,... | collective-permute-start | bytes 884744 | tf_op jit(solution)/shard_map/ppermute | solution.py:418
  57.0 14.7 %collective-permute-start.10 = (bf16[128,1152]{1,0:T(8,128)(2,1)S(1)}, bf16[128,1152]{1,0:T(8,128)(2,1)S(1)}, u32[]{:S(2)}, u32[]{:S(2)}) collective-permute-start(bf16[128,1152]{1,0:T(8,128)(2,1)S(1)} %get-tuple-element.32.refs_0_), channel_id=1, source_target_pairs={{0,32},{1,33},{2,34},{3,35},{4,36},{5,37},{6,38},{7,39},{8,40},{9,... | collective-permute-start | bytes 884744 | tf_op jit(solution)/shard_map/ppermute | solution.py:418
  59.6 18.4 %copy-start.13 = (bf16[1024,512]{1,0:T(8,128)(2,1)S(1)}, bf16[1024,512]{1,0:T(8,128)(2,1)}, u32[]{:S(2)}) copy-start(bf16[1024,512]{1,0:T(8,128)(2,1)} %constant.58.clone.refs_0_) | copy-start | bytes 3145732
  59.6 19.5 %copy-start.16 = (f32[2,2,64,64]{3,2,1,0:T(8,128)S(1)}, f32[2,2,64,64]{3,2,1,0:T(8,128)}, u32[]{:S(2)}) copy-start(f32[2,2,64,64]{3,2,1,0:T(8,128)} %w1_ref.1) | copy-start | bytes 196612
  59.6 19.5 %copy-start.17 = (f32[2,2,64,64]{3,2,1,0:T(8,128)S(1)}, f32[2,2,64,64]{3,2,1,0:T(8,128)}, u32[]{:S(2)}) copy-start(f32[2,2,64,64]{3,2,1,0:T(8,128)} %w2_ref.1) | copy-start | bytes 196612
  59.6 19.5 %copy-start.19 = (f32[2,2,64]{2,1,0:T(2,128)S(1)}, f32[2,2,64]{2,1,0:T(2,128)}, u32[]{:S(2)}) copy-start(f32[2,2,64]{2,1,0:T(2,128)} %b1_ref.1) | copy-start | bytes 3076
  59.6 19.5 %copy-start.20 = (f32[2,2,64]{2,1,0:T(2,128)S(1)}, f32[2,2,64]{2,1,0:T(2,128)}, u32[]{:S(2)}) copy-start(f32[2,2,64]{2,1,0:T(2,128)} %b2_ref.1) | copy-start | bytes 3076
  59.6 7.9 %collective-permute-start.9 = (bf16[128,1152]{1,0:T(8,128)(2,1)S(1)}, bf16[128,1152]{1,0:T(8,128)(2,1)S(1)}, u32[]{:S(2)}, u32[]{:S(2)}) collective-permute-start(bf16[128,1152]{1,0:T(8,128)(2,1)S(1)} %get-tuple-element.33.refs_1_), channel_id=1, source_target_pairs={{0,2},{1,3},{2,4},{3,5},{4,6},{5,7},{6,0},{7,1},{8,10},{9,11},{10,... | collective-permute-start | bytes 884744 | tf_op jit(solution)/shard_map/ppermute | solution.py:418
  60.9 13.9 %collective-permute-start.11 = (bf16[128,1152]{1,0:T(8,128)(2,1)S(1)}, bf16[128,1152]{1,0:T(8,128)(2,1)S(1)}, u32[]{:S(2)}, u32[]{:S(2)}) collective-permute-start(bf16[128,1152]{1,0:T(8,128)(2,1)S(1)} %get-tuple-element.33.refs_1_), channel_id=1, source_target_pairs={{0,4},{1,5},{2,6},{3,7},{4,0},{5,1},{6,2},{7,3},{8,12},{9,13},{10,... | collective-permute-start | bytes 884744 | tf_op jit(solution)/shard_map/ppermute | solution.py:418
  63.3 11.5 %collective-permute-start.12 = (bf16[128,1152]{1,0:T(8,128)(2,1)S(1)}, bf16[128,1152]{1,0:T(8,128)(2,1)S(1)}, u32[]{:S(2)}, u32[]{:S(2)}) collective-permute-start(bf16[128,1152]{1,0:T(8,128)(2,1)S(1)} %get-tuple-element.32.refs_0_), channel_id=1, source_target_pairs={{0,48},{1,49},{2,50},{3,51},{4,52},{5,53},{6,54},{7,55},{8,56},{9,... | collective-permute-start | bytes 884744 | tf_op jit(solution)/shard_map/ppermute | solution.py:418
  64.4 10.4 %collective-permute-start.13 = (bf16[128,1152]{1,0:T(8,128)(2,1)S(1)}, bf16[128,1152]{1,0:T(8,128)(2,1)S(1)}, u32[]{:S(2)}, u32[]{:S(2)}) collective-permute-start(bf16[128,1152]{1,0:T(8,128)(2,1)S(1)} %get-tuple-element.33.refs_1_), channel_id=1, source_target_pairs={{0,6},{1,7},{2,0},{3,1},{4,2},{5,3},{6,4},{7,5},{8,14},{9,15},{10,... | collective-permute-start | bytes 884744 | tf_op jit(solution)/shard_map/ppermute | solution.py:418
  75.0 54.2 %collective-permute-start.14 = (bf16[1024,1152]{1,0:T(8,128)(2,1)S(1)}, bf16[1024,1152]{1,0:T(8,128)(2,1)}, u32[]{:S(2)}, u32[]{:S(2)}) collective-permute-start(bf16[1024,1152]{1,0:T(8,128)(2,1)S(1)} %shard_map.139.wa_ref), channel_id=1, source_target_pairs={{0,1},{1,0},{2,3},{3,2},{4,5},{5,4},{6,7},{7,6},{8,9},{9,8},{10,11... | collective-permute-start | bytes 7077896 | tf_op jit(solution)/shard_map/ppermute | solution.py:453
  88.6 28.1 %all-to-all-start.1 = ((bf16[64,8,8,128]{3,2,1,0:T(8,128)(2,1)}), bf16[64,8,8,128]{3,2,1,0:T(8,128)(2,1)}, u32[]{:S(2)}, u32[]{:S(2)}) async-start(bf16[64,8,8,128]{3,2,1,0:T(8,128)(2,1)} %bitcast.9), calls=%async_computation.1 | async-start | bytes 2097152 | tf_op jit(solution)/shard_map/all_to_all | solution.py:431
  119.3 28.5 %copy-start.18 = (f32[512]{0:T(512)S(1)}, f32[512]{0:T(512)}, u32[]{:S(2)}) copy-start(f32[512]{0:T(512)} %param.19) | copy-start | bytes 6148
  121.3 11.1 %collective-permute-start.2 = (bf16[512,128]{1,0:T(8,128)(2,1)S(1)}, bf16[512,128]{1,0:T(8,128)(2,1)S(1)}, u32[]{:S(2)}, u32[]{:S(2)}) collective-permute-start(bf16[512,128]{1,0:T(8,128)(2,1)S(1)} %get-tuple-element.29), channel_id=1, source_target_pairs={{0,64},{64,128},{128,192},{192,0},{1,65},{65,129},{129,193},{193,1... | collective-permute-start | bytes 393224 | tf_op jit(solution)/shard_map/ppermute | solution.py:343
  124.6 11.1 %collective-permute-start.3 = (bf16[512,128]{1,0:T(8,128)(2,1)S(1)}, bf16[512,128]{1,0:T(8,128)(2,1)S(1)}, u32[]{:S(2)}, u32[]{:S(2)}) collective-permute-start(bf16[512,128]{1,0:T(8,128)(2,1)S(1)} %get-tuple-element.30), channel_id=1, source_target_pairs={{0,128},{64,192},{128,0},{192,64},{1,129},{65,193},{129,1},{193,65... | collective-permute-start | bytes 393224 | tf_op jit(solution)/shard_map/ppermute | solution.py:343
  125.8 22.0 %collective-permute-start.4 = (bf16[512,128]{1,0:T(8,128)(2,1)S(1)}, bf16[512,128]{1,0:T(8,128)(2,1)S(1)}, u32[]{:S(2)}, u32[]{:S(2)}) collective-permute-start(bf16[512,128]{1,0:T(8,128)(2,1)S(1)} %get-tuple-element.31), channel_id=1, source_target_pairs={{0,192},{64,0},{128,64},{192,128},{1,193},{65,1},{129,65},{193,129... | collective-permute-start | bytes 393224 | tf_op jit(solution)/shard_map/ppermute | solution.py:343
  129.1 28.5 %collective-permute-start.18 = (bf16[512,128]{1,0:T(8,128)(2,1)S(1)}, bf16[512,128]{1,0:T(8,128)(2,1)S(1)}, u32[]{:S(2)}, u32[]{:S(2)}) collective-permute-start(bf16[512,128]{1,0:T(8,128)(2,1)S(1)} %get-tuple-element.40), channel_id=1, source_target_pairs={{0,64},{64,128},{128,192},{192,0},{1,65},{65,129},{129,193},{193,1... | collective-permute-start | bytes 393224 | tf_op jit(solution)/shard_map/ppermute | solution.py:343
  129.1 31.8 %collective-permute-start.19 = (bf16[512,128]{1,0:T(8,128)(2,1)S(1)}, bf16[512,128]{1,0:T(8,128)(2,1)S(1)}, u32[]{:S(2)}, u32[]{:S(2)}) collective-permute-start(bf16[512,128]{1,0:T(8,128)(2,1)S(1)} %get-tuple-element.41), channel_id=1, source_target_pairs={{0,128},{64,192},{128,0},{192,64},{1,129},{65,193},{129,1},{193,65... | collective-permute-start | bytes 393224 | tf_op jit(solution)/shard_map/ppermute | solution.py:343
  132.4 28.5 %collective-permute-start.20 = (bf16[512,128]{1,0:T(8,128)(2,1)S(1)}, bf16[512,128]{1,0:T(8,128)(2,1)S(1)}, u32[]{:S(2)}, u32[]{:S(2)}) collective-permute-start(bf16[512,128]{1,0:T(8,128)(2,1)S(1)} %get-tuple-element.42), channel_id=1, source_target_pairs={{0,192},{64,0},{128,64},{192,128},{1,193},{65,1},{129,65},{193,129... | collective-permute-start | bytes 393224 | tf_op jit(solution)/shard_map/ppermute | solution.py:343
  153.1 16.5 %collective-permute-start.15 = (bf16[512,128]{1,0:T(8,128)(2,1)S(1)}, bf16[512,128]{1,0:T(8,128)(2,1)S(1)}, u32[]{:S(2)}, u32[]{:S(2)}) collective-permute-start(bf16[512,128]{1,0:T(8,128)(2,1)S(1)} %get-tuple-element.36), channel_id=1, source_target_pairs={{0,64},{64,128},{128,192},{192,0},{1,65},{65,129},{129,193},{193,1... | collective-permute-start | bytes 393224 | tf_op jit(solution)/shard_map/ppermute | solution.py:343
  156.5 14.7 %collective-permute-start.16 = (bf16[512,128]{1,0:T(8,128)(2,1)S(1)}, bf16[512,128]{1,0:T(8,128)(2,1)S(1)}, u32[]{:S(2)}, u32[]{:S(2)}) collective-permute-start(bf16[512,128]{1,0:T(8,128)(2,1)S(1)} %get-tuple-element.37), channel_id=1, source_target_pairs={{0,128},{64,192},{128,0},{192,64},{1,129},{65,193},{129,1},{193,65... | collective-permute-start | bytes 393224 | tf_op jit(solution)/shard_map/ppermute | solution.py:343
  157.7 14.9 %collective-permute-start.17 = (bf16[512,128]{1,0:T(8,128)(2,1)S(1)}, bf16[512,128]{1,0:T(8,128)(2,1)S(1)}, u32[]{:S(2)}, u32[]{:S(2)}) collective-permute-start(bf16[512,128]{1,0:T(8,128)(2,1)S(1)} %get-tuple-element.38), channel_id=1, source_target_pairs={{0,192},{64,0},{128,64},{192,128},{1,193},{65,1},{129,65},{193,129... | collective-permute-start | bytes 393224 | tf_op jit(solution)/shard_map/ppermute | solution.py:343
  166.3 6.3 %collective-permute-start.21 = (bf16[512,128]{1,0:T(8,128)(2,1)S(1)}, bf16[512,128]{1,0:T(8,128)(2,1)S(1)}, u32[]{:S(2)}, u32[]{:S(2)}) collective-permute-start(bf16[512,128]{1,0:T(8,128)(2,1)S(1)} %get-tuple-element.44), channel_id=1, source_target_pairs={{0,64},{64,128},{128,192},{192,0},{1,65},{65,129},{129,193},{193,1... | collective-permute-start | bytes 393224 | tf_op jit(solution)/shard_map/ppermute | solution.py:343
  166.4 13.6 %collective-permute-start.22 = (bf16[512,128]{1,0:T(8,128)(2,1)S(1)}, bf16[512,128]{1,0:T(8,128)(2,1)S(1)}, u32[]{:S(2)}, u32[]{:S(2)}) collective-permute-start(bf16[512,128]{1,0:T(8,128)(2,1)S(1)} %get-tuple-element.45), channel_id=1, source_target_pairs={{0,128},{64,192},{128,0},{192,64},{1,129},{65,193},{129,1},{193,65... | collective-permute-start | bytes 393224 | tf_op jit(solution)/shard_map/ppermute | solution.py:343
  169.6 10.3 %collective-permute-start.23 = (bf16[512,128]{1,0:T(8,128)(2,1)S(1)}, bf16[512,128]{1,0:T(8,128)(2,1)S(1)}, u32[]{:S(2)}, u32[]{:S(2)}) collective-permute-start(bf16[512,128]{1,0:T(8,128)(2,1)S(1)} %get-tuple-element.46), channel_id=1, source_target_pairs={{0,192},{64,0},{128,64},{192,128},{1,193},{65,1},{129,65},{193,129... | collective-permute-start | bytes 393224 | tf_op jit(solution)/shard_map/ppermute | solution.py:343
  (19 other events, 94.3 us)

commit v4 on v3

--- a/solution.py
+++ b/solution.py
@@ -15,17 +15,10 @@
 f32 = jnp.float32
 
 
-def tables(rows, width, per_owner):
-    owners = width // 2 // per_owner
-    place = np.arange(width)
-    freq = np.arange(width // 2).reshape(owners, 1, per_owner)
-    freq = np.broadcast_to(freq, (owners, 2, per_owner)).reshape(-1)
-    part = np.broadcast_to(np.arange(2).reshape(1, 2, 1), (owners, 2, per_owner)).reshape(-1)
-    angle = 2.0 * np.pi / width * ((freq[:, None] * place[None, :]) % width)
-    forward = np.where(part[:, None] == 0, np.cos(angle), -np.sin(angle))
-    grid = np.arange(rows)
-    turn = 2.0 * np.pi / rows * ((grid[:, None] * grid[None, :]) % rows)
-    return forward, np.cos(turn), np.sin(turn)
+def circle_table(size):
+    grid = np.arange(size)
+    turn = 2.0 * np.pi / size * ((grid[:, None] * grid[None, :]) % size)
+    return np.concatenate([np.cos(turn[: size // 2]), np.sin(turn[: size // 2])], axis=0)
 
 
 def mm(left, right):
@@ -54,10 +47,37 @@
     o_ref[...] = left_ref[...] + right_ref[...]
 
 
-def warm_kernel(*refs):
-    count = len(refs) // 2
-    for source, target in zip(refs[:count], refs[count:]):
-        target[...] = source[...]
+def table_kernel(per_owner, turn_ref, gain_ref, o_ref, g_ref, half_ref, full_ref):
+    g_ref[...] = gain_ref[...]
+    size, lanes = half_ref.shape
+    owners = size // per_owner
+    for lane in range(0, o_ref.shape[1], lanes):
+        for part in range(2):
+            start = part * (turn_ref.shape[0] // 2)
+            half_ref[...] = turn_ref[start : start + size, lane : lane + lanes].astype(f32) * (1.0 - 2.0 * part)
+            for place in range(per_owner):
+                full_ref[pl.ds(part * per_owner + place, owners, stride=2 * per_owner), :] = half_ref[
+                    pl.ds(place, owners, stride=per_owner), :
+                ]
+        o_ref[:, lane : lane + lanes] = full_ref[...].astype(bf16)
+
+
+def turn_kernel(half_ref, w1_ref, b1_ref, w2_ref, b2_ref, o_ref):
+    size, width = half_ref.shape[0] // 2, half_ref.shape[1]
+    column = lax.broadcasted_iota(jnp.int32, (size, width), 1)
+    sign = jnp.where(column % 2 == 0, 1.0, -1.0)
+    for part in range(2):
+        top = half_ref[part * size : (part + 1) * size, :]
+        o_ref[2 * part * size : (2 * part + 1) * size, :] = top
+        o_ref[(2 * part + 1) * size : (2 * part + 2) * size, :] = (top.astype(f32) * sign).astype(bf16)
+    start, wide = 4 * size, o_ref.shape[1] // 2
+    for place, (w_ref, b_ref) in enumerate(((w1_ref, b1_ref), (w2_ref, b2_ref))):
+        cut = slice(place * wide, (place + 1) * wide)
+        o_ref[start : start + wide, cut] = complex_matrix(w_ref)
+        bias = bias_row(b_ref)
+        high = bias.astype(bf16).astype(f32)
+        rows = jnp.concatenate([high, bias - high, jnp.zeros((14, wide), f32)], axis=0)
+        o_ref[start + wide :, cut] = rows.astype(bf16)
 
 
 def moments(left_ref, right_ref, channels):
@@ -87,20 +107,21 @@
             )
 
 
-def residual_kernel(channels, x_ref, left_ref, right_ref, gain_ref, o_ref):
-    rows = x_ref.shape[0]
-    flipped = moments(left_ref, right_ref, channels)
-    for row in range(rows):
-        source = x_ref[row].astype(f32)
-        o_ref[row] = normed_row(source, flipped, row, rows, gain_ref[...]) + source
-
-
-def flip_kernel(per_owner, lanes, table_ref, i_ref):
+def flip_kernel(per_owner, lanes, channels, table_ref, left_ref, right_ref, i_ref):
     for start in range(0, table_ref.shape[0], lanes):
         place = lax.broadcasted_iota(jnp.int32, (lanes, 1), 0) + start
         weight = jnp.where((place == 0) | (place == per_owner), 1.0, 2.0)
         part = table_ref[start : start + lanes, :].astype(f32) * weight
         i_ref[:, start : start + lanes] = jnp.transpose(part).astype(bf16)
+    rest = moments(left_ref, right_ref, channels)
+    pieces = []
+    for _ in range(3):
+        piece = rest.astype(bf16).astype(f32)
+        pieces.append(piece)
+        rest = rest - piece
+    width, count = rest.shape
+    pieces.append(jnp.zeros((width, lanes - 3 * count), f32))
+    i_ref[:, table_ref.shape[0] :] = jnp.concatenate(pieces, axis=1).astype(bf16)
 
 
 def soften(values):
@@ -136,11 +157,12 @@
 
 
 def column_kernel(
-    scale, x_ref, table_ref, w_ref, o_ref, wide_ref, real_ref, imag_ref
+    scale, x_ref, table_ref, o_ref, wide_ref, real_ref, imag_ref
 ):
-    size = w_ref.shape[1]
-    tail = w_ref[2 * size :, :].astype(f32)
-    bias_one, bias_two = tail[0:1] + tail[1:2], tail[2:3] + tail[3:4]
+    size = 2 * x_ref.shape[1]
+    start = 2 * table_ref.shape[1]
+    tail = table_ref[start + size :, :].astype(f32)
+    bias = tail[0:1] + tail[1:2]
     height = table_ref.shape[1]
     lanes = x_ref.shape[1]
     step = x_ref.shape[0] // height
@@ -152,9 +174,9 @@
                 pl.ds(part * count + k, height, stride=step), :
             ].astype(bf16)
 
-    for half in range(count // 2):
-        span = pl.ds(half * 2 * lanes, 2 * lanes)
-        cos, sin = table_ref[0:height, :], table_ref[height:, :]
+    def body(half, carry):
+        span = pl.ds(pl.multiple_of(half * 2 * lanes, 2 * lanes), 2 * lanes)
+        cos, sin = table_ref[0:height, :], table_ref[height : 2 * height, :]
         real, imag = real_ref[:, span], imag_ref[:, span]
         out_real = (mm(cos, real) + mm(sin, imag)) * scale
         out_imag = (mm(cos, imag) - mm(sin, real)) * scale
@@ -162,8 +184,8 @@
         for side in range(2):
             cut = slice(side * lanes, (side + 1) * lanes)
             both = jnp.concatenate([out_real[:, cut].astype(bf16), out_imag[:, cut].astype(bf16)], axis=1)
-            first = jnp.maximum(mm(both, w_ref[0:size, :]) + bias_one, 0.0).astype(bf16)
-            second = soften(mm(first, w_ref[size : 2 * size, :]) + bias_two).astype(bf16)
+            first = jnp.maximum(mm(both, table_ref[start : start + size, 0:size]) + bias[:, 0:size], 0.0).astype(bf16)
+            second = soften(mm(first, table_ref[start : start + size, size:]) + bias[:, size:]).astype(bf16)
             next_real.append(second[:, :lanes])
             next_imag.append(second[:, lanes:])
         real, imag = jnp.concatenate(next_real, axis=1), jnp.concatenate(next_imag, axis=1)
@@ -174,21 +196,33 @@
             k = half * 2 + side
             wide_ref[pl.ds(k, height, stride=step), :] = back_real[:, cut]
             wide_ref[pl.ds(count + k, height, stride=step), :] = back_imag[:, cut]
+        return carry
+
+    lax.fori_loop(0, count // 2, body, 0)
     o_ref[...] = wide_ref[...].astype(bf16)
 
 
-def inverse_kernel(scale, me_ref, x_ref, table_ref, r_ref, *o_refs):
+def inverse_kernel(scale, me_ref, x_ref, table_ref, t_ref, gain_ref, *o_refs):
     ways = len(o_refs) // 2
-    _, _, lanes = r_ref.shape
+    rows, width, lanes = t_ref.shape
+    count = 2 * rows
+    tail = table_ref[:, width:].astype(f32)
+    flipped = (tail[:, 0:count] + tail[:, count : 2 * count]) + tail[:, 2 * count : 3 * count]
+    column = lax.broadcasted_iota(jnp.int32, flipped.shape, 1)
     for shift in range(ways):
         owner = lax.rem(me_ref[0] + shift, ways)
         sides = [
             x_ref[:, 2 * owner + side].astype(f32).reshape(-1, lanes).astype(bf16) for side in range(2)
         ]
-        out = mm(table_ref[...], jnp.concatenate(sides, axis=1)) * scale
+        out = mm(table_ref[:, 0:width], jnp.concatenate(sides, axis=1)) * scale
         for side in range(2):
+            row = 2 * owner + side
+            source = t_ref[row].astype(f32)
+            center = jnp.sum(jnp.where(column == row, flipped, 0.0), axis=1, keepdims=True)
+            factor = jnp.sum(jnp.where(column == row + rows, flipped, 0.0), axis=1, keepdims=True)
+            normed = (source - center) * factor * gain_ref[...]
             o_refs[side * ways + shift][...] = (
-                out[:, side * lanes : (side + 1) * lanes] + r_ref[2 * owner + side]
+                (out[:, side * lanes : (side + 1) * lanes] + normed) + source
             ).astype(bf16)
 
 
@@ -203,21 +237,26 @@
 
 
 def mlp_kernel(
-    tile, me_ref, x0, x1, x2, x3, wa_ref, wb_ref, gain_ref, bias_ref, y0, y1, y2, y3, x_ref, y_ref
+    tile, me_ref, x0, x1, x2, x3, wa_ref, wb_ref, gain_ref, bias_ref, y0, y1, y2, y3, x_ref, y_ref, w_ref, sems
 ):
     ways, tokens, lanes = x_ref.shape
     channels = ways * lanes
     me = me_ref[0]
+    count, hidden_block = w_ref.shape[0], w_ref.shape[1]
+    per_side = wa_ref.shape[0] // hidden_block
+    fetches = [
+        pltpu.make_async_copy(
+            (wa_ref, wb_ref)[block // per_side].at[pl.ds(block % per_side * hidden_block, hidden_block)],
+            w_ref.at[block],
+            sems.at[block],
+        )
+        for block in range(count)
+    ]
+    for fetch in fetches:
+        fetch.start()
     for shift, ref in enumerate((x0, x1, x2, x3)):
         x_ref[lax.rem(me + ways - shift, ways)] = ref[...]
     unit = eye(8, lanes).astype(bf16)
-    hidden_block = 512
-    blocks = [
-        (ref, pl.ds(start, hidden_block))
-        for ref in (wa_ref, wb_ref)
-        for start in range(0, ref.shape[0], hidden_block)
-    ]
-    biases = [mm_t(unit, ref[span, 2 * channels :])[0:1] for ref, span in blocks]
 
     def body(index, carry):
         span = pl.ds(pl.multiple_of(index * tile, tile), tile)
@@ -235,9 +274,11 @@
             axis=1,
         )
         acc = None
-        for (ref, rows), bias in zip(blocks, biases):
-            hidden = gelu(mm_t(normed, ref[rows, :channels]) + bias).astype(bf16)
-            product = mm(hidden, ref[rows, channels : 2 * channels])
+        for block in range(count):
+            pl.when(index == 0)(fetches[block].wait)
+            bias = mm_t(unit, w_ref[block, :, 2 * channels :])[0:1]
+            hidden = gelu(mm_t(normed, w_ref[block, :, :channels]) + bias).astype(bf16)
+            product = mm(hidden, w_ref[block, :, channels : 2 * channels])
             acc = product if acc is None else acc + product
         for b in range(ways):
             cut = slice(b * lanes, (b + 1) * lanes)
@@ -281,19 +322,6 @@
         o_ref[target, 2 * channels :] = values.astype(bf16)
 
 
-def prep_kernel(w1_ref, b1_ref, w2_ref, b2_ref, o_ref):
-    size = o_ref.shape[1]
-    o_ref[0:size, :] = complex_matrix(w1_ref)
-    o_ref[size : 2 * size, :] = complex_matrix(w2_ref)
-    rows = []
-    for ref in (b1_ref, b2_ref):
-        bias = bias_row(ref)
-        high = bias.astype(bf16).astype(f32)
-        rows += [high, bias - high]
-    rows.append(jnp.zeros((12, size), f32))
-    o_ref[2 * size :, :] = jnp.concatenate(rows, axis=0).astype(bf16)
-
-
 def split_kernel(me_ref, *refs):
     *parts, first_ref, second_ref, bias_ref = refs
     ways = len(parts)
@@ -365,9 +393,7 @@
     channels = lanes * ways
     per_owner = width // 2 // owners
     me = lax.axis_index("chan").astype(jnp.int32).reshape(1)
-    forward, cos, sin = tables(height, width, per_owner)
-    forward = jnp.asarray(forward, bf16)
-    turns = jnp.asarray(np.concatenate([cos, sin], axis=0), bf16)
+    turns = jnp.asarray(circle_table(height), bf16)
     half_scale = 2.0 ** math.floor(math.log2(math.sqrt(width)))
     first_scale, second_scale = 1.0 / half_scale, half_scale / math.sqrt(width * height)
 
@@ -376,8 +402,11 @@
     left = call(add_kernel, shape(stats.shape, f32), vmem(2))(stats, other)
     right = lax.ppermute(left, "chan", [(i, i ^ 2) for i in range(ways)])
     table, gain = call(
-        warm_kernel, [shape(forward.shape, bf16), shape((1, lanes), f32)], vmem(2)
-    )(forward, gain_in.reshape(1, lanes))
+        partial(table_kernel, per_owner),
+        [shape((width, width), bf16), shape((1, lanes), f32)],
+        vmem(2),
+        scratch=[pltpu.VMEM((width // 2, lanes), f32), pltpu.VMEM((width, lanes), f32)],
+    )(turns, gain_in.reshape(1, lanes))
     spectra = call(
         partial(forward_kernel, channels, first_scale),
         shape((owners, rows, 2 * per_owner, lanes), bf16),
@@ -396,11 +425,9 @@
         [smem] + vmem(4),
         scratch=[pltpu.VMEM((lanes, channels + lanes), f32)],
     )(piece, fc1_weight, fc1_bias.reshape(1, -1), fc2_weight, fc2_bias.reshape(1, lanes))
-    wide = 2 * lanes
-    spectral = call(prep_kernel, shape((2 * wide + 16, wide), bf16), vmem(4))(
-        spectral_w1, spectral_b1, spectral_w2, spectral_b2
-    )
-    circle = call(warm_kernel, [shape(turns.shape, bf16)], vmem(1))(turns)[0]
+    circle = call(turn_kernel, shape((2 * height + 2 * lanes + 16, height), bf16), vmem(5))(
+        turns, spectral_w1, spectral_b1, spectral_w2, spectral_b2
+    )
     stage = [mine] + shifts(lambda s: mine, "chan", ways)
     count = ways * units // 2
     *sides, out_bias = call(
@@ -421,35 +448,28 @@
     back = call(
         partial(column_kernel, second_scale),
         shape((total, lanes), bf16),
-        vmem(3),
+        vmem(2),
         scratch=[
             pltpu.VMEM((total, lanes), f32),
             pltpu.VMEM((height, per_owner * lanes), bf16),
             pltpu.VMEM((height, per_owner * lanes), bf16),
         ],
-    )(columns.reshape(total, lanes), circle, spectral)
+    )(columns.reshape(total, lanes), circle)
     returned = lax.all_to_all(
         back.reshape(owners, rows, 2 * per_owner, lanes), "rows", split_axis=0, concat_axis=0
     )
-    resid = call(
-        partial(residual_kernel, channels),
-        shape((rows, width, lanes), f32),
-        vmem(4),
-    )(tokens, left, right, gain_in.reshape(1, lanes))
-    inverse = call(partial(flip_kernel, per_owner, lanes), shape((width, width), bf16), vmem(1))(forward)
+    inverse = call(
+        partial(flip_kernel, per_owner, lanes, channels), shape((width, width + lanes), bf16), vmem(3)
+    )(table, left, right)
     share = rows // ways * width // 2
     mixed = call(
         partial(inverse_kernel, first_scale),
         [shape((share, lanes), bf16)] * (2 * ways),
-        [smem] + vmem(3),
-    )(me, returned, inverse, resid)
+        [smem] + vmem(4),
+    )(me, returned, inverse, tokens, gain_in.reshape(1, lanes))
     halves = [mixed[:ways], mixed[ways:]]
     whole_a = [halves[0][0]] + shifts(lambda s: halves[0][s], "chan", ways)
-    near = call(
-        join_kernel,
-        shape((2 * ring_x * parts[0].shape[0], parts[0].shape[1]), bf16),
-        vmem(len(parts)),
-    )(*parts)
+    near = call(join_kernel, shape((2 * ring_x * parts[0].shape[0], parts[0].shape[1]), bf16), vmem(len(parts)))(*parts)
     far = lax.ppermute(near, "rows", [(i, i ^ 1) for i in range(owners)])
     whole_b = [halves[1][0]] + shifts(lambda s: halves[1][s], "chan", ways)
 
@@ -457,10 +477,12 @@
         return call(
             partial(mlp_kernel, 256),
             [shape((share, lanes), bf16)] * ways,
-            [smem] + vmem(8),
+            [smem] + vmem(4) + [pl.BlockSpec(memory_space=pl.ANY)] * 2 + vmem(2),
             scratch=[
                 pltpu.VMEM((ways, share, lanes), bf16),
                 pltpu.VMEM((ways, share, lanes), bf16),
+                pltpu.VMEM((4, near.shape[0] // 2, near.shape[1]), bf16),
+                pltpu.SemaphoreType.DMA((4,)),
             ],
         )(me, *whole, near, far, gain_out.reshape(1, channels), out_bias)
 

time: 182 us -> 181 us (level)
  local copies, waits for them, and re-layouts: 13.6 us -> 10.1 us
  waiting for transfers between devices: 62 us -> 64.4 us
    unnamed x50 -> x44, local copies, waits for them, and re-layouts: 13.6 us -> 10.1 us
    all_to_all x1, waiting for transfers between devices: 13.1 us -> 15.5 us  [local(): lax.all_to_all(back.reshape(owners, rows, 2 * per_owner, lanes), 'rows',...]
where the time goes in v4:
time: 181 us
  starting transfers between devices  78.9 us (44%)
  waiting for transfers between devices  64.4 us (36%)
  Pallas kernels  26.9 us (15%)
  local copies, waits for them, and re-layouts  10.1 us (6%)
    ppermute x15, waiting for transfers between devices, shifts(): lax.ppermute(value_of(shift), axis, [(i, (i + shift) % ways) for i in ran...  39.3 us
    ppermute x15, starting transfers between devices, shifts(): lax.ppermute(value_of(shift), axis, [(i, (i + shift) % ways) for i in ran...  34.2 us
    all_to_all x1, waiting for transfers between devices, local(): lax.all_to_all(back.reshape(owners, rows, 2 * per_owner, lanes), 'rows',...  15.5 us
    ppermute x6, starting transfers between devices, local(): parts.append(lax.ppermute(sides[half], 'rows', ring[half]))  10.9 us
    pallas_call x2, Pallas kernels, mlp(): call(partial(mlp_kernel, 256), [shape((share, lanes), bf16)] * ways, [sme...  10.8 us
    all_to_all x1, starting transfers between devices, local(): columns = lax.all_to_all(spectra, 'rows', split_axis=0, concat_axis=0)  10.4 us
    all_to_all x1, starting transfers between devices, local(): lax.all_to_all(back.reshape(owners, rows, 2 * per_owner, lanes), 'rows',...  10.2 us
    unnamed x44, local copies, waits for them, and re-layouts  10.1 us
  transfers between devices with their start and end apart: 26, of which 11 were waited for; matrix products, arithmetic and copies ran while one was open for 0% of the time, Pallas kernels for 12%

profile of v4, /device:TPU:1, one launch (start us, length us, event | category | flops | bytes accessed | tf_op | source)
XLA Modules:
  0.0 180.6 jit_solution(10897501557436566782)
XLA Ops:
  2.1 3.8 %collective-permute-start = (f32[2,8,512]{2,1,0:T(8,128)S(1)}, f32[2,8,512]{2,1,0:T(8,128)S(1)}, u32[]{:S(2)}, u32[]{:S(2)}) collective-permute-start(f32[2,8,512]{2,1,0:T(8,128)S(1)} %shard_map.118.left_ref), channel_id=1, source_target_pairs={{0,64},{64,0},{128,192},{192,128},{1,65},{65,1},{129,193},{193,129... | collective-permute-start | bytes 98312 | tf_op jit(solution)/shard_map/ppermute | solution.py:401
  7.3 6.3 %collective-permute-start.1 = (f32[2,8,512]{2,1,0:T(8,128)S(1)}, f32[2,8,512]{2,1,0:T(8,128)S(1)}, u32[]{:S(2)}, u32[]{:S(2)}) collective-permute-start(f32[2,8,512]{2,1,0:T(8,128)S(1)} %shard_map.119.left_ref), channel_id=1, source_target_pairs={{0,128},{64,192},{128,0},{192,64},{1,129},{65,193},{129,1},{193,65... | collective-permute-start | bytes 98312 | tf_op jit(solution)/shard_map/ppermute | solution.py:403
  15.7 2.7 %shard_map.121 = bf16[64,8,8,128]{3,2,1,0:T(8,128)(2,1)} custom-call(bf16[8,512,128]{2,1,0:T(8,128)(2,1)S(1)} %copy-done.1, f32[2,8,512]{2,1,0:T(8,128)S(1)} %shard_map.119.left_ref, f32[2,8,512]{2,1,0:T(8,128)S(1)} %collective-permute-done.1.right_ref, f32[1,128]{1,0:T(1,128)S(1)} %get-tuple-element.26.gain_ref, ...), custom_call_target="tpu_custom_call" | custom-call | tf_op jit(solution)/shard_map/pallas_call | solution.py:410
  19.2 10.4 %all-to-all-start = ((bf16[64,8,8,128]{3,2,1,0:T(8,128)(2,1)}), bf16[64,8,8,128]{3,2,1,0:T(8,128)(2,1)}, u32[]{:S(2)}, u32[]{:S(2)}) async-start(bf16[64,8,8,128]{3,2,1,0:T(8,128)(2,1)} %shard_map.121), calls=%async_computation | async-start | bytes 2097152 | tf_op jit(solution)/shard_map/all_to_all | solution.py:415
  30.6 2.3 %collective-permute-start.5 = (bf16[64,1152]{1,0:T(8,128)(2,1)S(1)}, bf16[64,1152]{1,0:T(8,128)(2,1)S(1)}, u32[]{:S(2)}, u32[]{:S(2)}) collective-permute-start(bf16[64,1152]{1,0:T(8,128)(2,1)S(1)} %shard_map.126.refs_0_), channel_id=1, source_target_pairs={{0,64},{64,128},{128,192},{192,0},{1,65},{65,129},{129,193},{193,1... | collective-permute-start | bytes 442376 | tf_op jit(solution)/shard_map/ppermute | solution.py:371
  32.9 4.2 %collective-permute-start.6 = (bf16[64,1152]{1,0:T(8,128)(2,1)S(1)}, bf16[64,1152]{1,0:T(8,128)(2,1)S(1)}, u32[]{:S(2)}, u32[]{:S(2)}) collective-permute-start(bf16[64,1152]{1,0:T(8,128)(2,1)S(1)} %shard_map.126.refs_0_), channel_id=1, source_target_pairs={{0,128},{64,192},{128,0},{192,64},{1,129},{65,193},{129,1},{193,65... | collective-permute-start | bytes 442376 | tf_op jit(solution)/shard_map/ppermute | solution.py:371
  37.2 2.4 %collective-permute-start.7 = (bf16[64,1152]{1,0:T(8,128)(2,1)S(1)}, bf16[64,1152]{1,0:T(8,128)(2,1)S(1)}, u32[]{:S(2)}, u32[]{:S(2)}) collective-permute-start(bf16[64,1152]{1,0:T(8,128)(2,1)S(1)} %shard_map.126.refs_0_), channel_id=1, source_target_pairs={{0,192},{64,0},{128,64},{192,128},{1,193},{65,1},{129,65},{193,129... | collective-permute-start | bytes 442376 | tf_op jit(solution)/shard_map/ppermute | solution.py:371
  39.5 12.4 %collective-permute-done.5.refs_1_ = bf16[64,1152]{1,0:T(8,128)(2,1)S(1)} collective-permute-done((bf16[64,1152]{1,0:T(8,128)(2,1)S(1)}, bf16[64,1152]{1,0:T(8,128)(2,1)S(1)}, u32[]{:S(2)}, u32[]{:S(2)}) %collective-permute-start.5) | collective-permute-done | bytes 147488 | tf_op jit(solution)/shard_map/ppermute | solution.py:371
  51.9 4.3 %collective-permute-done.6.refs_2_ = bf16[64,1152]{1,0:T(8,128)(2,1)S(1)} collective-permute-done((bf16[64,1152]{1,0:T(8,128)(2,1)S(1)}, bf16[64,1152]{1,0:T(8,128)(2,1)S(1)}, u32[]{:S(2)}, u32[]{:S(2)}) %collective-permute-start.6) | collective-permute-done | bytes 147488 | tf_op jit(solution)/shard_map/ppermute | solution.py:371
  57.8 2.6 %collective-permute-start.10 = (bf16[128,1152]{1,0:T(8,128)(2,1)S(1)}, bf16[128,1152]{1,0:T(8,128)(2,1)S(1)}, u32[]{:S(2)}, u32[]{:S(2)}) collective-permute-start(bf16[128,1152]{1,0:T(8,128)(2,1)S(1)} %get-tuple-element.32.refs_0_), channel_id=1, source_target_pairs={{0,32},{1,33},{2,34},{3,35},{4,36},{5,37},{6,38},{7,39},{8,40},{9,... | collective-permute-start | bytes 884744 | tf_op jit(solution)/shard_map/ppermute | solution.py:445
  61.7 2.4 %collective-permute-start.11 = (bf16[128,1152]{1,0:T(8,128)(2,1)S(1)}, bf16[128,1152]{1,0:T(8,128)(2,1)S(1)}, u32[]{:S(2)}, u32[]{:S(2)}) collective-permute-start(bf16[128,1152]{1,0:T(8,128)(2,1)S(1)} %get-tuple-element.33.refs_1_), channel_id=1, source_target_pairs={{0,4},{1,5},{2,6},{3,7},{4,0},{5,1},{6,2},{7,3},{8,12},{9,13},{10,... | collective-permute-start | bytes 884744 | tf_op jit(solution)/shard_map/ppermute | solution.py:445
  65.2 2.2 %collective-permute-start.13 = (bf16[128,1152]{1,0:T(8,128)(2,1)S(1)}, bf16[128,1152]{1,0:T(8,128)(2,1)S(1)}, u32[]{:S(2)}, u32[]{:S(2)}) collective-permute-start(bf16[128,1152]{1,0:T(8,128)(2,1)S(1)} %get-tuple-element.33.refs_1_), channel_id=1, source_target_pairs={{0,6},{1,7},{2,0},{3,1},{4,2},{5,3},{6,4},{7,5},{8,14},{9,15},{10,... | collective-permute-start | bytes 884744 | tf_op jit(solution)/shard_map/ppermute | solution.py:445
  68.3 4.1 %collective-permute-done.10.refs_4_ = bf16[128,1152]{1,0:T(8,128)(2,1)S(1)} collective-permute-done((bf16[128,1152]{1,0:T(8,128)(2,1)S(1)}, bf16[128,1152]{1,0:T(8,128)(2,1)S(1)}, u32[]{:S(2)}, u32[]{:S(2)}) %collective-permute-start.10) | collective-permute-done | bytes 294944 | tf_op jit(solution)/shard_map/ppermute | solution.py:445
  72.4 3.2 %collective-permute-done.11.refs_5_ = bf16[128,1152]{1,0:T(8,128)(2,1)S(1)} collective-permute-done((bf16[128,1152]{1,0:T(8,128)(2,1)S(1)}, bf16[128,1152]{1,0:T(8,128)(2,1)S(1)}, u32[]{:S(2)}, u32[]{:S(2)}) %collective-permute-start.11) | collective-permute-done | bytes 294944 | tf_op jit(solution)/shard_map/ppermute | solution.py:445
  75.8 3.0 %collective-permute-start.14 = (bf16[1024,1152]{1,0:T(8,128)(2,1)S(1)}, bf16[1024,1152]{1,0:T(8,128)(2,1)}, u32[]{:S(2)}, u32[]{:S(2)}) collective-permute-start(bf16[1024,1152]{1,0:T(8,128)(2,1)S(1)} %shard_map.128.wa_ref), channel_id=1, source_target_pairs={{0,1},{1,0},{2,3},{3,2},{4,5},{5,4},{6,7},{7,6},{8,9},{9,8},{10,11... | collective-permute-start | bytes 7077896 | tf_op jit(solution)/shard_map/ppermute | solution.py:473
  81.5 6.5 %shard_map.123 = bf16[4096,128]{1,0:T(8,128)(2,1)S(1)} custom-call(bf16[4096,128]{1,0:T(8,128)(2,1)} %bitcast.2.x_ref, bf16[1296,512]{1,0:T(8,128)(2,1)S(1)} %copy-done.3), custom_call_target="tpu_custom_call" | custom-call | tf_op jit(solution)/shard_map/pallas_call | solution.py:448
  88.9 10.2 %all-to-all-start.1 = ((bf16[64,8,8,128]{3,2,1,0:T(8,128)(2,1)}), bf16[64,8,8,128]{3,2,1,0:T(8,128)(2,1)}, u32[]{:S(2)}, u32[]{:S(2)}) async-start(bf16[64,8,8,128]{3,2,1,0:T(8,128)(2,1)} %bitcast.9), calls=%async_computation.1 | async-start | bytes 2097152 | tf_op jit(solution)/shard_map/all_to_all | solution.py:458
  101.5 15.5 %all-to-all-done.1.x_ref = bf16[64,8,8,128]{3,2,1,0:T(8,128)(2,1)} async-done(((bf16[64,8,8,128]{3,2,1,0:T(8,128)(2,1)}), bf16[64,8,8,128]{3,2,1,0:T(8,128)(2,1)}, u32[]{:S(2)}, u32[]{:S(2)}) %all-to-all-start.1) | async-done | bytes 1048608 | tf_op jit(solution)/shard_map/all_to_all | solution.py:458
  118.1 2.6 %shard_map.125 = (bf16[512,128]{1,0:T(8,128)(2,1)S(1)}, bf16[512,128]{1,0:T(8,128)(2,1)S(1)}, bf16[512,128]{1,0:T(8,128)(2,1)S(1)}, bf16[512,128]{1,0:T(8,128)(2...) custom-call(s32[1]{0:T(128)} %bitcast.me_ref, ...), custom_call_target="tpu_custom_call" | custom-call | tf_op jit(solution)/shard_map/pallas_call | solution.py:465
  120.7 3.4 %collective-permute-start.2 = (bf16[512,128]{1,0:T(8,128)(2,1)S(1)}, bf16[512,128]{1,0:T(8,128)(2,1)S(1)}, u32[]{:S(2)}, u32[]{:S(2)}) collective-permute-start(bf16[512,128]{1,0:T(8,128)(2,1)S(1)} %get-tuple-element.29), channel_id=1, source_target_pairs={{0,64},{64,128},{128,192},{192,0},{1,65},{65,129},{129,193},{193,1... | collective-permute-start | bytes 393224 | tf_op jit(solution)/shard_map/ppermute | solution.py:371
  125.2 3.3 %collective-permute-start.4 = (bf16[512,128]{1,0:T(8,128)(2,1)S(1)}, bf16[512,128]{1,0:T(8,128)(2,1)S(1)}, u32[]{:S(2)}, u32[]{:S(2)}) collective-permute-start(bf16[512,128]{1,0:T(8,128)(2,1)S(1)} %get-tuple-element.31), channel_id=1, source_target_pairs={{0,192},{64,0},{128,64},{192,128},{1,193},{65,1},{129,65},{193,129... | collective-permute-start | bytes 393224 | tf_op jit(solution)/shard_map/ppermute | solution.py:371
  128.6 3.3 %collective-permute-start.19 = (bf16[512,128]{1,0:T(8,128)(2,1)S(1)}, bf16[512,128]{1,0:T(8,128)(2,1)S(1)}, u32[]{:S(2)}, u32[]{:S(2)}) collective-permute-start(bf16[512,128]{1,0:T(8,128)(2,1)S(1)} %get-tuple-element.41), channel_id=1, source_target_pairs={{0,128},{64,192},{128,0},{192,64},{1,129},{65,193},{129,1},{193,65... | collective-permute-start | bytes 393224 | tf_op jit(solution)/shard_map/ppermute | solution.py:371
  131.8 1.5 collective-permute-start.20
  133.3 1.9 %collective-permute-done.3.x2 = bf16[512,128]{1,0:T(8,128)(2,1)S(1)} collective-permute-done((bf16[512,128]{1,0:T(8,128)(2,1)S(1)}, bf16[512,128]{1,0:T(8,128)(2,1)S(1)}, u32[]{:S(2)}, u32[]{:S(2)}) %collective-permute-start.3) | collective-permute-done | bytes 131104 | tf_op jit(solution)/shard_map/ppermute | solution.py:371
  135.2 12.1 %collective-permute-done.4.x3 = bf16[512,128]{1,0:T(8,128)(2,1)S(1)} collective-permute-done((bf16[512,128]{1,0:T(8,128)(2,1)S(1)}, bf16[512,128]{1,0:T(8,128)(2,1)S(1)}, u32[]{:S(2)}, u32[]{:S(2)}) %collective-permute-start.4) | collective-permute-done | bytes 131104 | tf_op jit(solution)/shard_map/ppermute | solution.py:371
  147.2 5.4 %shard_map.129 = (bf16[512,128]{1,0:T(8,128)(2,1)S(1)}, bf16[512,128]{1,0:T(8,128)(2,1)S(1)}, bf16[512,128]{1,0:T(8,128)(2,1)S(1)}, bf16[512,128]{1,0:T(8,128)(2,1)S(1)}) custom-call(s32[1]{0:T(128)} %bitcast.me_ref, bf16[512,128]{1,0:T(8,128)(2,1)S(1)} %get-tuple-element.28.x0, bf16[512,128]{1,0:T(8,128)(2,1)S(1)} %collective-permute-done.2.x1, ...), custom_call_target="tpu_custom_call" | custom-call | tf_op jit(solution)/shard_map/pallas_call | solution.py:477
  152.7 3.3 %collective-permute-start.15 = (bf16[512,128]{1,0:T(8,128)(2,1)S(1)}, bf16[512,128]{1,0:T(8,128)(2,1)S(1)}, u32[]{:S(2)}, u32[]{:S(2)}) collective-permute-start(bf16[512,128]{1,0:T(8,128)(2,1)S(1)} %get-tuple-element.36), channel_id=1, source_target_pairs={{0,64},{64,128},{128,192},{192,0},{1,65},{65,129},{129,193},{193,1... | collective-permute-start | bytes 393224 | tf_op jit(solution)/shard_map/ppermute | solution.py:371
  157.2 3.2 %collective-permute-start.17 = (bf16[512,128]{1,0:T(8,128)(2,1)S(1)}, bf16[512,128]{1,0:T(8,128)(2,1)S(1)}, u32[]{:S(2)}, u32[]{:S(2)}) collective-permute-start(bf16[512,128]{1,0:T(8,128)(2,1)S(1)} %get-tuple-element.38), channel_id=1, source_target_pairs={{0,192},{64,0},{128,64},{192,128},{1,193},{65,1},{129,65},{193,129... | collective-permute-start | bytes 393224 | tf_op jit(solution)/shard_map/ppermute | solution.py:371
  160.5 5.4 %shard_map.130 = (bf16[512,128]{1,0:T(8,128)(2,1)S(1)}, bf16[512,128]{1,0:T(8,128)(2,1)S(1)}, bf16[512,128]{1,0:T(8,128)(2,1)S(1)}, bf16[512,128]{1,0:T(8,128)(2,1)S(1)}) custom-call(s32[1]{0:T(128)} %bitcast.me_ref, bf16[512,128]{1,0:T(8,128)(2,1)S(1)} %get-tuple-element.39.x0, bf16[512,128]{1,0:T(8,128)(2,1)S(1)} %collective-permute-done.18.x1, ...), custom_call_target="tpu_custom_call" | custom-call | tf_op jit(solution)/shard_map/pallas_call | solution.py:477
  166.0 3.3 %collective-permute-start.22 = (bf16[512,128]{1,0:T(8,128)(2,1)S(1)}, bf16[512,128]{1,0:T(8,128)(2,1)S(1)}, u32[]{:S(2)}, u32[]{:S(2)}) collective-permute-start(bf16[512,128]{1,0:T(8,128)(2,1)S(1)} %get-tuple-element.45), channel_id=1, source_target_pairs={{0,128},{64,192},{128,0},{192,64},{1,129},{65,193},{129,1},{193,65... | collective-permute-start | bytes 393224 | tf_op jit(solution)/shard_map/ppermute | solution.py:371
  169.2 1.6 collective-permute-start.23
  171.9 7.6 %collective-permute-done.22.refs_6_ = bf16[512,128]{1,0:T(8,128)(2,1)S(1)} collective-permute-done((bf16[512,128]{1,0:T(8,128)(2,1)S(1)}, bf16[512,128]{1,0:T(8,128)(2,1)S(1)}, u32[]{:S(2)}, u32[]{:S(2)}) %collective-permute-start.22) | collective-permute-done | bytes 131104 | tf_op jit(solution)/shard_map/ppermute | solution.py:371
  (80 shorter events, 23.9 us)
Async XLA Ops:
  2.1 5.2 %collective-permute-start = (f32[2,8,512]{2,1,0:T(8,128)S(1)}, f32[2,8,512]{2,1,0:T(8,128)S(1)}, u32[]{:S(2)}, u32[]{:S(2)}) collective-permute-start(f32[2,8,512]{2,1,0:T(8,128)S(1)} %shard_map.118.left_ref), channel_id=1, source_target_pairs={{0,64},{64,0},{128,192},{192,128},{1,65},{65,1},{129,193},{193,129... | collective-permute-start | bytes 98312 | tf_op jit(solution)/shard_map/ppermute | solution.py:401
  7.3 8.4 %collective-permute-start.1 = (f32[2,8,512]{2,1,0:T(8,128)S(1)}, f32[2,8,512]{2,1,0:T(8,128)S(1)}, u32[]{:S(2)}, u32[]{:S(2)}) collective-permute-start(f32[2,8,512]{2,1,0:T(8,128)S(1)} %shard_map.119.left_ref), channel_id=1, source_target_pairs={{0,128},{64,192},{128,0},{192,64},{1,129},{65,193},{129,1},{193,65... | collective-permute-start | bytes 98312 | tf_op jit(solution)/shard_map/ppermute | solution.py:403
  19.2 60.9 %all-to-all-start = ((bf16[64,8,8,128]{3,2,1,0:T(8,128)(2,1)}), bf16[64,8,8,128]{3,2,1,0:T(8,128)(2,1)}, u32[]{:S(2)}, u32[]{:S(2)}) async-start(bf16[64,8,8,128]{3,2,1,0:T(8,128)(2,1)} %shard_map.121), calls=%async_computation | async-start | bytes 2097152 | tf_op jit(solution)/shard_map/all_to_all | solution.py:415
  30.6 21.3 %collective-permute-start.5 = (bf16[64,1152]{1,0:T(8,128)(2,1)S(1)}, bf16[64,1152]{1,0:T(8,128)(2,1)S(1)}, u32[]{:S(2)}, u32[]{:S(2)}) collective-permute-start(bf16[64,1152]{1,0:T(8,128)(2,1)S(1)} %shard_map.126.refs_0_), channel_id=1, source_target_pairs={{0,64},{64,128},{128,192},{192,0},{1,65},{65,129},{129,193},{193,1... | collective-permute-start | bytes 442376 | tf_op jit(solution)/shard_map/ppermute | solution.py:371
  32.9 23.3 %collective-permute-start.6 = (bf16[64,1152]{1,0:T(8,128)(2,1)S(1)}, bf16[64,1152]{1,0:T(8,128)(2,1)S(1)}, u32[]{:S(2)}, u32[]{:S(2)}) collective-permute-start(bf16[64,1152]{1,0:T(8,128)(2,1)S(1)} %shard_map.126.refs_0_), channel_id=1, source_target_pairs={{0,128},{64,192},{128,0},{192,64},{1,129},{65,193},{129,1},{193,65... | collective-permute-start | bytes 442376 | tf_op jit(solution)/shard_map/ppermute | solution.py:371
  37.2 19.0 %collective-permute-start.7 = (bf16[64,1152]{1,0:T(8,128)(2,1)S(1)}, bf16[64,1152]{1,0:T(8,128)(2,1)S(1)}, u32[]{:S(2)}, u32[]{:S(2)}) collective-permute-start(bf16[64,1152]{1,0:T(8,128)(2,1)S(1)} %shard_map.126.refs_0_), channel_id=1, source_target_pairs={{0,192},{64,0},{128,64},{192,128},{1,193},{65,1},{129,65},{193,129... | collective-permute-start | bytes 442376 | tf_op jit(solution)/shard_map/ppermute | solution.py:371
  56.4 8.8 %collective-permute-start.8 = (bf16[128,1152]{1,0:T(8,128)(2,1)S(1)}, bf16[128,1152]{1,0:T(8,128)(2,1)S(1)}, u32[]{:S(2)}, u32[]{:S(2)}) collective-permute-start(bf16[128,1152]{1,0:T(8,128)(2,1)S(1)} %get-tuple-element.32.refs_0_), channel_id=1, source_target_pairs={{0,16},{1,17},{2,18},{3,19},{4,20},{5,21},{6,22},{7,23},{8,24},{9,... | collective-permute-start | bytes 884744 | tf_op jit(solution)/shard_map/ppermute | solution.py:445
  57.8 14.7 %collective-permute-start.10 = (bf16[128,1152]{1,0:T(8,128)(2,1)S(1)}, bf16[128,1152]{1,0:T(8,128)(2,1)S(1)}, u32[]{:S(2)}, u32[]{:S(2)}) collective-permute-start(bf16[128,1152]{1,0:T(8,128)(2,1)S(1)} %get-tuple-element.32.refs_0_), channel_id=1, source_target_pairs={{0,32},{1,33},{2,34},{3,35},{4,36},{5,37},{6,38},{7,39},{8,40},{9,... | collective-permute-start | bytes 884744 | tf_op jit(solution)/shard_map/ppermute | solution.py:445
  60.4 18.4 %copy-start.13 = (f32[2,2,64,64]{3,2,1,0:T(8,128)S(1)}, f32[2,2,64,64]{3,2,1,0:T(8,128)}, u32[]{:S(2)}) copy-start(f32[2,2,64,64]{3,2,1,0:T(8,128)} %w1_ref.1) | copy-start | bytes 196612
  60.4 18.4 %copy-start.14 = (f32[2,2,64,64]{3,2,1,0:T(8,128)S(1)}, f32[2,2,64,64]{3,2,1,0:T(8,128)}, u32[]{:S(2)}) copy-start(f32[2,2,64,64]{3,2,1,0:T(8,128)} %w2_ref.1) | copy-start | bytes 196612
  60.4 18.4 %copy-start.18 = (f32[2,2,64]{2,1,0:T(2,128)S(1)}, f32[2,2,64]{2,1,0:T(2,128)}, u32[]{:S(2)}) copy-start(f32[2,2,64]{2,1,0:T(2,128)} %b1_ref.1) | copy-start | bytes 3076
  60.4 18.4 %copy-start.19 = (f32[2,2,64]{2,1,0:T(2,128)S(1)}, f32[2,2,64]{2,1,0:T(2,128)}, u32[]{:S(2)}) copy-start(f32[2,2,64]{2,1,0:T(2,128)} %b2_ref.1) | copy-start | bytes 3076
  60.4 7.9 %collective-permute-start.9 = (bf16[128,1152]{1,0:T(8,128)(2,1)S(1)}, bf16[128,1152]{1,0:T(8,128)(2,1)S(1)}, u32[]{:S(2)}, u32[]{:S(2)}) collective-permute-start(bf16[128,1152]{1,0:T(8,128)(2,1)S(1)} %get-tuple-element.33.refs_1_), channel_id=1, source_target_pairs={{0,2},{1,3},{2,4},{3,5},{4,6},{5,7},{6,0},{7,1},{8,10},{9,11},{10,... | collective-permute-start | bytes 884744 | tf_op jit(solution)/shard_map/ppermute | solution.py:445
  61.7 13.9 %collective-permute-start.11 = (bf16[128,1152]{1,0:T(8,128)(2,1)S(1)}, bf16[128,1152]{1,0:T(8,128)(2,1)S(1)}, u32[]{:S(2)}, u32[]{:S(2)}) collective-permute-start(bf16[128,1152]{1,0:T(8,128)(2,1)S(1)} %get-tuple-element.33.refs_1_), channel_id=1, source_target_pairs={{0,4},{1,5},{2,6},{3,7},{4,0},{5,1},{6,2},{7,3},{8,12},{9,13},{10,... | collective-permute-start | bytes 884744 | tf_op jit(solution)/shard_map/ppermute | solution.py:445
  64.1 11.5 %collective-permute-start.12 = (bf16[128,1152]{1,0:T(8,128)(2,1)S(1)}, bf16[128,1152]{1,0:T(8,128)(2,1)S(1)}, u32[]{:S(2)}, u32[]{:S(2)}) collective-permute-start(bf16[128,1152]{1,0:T(8,128)(2,1)S(1)} %get-tuple-element.32.refs_0_), channel_id=1, source_target_pairs={{0,48},{1,49},{2,50},{3,51},{4,52},{5,53},{6,54},{7,55},{8,56},{9,... | collective-permute-start | bytes 884744 | tf_op jit(solution)/shard_map/ppermute | solution.py:445
  65.2 10.4 %collective-permute-start.13 = (bf16[128,1152]{1,0:T(8,128)(2,1)S(1)}, bf16[128,1152]{1,0:T(8,128)(2,1)S(1)}, u32[]{:S(2)}, u32[]{:S(2)}) collective-permute-start(bf16[128,1152]{1,0:T(8,128)(2,1)S(1)} %get-tuple-element.33.refs_1_), channel_id=1, source_target_pairs={{0,6},{1,7},{2,0},{3,1},{4,2},{5,3},{6,4},{7,5},{8,14},{9,15},{10,... | collective-permute-start | bytes 884744 | tf_op jit(solution)/shard_map/ppermute | solution.py:445
  75.8 52.8 %collective-permute-start.14 = (bf16[1024,1152]{1,0:T(8,128)(2,1)S(1)}, bf16[1024,1152]{1,0:T(8,128)(2,1)}, u32[]{:S(2)}, u32[]{:S(2)}) collective-permute-start(bf16[1024,1152]{1,0:T(8,128)(2,1)S(1)} %shard_map.128.wa_ref), channel_id=1, source_target_pairs={{0,1},{1,0},{2,3},{3,2},{4,5},{5,4},{6,7},{7,6},{8,9},{9,8},{10,11... | collective-permute-start | bytes 7077896 | tf_op jit(solution)/shard_map/ppermute | solution.py:473
  88.9 28.1 %copy-start.17 = (f32[128]{0:T(128)S(1)}, f32[128]{0:T(128)}, u32[]{:S(2)}) copy-start(f32[128]{0:T(128)} %param.13) | copy-start | bytes 1540
  88.9 28.1 %all-to-all-start.1 = ((bf16[64,8,8,128]{3,2,1,0:T(8,128)(2,1)}), bf16[64,8,8,128]{3,2,1,0:T(8,128)(2,1)}, u32[]{:S(2)}, u32[]{:S(2)}) async-start(bf16[64,8,8,128]{3,2,1,0:T(8,128)(2,1)} %bitcast.9), calls=%async_computation.1 | async-start | bytes 2097152 | tf_op jit(solution)/shard_map/all_to_all | solution.py:458
  100.2 47.0 %copy-start.15 = (f32[512]{0:T(512)S(1)}, f32[512]{0:T(512)}, u32[]{:S(2)}) copy-start(f32[512]{0:T(512)} %param.18) | copy-start | bytes 6148
  120.7 11.1 %collective-permute-start.2 = (bf16[512,128]{1,0:T(8,128)(2,1)S(1)}, bf16[512,128]{1,0:T(8,128)(2,1)S(1)}, u32[]{:S(2)}, u32[]{:S(2)}) collective-permute-start(bf16[512,128]{1,0:T(8,128)(2,1)S(1)} %get-tuple-element.29), channel_id=1, source_target_pairs={{0,64},{64,128},{128,192},{192,0},{1,65},{65,129},{129,193},{193,1... | collective-permute-start | bytes 393224 | tf_op jit(solution)/shard_map/ppermute | solution.py:371
  124.1 11.1 %collective-permute-start.3 = (bf16[512,128]{1,0:T(8,128)(2,1)S(1)}, bf16[512,128]{1,0:T(8,128)(2,1)S(1)}, u32[]{:S(2)}, u32[]{:S(2)}) collective-permute-start(bf16[512,128]{1,0:T(8,128)(2,1)S(1)} %get-tuple-element.30), channel_id=1, source_target_pairs={{0,128},{64,192},{128,0},{192,64},{1,129},{65,193},{129,1},{193,65... | collective-permute-start | bytes 393224 | tf_op jit(solution)/shard_map/ppermute | solution.py:371
  125.2 22.0 %collective-permute-start.4 = (bf16[512,128]{1,0:T(8,128)(2,1)S(1)}, bf16[512,128]{1,0:T(8,128)(2,1)S(1)}, u32[]{:S(2)}, u32[]{:S(2)}) collective-permute-start(bf16[512,128]{1,0:T(8,128)(2,1)S(1)} %get-tuple-element.31), channel_id=1, source_target_pairs={{0,192},{64,0},{128,64},{192,128},{1,193},{65,1},{129,65},{193,129... | collective-permute-start | bytes 393224 | tf_op jit(solution)/shard_map/ppermute | solution.py:371
  128.6 28.7 %collective-permute-start.18 = (bf16[512,128]{1,0:T(8,128)(2,1)S(1)}, bf16[512,128]{1,0:T(8,128)(2,1)S(1)}, u32[]{:S(2)}, u32[]{:S(2)}) collective-permute-start(bf16[512,128]{1,0:T(8,128)(2,1)S(1)} %get-tuple-element.40), channel_id=1, source_target_pairs={{0,64},{64,128},{128,192},{192,0},{1,65},{65,129},{129,193},{193,1... | collective-permute-start | bytes 393224 | tf_op jit(solution)/shard_map/ppermute | solution.py:371
  128.6 31.9 %collective-permute-start.19 = (bf16[512,128]{1,0:T(8,128)(2,1)S(1)}, bf16[512,128]{1,0:T(8,128)(2,1)S(1)}, u32[]{:S(2)}, u32[]{:S(2)}) collective-permute-start(bf16[512,128]{1,0:T(8,128)(2,1)S(1)} %get-tuple-element.41), channel_id=1, source_target_pairs={{0,128},{64,192},{128,0},{192,64},{1,129},{65,193},{129,1},{193,65... | collective-permute-start | bytes 393224 | tf_op jit(solution)/shard_map/ppermute | solution.py:371
  131.8 28.6 %collective-permute-start.20 = (bf16[512,128]{1,0:T(8,128)(2,1)S(1)}, bf16[512,128]{1,0:T(8,128)(2,1)S(1)}, u32[]{:S(2)}, u32[]{:S(2)}) collective-permute-start(bf16[512,128]{1,0:T(8,128)(2,1)S(1)} %get-tuple-element.42), channel_id=1, source_target_pairs={{0,192},{64,0},{128,64},{192,128},{1,193},{65,1},{129,65},{193,129... | collective-permute-start | bytes 393224 | tf_op jit(solution)/shard_map/ppermute | solution.py:371
  152.7 16.6 %collective-permute-start.15 = (bf16[512,128]{1,0:T(8,128)(2,1)S(1)}, bf16[512,128]{1,0:T(8,128)(2,1)S(1)}, u32[]{:S(2)}, u32[]{:S(2)}) collective-permute-start(bf16[512,128]{1,0:T(8,128)(2,1)S(1)} %get-tuple-element.36), channel_id=1, source_target_pairs={{0,64},{64,128},{128,192},{192,0},{1,65},{65,129},{129,193},{193,1... | collective-permute-start | bytes 393224 | tf_op jit(solution)/shard_map/ppermute | solution.py:371
  156.0 14.8 %collective-permute-start.16 = (bf16[512,128]{1,0:T(8,128)(2,1)S(1)}, bf16[512,128]{1,0:T(8,128)(2,1)S(1)}, u32[]{:S(2)}, u32[]{:S(2)}) collective-permute-start(bf16[512,128]{1,0:T(8,128)(2,1)S(1)} %get-tuple-element.37), channel_id=1, source_target_pairs={{0,128},{64,192},{128,0},{192,64},{1,129},{65,193},{129,1},{193,65... | collective-permute-start | bytes 393224 | tf_op jit(solution)/shard_map/ppermute | solution.py:371
  157.2 14.7 %collective-permute-start.17 = (bf16[512,128]{1,0:T(8,128)(2,1)S(1)}, bf16[512,128]{1,0:T(8,128)(2,1)S(1)}, u32[]{:S(2)}, u32[]{:S(2)}) collective-permute-start(bf16[512,128]{1,0:T(8,128)(2,1)S(1)} %get-tuple-element.38), channel_id=1, source_target_pairs={{0,192},{64,0},{128,64},{192,128},{1,193},{65,1},{129,65},{193,129... | collective-permute-start | bytes 393224 | tf_op jit(solution)/shard_map/ppermute | solution.py:371
  165.9 6.0 %collective-permute-start.21 = (bf16[512,128]{1,0:T(8,128)(2,1)S(1)}, bf16[512,128]{1,0:T(8,128)(2,1)S(1)}, u32[]{:S(2)}, u32[]{:S(2)}) collective-permute-start(bf16[512,128]{1,0:T(8,128)(2,1)S(1)} %get-tuple-element.44), channel_id=1, source_target_pairs={{0,64},{64,128},{128,192},{192,0},{1,65},{65,129},{129,193},{193,1... | collective-permute-start | bytes 393224 | tf_op jit(solution)/shard_map/ppermute | solution.py:371
  166.0 13.6 %collective-permute-start.22 = (bf16[512,128]{1,0:T(8,128)(2,1)S(1)}, bf16[512,128]{1,0:T(8,128)(2,1)S(1)}, u32[]{:S(2)}, u32[]{:S(2)}) collective-permute-start(bf16[512,128]{1,0:T(8,128)(2,1)S(1)} %get-tuple-element.45), channel_id=1, source_target_pairs={{0,128},{64,192},{128,0},{192,64},{1,129},{65,193},{129,1},{193,65... | collective-permute-start | bytes 393224 | tf_op jit(solution)/shard_map/ppermute | solution.py:371
  169.2 10.3 %collective-permute-start.23 = (bf16[512,128]{1,0:T(8,128)(2,1)S(1)}, bf16[512,128]{1,0:T(8,128)(2,1)S(1)}, u32[]{:S(2)}, u32[]{:S(2)}) collective-permute-start(bf16[512,128]{1,0:T(8,128)(2,1)S(1)} %get-tuple-element.46), channel_id=1, source_target_pairs={{0,192},{64,0},{128,64},{192,128},{1,193},{65,1},{129,65},{193,129... | collective-permute-start | bytes 393224 | tf_op jit(solution)/shard_map/ppermute | solution.py:371
  (16 other events, 99.0 us)

commit v5 on v3

--- a/solution.py
+++ b/solution.py
@@ -15,17 +15,20 @@
 f32 = jnp.float32
 
 
-def tables(rows, width, per_owner):
+def circle_table(size):
+    grid = np.arange(size)
+    turn = 2.0 * np.pi / size * ((grid[:, None] * grid[None, :]) % size)
+    return np.concatenate([np.cos(turn[: size // 2]), np.sin(turn[: size // 2])], axis=0)
+
+
+def forward_table(width, per_owner):
     owners = width // 2 // per_owner
     place = np.arange(width)
     freq = np.arange(width // 2).reshape(owners, 1, per_owner)
     freq = np.broadcast_to(freq, (owners, 2, per_owner)).reshape(-1)
     part = np.broadcast_to(np.arange(2).reshape(1, 2, 1), (owners, 2, per_owner)).reshape(-1)
     angle = 2.0 * np.pi / width * ((freq[:, None] * place[None, :]) % width)
-    forward = np.where(part[:, None] == 0, np.cos(angle), -np.sin(angle))
-    grid = np.arange(rows)
-    turn = 2.0 * np.pi / rows * ((grid[:, None] * grid[None, :]) % rows)
-    return forward, np.cos(turn), np.sin(turn)
+    return np.where(part[:, None] == 0, np.cos(angle), -np.sin(angle))
 
 
 def mm(left, right):
@@ -58,6 +61,24 @@
     count = len(refs) // 2
     for source, target in zip(refs[:count], refs[count:]):
         target[...] = source[...]
+
+
+def flip_kernel(per_owner, lanes, table_ref, i_ref):
+    for start in range(0, table_ref.shape[0], lanes):
+        place = lax.broadcasted_iota(jnp.int32, (lanes, 1), 0) + start
+        weight = jnp.where((place == 0) | (place == per_owner), 1.0, 2.0)
+        part = table_ref[start : start + lanes, :].astype(f32) * weight
+        i_ref[:, start : start + lanes] = jnp.transpose(part).astype(bf16)
+
+
+def turn_kernel(half_ref, o_ref):
+    size, width = half_ref.shape[0] // 2, half_ref.shape[1]
+    column = lax.broadcasted_iota(jnp.int32, (size, width), 1)
+    sign = jnp.where(column % 2 == 0, 1.0, -1.0)
+    for part in range(2):
+        top = half_ref[part * size : (part + 1) * size, :]
+        o_ref[2 * part * size : (2 * part + 1) * size, :] = top
+        o_ref[(2 * part + 1) * size : (2 * part + 2) * size, :] = (top.astype(f32) * sign).astype(bf16)
 
 
 def moments(left_ref, right_ref, channels):
@@ -87,20 +108,19 @@
             )
 
 
-def residual_kernel(channels, x_ref, left_ref, right_ref, gain_ref, o_ref):
+def residual_kernel(channels, x_ref, left_ref, right_ref, gain_ref, o_ref, f_ref):
     rows = x_ref.shape[0]
-    flipped = moments(left_ref, right_ref, channels)
-    for row in range(rows):
+    f_ref[...] = moments(left_ref, right_ref, channels)
+    column = lax.broadcasted_iota(jnp.int32, f_ref.shape, 1)
+
+    def body(row, carry):
         source = x_ref[row].astype(f32)
-        o_ref[row] = normed_row(source, flipped, row, rows, gain_ref[...]) + source
-
-
-def flip_kernel(per_owner, lanes, table_ref, i_ref):
-    for start in range(0, table_ref.shape[0], lanes):
-        place = lax.broadcasted_iota(jnp.int32, (lanes, 1), 0) + start
-        weight = jnp.where((place == 0) | (place == per_owner), 1.0, 2.0)
-        part = table_ref[start : start + lanes, :].astype(f32) * weight
-        i_ref[:, start : start + lanes] = jnp.transpose(part).astype(bf16)
+        center = jnp.sum(jnp.where(column == row, f_ref[...], 0.0), axis=1, keepdims=True)
+        factor = jnp.sum(jnp.where(column == row + rows, f_ref[...], 0.0), axis=1, keepdims=True)
+        o_ref[row] = (source - center) * factor * gain_ref[...] + source
+        return carry
+
+    lax.fori_loop(0, rows, body, 0)
 
 
 def soften(values):
@@ -308,7 +328,7 @@
 
 
 def join_kernel(*refs):
-    *parts, o_ref = refs
+    *parts, after_ref, o_ref = refs
     start = 0
     for part in parts:
         o_ref[start : start + part.shape[0], :] = part[...]
@@ -365,9 +385,8 @@
     channels = lanes * ways
     per_owner = width // 2 // owners
     me = lax.axis_index("chan").astype(jnp.int32).reshape(1)
-    forward, cos, sin = tables(height, width, per_owner)
-    forward = jnp.asarray(forward, bf16)
-    turns = jnp.asarray(np.concatenate([cos, sin], axis=0), bf16)
+    forward = jnp.asarray(forward_table(width, per_owner), bf16)
+    turns = jnp.asarray(circle_table(height), bf16)
     half_scale = 2.0 ** math.floor(math.log2(math.sqrt(width)))
     first_scale, second_scale = 1.0 / half_scale, half_scale / math.sqrt(width * height)
 
@@ -400,7 +419,7 @@
     spectral = call(prep_kernel, shape((2 * wide + 16, wide), bf16), vmem(4))(
         spectral_w1, spectral_b1, spectral_w2, spectral_b2
     )
-    circle = call(warm_kernel, [shape(turns.shape, bf16)], vmem(1))(turns)[0]
+    circle = call(turn_kernel, shape((2 * height, height), bf16), vmem(1))(turns)
     stage = [mine] + shifts(lambda s: mine, "chan", ways)
     count = ways * units // 2
     *sides, out_bias = call(
@@ -435,6 +454,7 @@
         partial(residual_kernel, channels),
         shape((rows, width, lanes), f32),
         vmem(4),
+        scratch=[pltpu.VMEM((width, 2 * rows), f32)],
     )(tokens, left, right, gain_in.reshape(1, lanes))
     inverse = call(partial(flip_kernel, per_owner, lanes), shape((width, width), bf16), vmem(1))(forward)
     share = rows // ways * width // 2
@@ -448,10 +468,12 @@
     near = call(
         join_kernel,
         shape((2 * ring_x * parts[0].shape[0], parts[0].shape[1]), bf16),
-        vmem(len(parts)),
-    )(*parts)
+        vmem(len(parts)) + [pl.BlockSpec(memory_space=pl.ANY)],
+    )(*parts, mixed[0])
     far = lax.ppermute(near, "rows", [(i, i ^ 1) for i in range(owners)])
-    whole_b = [halves[1][0]] + shifts(lambda s: halves[1][s], "chan", ways)
+    whole_b = [halves[1][0]]
+    for shift in range(1, ways):
+        whole_b.append(lax.ppermute(halves[1][shift], "chan", [(i, (i + shift) % ways) for i in range(ways)]))
 
     def mlp(whole):
         return call(

time: 182 us -> 169 us (0.929)
  the two profiles are of different devices: /device:TPU:1 before, /device:TPU:4 now
where the time goes in v5:
time: 169 us; the launch traced here: 168 us
  starting transfers between devices  75.1 us (44%)
  waiting for transfers between devices  59.4 us (35%)
  Pallas kernels  25.1 us (15%)
  local copies, waits for them, and re-layouts  8.4 us (5%)
    ppermute x12, waiting for transfers between devices, shifts(): lax.ppermute(value_of(shift), axis, [(i, (i + shift) % ways) for i in ran...  37.6 us
    ppermute x12, starting transfers between devices, shifts(): lax.ppermute(value_of(shift), axis, [(i, (i + shift) % ways) for i in ran...  34.4 us
    all_to_all x1, waiting for transfers between devices, local(): columns = lax.all_to_all(spectra, 'rows', split_axis=0, concat_axis=0)  12.3 us
    ppermute x6, starting transfers between devices, local(): parts.append(lax.ppermute(sides[half], 'rows', ring[half]))  9.87 us
    all_to_all x1, starting transfers between devices, local(): columns = lax.all_to_all(spectra, 'rows', split_axis=0, concat_axis=0)  9.03 us
    unnamed x40, local copies, waits for them, and re-layouts  8.39 us
    all_to_all x1, starting transfers between devices, local(): lax.all_to_all(back.reshape(owners, rows, 2 * per_owner, lanes), 'rows',...  7.89 us
    ppermute x6, waiting for transfers between devices, local(): parts.append(lax.ppermute(sides[half], 'rows', ring[half]))  7.45 us
  transfers between devices with their start and end apart: 26, of which 10 were waited for; matrix products, arithmetic and copies ran while one was open for 0% of the time, Pallas kernels for 8%

profile of v5, /device:TPU:4, one launch (start us, length us, event | category | flops | bytes accessed | tf_op | source)
XLA Modules:
  0.0 168.4 jit_solution(15474919624342399400)
XLA Ops:
  2.1 3.3 %collective-permute-start = (f32[2,8,512]{2,1,0:T(8,128)S(1)}, f32[2,8,512]{2,1,0:T(8,128)S(1)}, u32[]{:S(2)}, u32[]{:S(2)}) collective-permute-start(f32[2,8,512]{2,1,0:T(8,128)S(1)} %shard_map.127.left_ref), channel_id=1, source_target_pairs={{0,64},{64,0},{128,192},{192,128},{1,65},{65,1},{129,193},{193,129... | collective-permute-start | bytes 98312 | tf_op jit(solution)/shard_map/ppermute | solution.py:394
  5.5 1.9 %collective-permute-done.right_ref = f32[2,8,512]{2,1,0:T(8,128)S(1)} collective-permute-done((f32[2,8,512]{2,1,0:T(8,128)S(1)}, f32[2,8,512]{2,1,0:T(8,128)S(1)}, u32[]{:S(2)}, u32[]{:S(2)}) %collective-permute-start) | collective-permute-done | bytes 32800 | tf_op jit(solution)/shard_map/ppermute | solution.py:394
  7.4 6.8 %collective-permute-start.1 = (f32[2,8,512]{2,1,0:T(8,128)S(1)}, f32[2,8,512]{2,1,0:T(8,128)S(1)}, u32[]{:S(2)}, u32[]{:S(2)}) collective-permute-start(f32[2,8,512]{2,1,0:T(8,128)S(1)} %shard_map.128.left_ref), channel_id=1, source_target_pairs={{0,128},{64,192},{128,0},{192,64},{1,129},{65,193},{129,1},{193,65... | collective-permute-start | bytes 98312 | tf_op jit(solution)/shard_map/ppermute | solution.py:396
  16.1 2.7 %shard_map.130 = bf16[64,8,8,128]{3,2,1,0:T(8,128)(2,1)} custom-call(bf16[8,512,128]{2,1,0:T(8,128)(2,1)S(1)} %copy-done.1, f32[2,8,512]{2,1,0:T(8,128)S(1)} %shard_map.128.left_ref, f32[2,8,512]{2,1,0:T(8,128)S(1)} %collective-permute-done.1.right_ref, f32[1,128]{1,0:T(1,128)S(1)} %get-tuple-element.26.gain_ref, ...), custom_call_target="tpu_custom_call" | custom-call | tf_op jit(solution)/shard_map/pallas_call | solution.py:400
  18.8 9.0 %all-to-all-start = ((bf16[64,8,8,128]{3,2,1,0:T(8,128)(2,1)}), bf16[64,8,8,128]{3,2,1,0:T(8,128)(2,1)S(1)}, u32[]{:S(2)}, u32[]{:S(2)}) async-start(bf16[64,8,8,128]{3,2,1,0:T(8,128)(2,1)} %shard_map.130), calls=%async_computation | async-start | bytes 2097152 | tf_op jit(solution)/shard_map/all_to_all | solution.py:405
  30.9 12.3 %all-to-all-done = bf16[64,8,8,128]{3,2,1,0:T(8,128)(2,1)S(1)} async-done(((bf16[64,8,8,128]{3,2,1,0:T(8,128)(2,1)}), bf16[64,8,8,128]{3,2,1,0:T(8,128)(2,1)S(1)}, u32[]{:S(2)}, u32[]{:S(2)}) %all-to-all-start) | async-done | bytes 1048608 | tf_op jit(solution)/shard_map/all_to_all | solution.py:405
  43.2 5.3 %shard_map.133 = bf16[4096,128]{1,0:T(8,128)(2,1)} custom-call(bf16[4096,128]{1,0:T(8,128)(2,1)S(1)} %bitcast.9, bf16[1024,512]{1,0:T(8,128)(2,1)S(1)} %shard_map.131.table_ref, bf16[528,256]{1,0:T(8,128)(2,1)S(1)} %shard_map.132.w_ref), custom_call_target="tpu_custom_call" | custom-call | tf_op jit(solution)/shard_map/pallas_call | solution.py:440
  48.5 7.9 %all-to-all-start.1 = ((bf16[64,8,8,128]{3,2,1,0:T(8,128)(2,1)}), bf16[64,8,8,128]{3,2,1,0:T(8,128)(2,1)}, u32[]{:S(2)}, u32[]{:S(2)}) async-start(bf16[64,8,8,128]{3,2,1,0:T(8,128)(2,1)} %bitcast.3), calls=%async_computation.1 | async-start | bytes 2097152 | tf_op jit(solution)/shard_map/all_to_all | solution.py:450
  57.4 2.6 %collective-permute-start.5 = (bf16[64,1152]{1,0:T(8,128)(2,1)S(1)}, bf16[64,1152]{1,0:T(8,128)(2,1)S(1)}, u32[]{:S(2)}, u32[]{:S(2)}) collective-permute-start(bf16[64,1152]{1,0:T(8,128)(2,1)S(1)} %shard_map.137.refs_0_), channel_id=1, source_target_pairs={{0,64},{64,128},{128,192},{192,0},{1,65},{65,129},{129,193},{193,1... | collective-permute-start | bytes 442376 | tf_op jit(solution)/shard_map/ppermute | solution.py:363
  60.0 4.5 %collective-permute-start.6 = (bf16[64,1152]{1,0:T(8,128)(2,1)S(1)}, bf16[64,1152]{1,0:T(8,128)(2,1)S(1)}, u32[]{:S(2)}, u32[]{:S(2)}) collective-permute-start(bf16[64,1152]{1,0:T(8,128)(2,1)S(1)} %shard_map.137.refs_0_), channel_id=1, source_target_pairs={{0,128},{64,192},{128,0},{192,64},{1,129},{65,193},{129,1},{193,65... | collective-permute-start | bytes 442376 | tf_op jit(solution)/shard_map/ppermute | solution.py:363
  64.5 2.7 %collective-permute-start.7 = (bf16[64,1152]{1,0:T(8,128)(2,1)S(1)}, bf16[64,1152]{1,0:T(8,128)(2,1)S(1)}, u32[]{:S(2)}, u32[]{:S(2)}) collective-permute-start(bf16[64,1152]{1,0:T(8,128)(2,1)S(1)} %shard_map.137.refs_0_), channel_id=1, source_target_pairs={{0,192},{64,0},{128,64},{192,128},{1,193},{65,1},{129,65},{193,129... | collective-permute-start | bytes 442376 | tf_op jit(solution)/shard_map/ppermute | solution.py:363
  67.2 12.8 %collective-permute-done.5.refs_1_ = bf16[64,1152]{1,0:T(8,128)(2,1)S(1)} collective-permute-done((bf16[64,1152]{1,0:T(8,128)(2,1)S(1)}, bf16[64,1152]{1,0:T(8,128)(2,1)S(1)}, u32[]{:S(2)}, u32[]{:S(2)}) %collective-permute-start.5) | collective-permute-done | bytes 147488 | tf_op jit(solution)/shard_map/ppermute | solution.py:363
  80.0 3.9 %collective-permute-done.6.refs_2_ = bf16[64,1152]{1,0:T(8,128)(2,1)S(1)} collective-permute-done((bf16[64,1152]{1,0:T(8,128)(2,1)S(1)}, bf16[64,1152]{1,0:T(8,128)(2,1)S(1)}, u32[]{:S(2)}, u32[]{:S(2)}) %collective-permute-start.6) | collective-permute-done | bytes 147488 | tf_op jit(solution)/shard_map/ppermute | solution.py:363
  88.3 2.7 %collective-permute-start.11 = (bf16[128,1152]{1,0:T(8,128)(2,1)}, bf16[128,1152]{1,0:T(8,128)(2,1)}, u32[]{:S(2)}, u32[]{:S(2)}) collective-permute-start(bf16[128,1152]{1,0:T(8,128)(2,1)} %get-tuple-element.33.refs_1_), channel_id=1, source_target_pairs={{0,4},{1,5},{2,6},{3,7},{4,0},{5,1},{6,2},{7,3},{8,12},{9,13},{10,... | collective-permute-start | bytes 884744 | tf_op jit(solution)/shard_map/ppermute | solution.py:437
  92.1 7.4 %collective-permute-done.8.refs_2_ = bf16[128,1152]{1,0:T(8,128)(2,1)S(1)} collective-permute-done((bf16[128,1152]{1,0:T(8,128)(2,1)}, bf16[128,1152]{1,0:T(8,128)(2,1)S(1)}, u32[]{:S(2)}, u32[]{:S(2)}) %collective-permute-start.8) | collective-permute-done | bytes 294944 | tf_op jit(solution)/shard_map/ppermute | solution.py:437
  100.2 2.7 %collective-permute-start.13 = (bf16[128,1152]{1,0:T(8,128)(2,1)}, bf16[128,1152]{1,0:T(8,128)(2,1)}, u32[]{:S(2)}, u32[]{:S(2)}) collective-permute-start(bf16[128,1152]{1,0:T(8,128)(2,1)} %get-tuple-element.33.refs_1_), channel_id=1, source_target_pairs={{0,6},{1,7},{2,0},{3,1},{4,2},{5,3},{6,4},{7,5},{8,14},{9,15},{10,... | collective-permute-start | bytes 884744 | tf_op jit(solution)/shard_map/ppermute | solution.py:437
  104.0 1.8 %shard_map.135.r_ref = f32[8,512,128]{2,1,0:T(8,128)S(1)} custom-call(bf16[8,512,128]{2,1,0:T(8,128)(2,1)S(1)} %copy-done.1, f32[2,8,512]{2,1,0:T(8,128)S(1)} %shard_map.128.left_ref, f32[2,8,512]{2,1,0:T(8,128)S(1)} %collective-permute-done.1.right_ref, f32[1,128]{1,0:T(1,128)S(1)} %bitcast.13), custom_call_target="tpu_custom_call" | custom-call | tf_op jit(solution)/shard_map/pallas_call | solution.py:453
  106.9 2.0 %shard_map.136 = (bf16[512,128]{1,0:T(8,128)(2,1)S(1)}, bf16[512,128]{1,0:T(8,128)(2,1)S(1)}, bf16[512,128]{1,0:T(8,128)(2,1)S(1)}, bf16[512,128]{1,0:T(8,128)(2...) custom-call(s32[1]{0:T(128)} %bitcast.me_ref, ...), custom_call_target="tpu_custom_call" | custom-call | tf_op jit(solution)/shard_map/pallas_call | solution.py:461
  110.8 4.5 %collective-permute-start.2 = (bf16[512,128]{1,0:T(8,128)(2,1)S(1)}, bf16[512,128]{1,0:T(8,128)(2,1)S(1)}, u32[]{:S(2)}, u32[]{:S(2)}) collective-permute-start(bf16[512,128]{1,0:T(8,128)(2,1)S(1)} %get-tuple-element.29), channel_id=1, source_target_pairs={{0,64},{64,128},{128,192},{192,0},{1,65},{65,129},{129,193},{193,1... | collective-permute-start | bytes 393224 | tf_op jit(solution)/shard_map/ppermute | solution.py:363
  116.7 2.2 %collective-permute-start.4 = (bf16[512,128]{1,0:T(8,128)(2,1)S(1)}, bf16[512,128]{1,0:T(8,128)(2,1)S(1)}, u32[]{:S(2)}, u32[]{:S(2)}) collective-permute-start(bf16[512,128]{1,0:T(8,128)(2,1)S(1)} %get-tuple-element.31), channel_id=1, source_target_pairs={{0,192},{64,0},{128,64},{192,128},{1,193},{65,1},{129,65},{193,129... | collective-permute-start | bytes 393224 | tf_op jit(solution)/shard_map/ppermute | solution.py:363
  119.6 3.0 %collective-permute-done.2.x1 = bf16[512,128]{1,0:T(8,128)(2,1)S(1)} collective-permute-done((bf16[512,128]{1,0:T(8,128)(2,1)S(1)}, bf16[512,128]{1,0:T(8,128)(2,1)S(1)}, u32[]{:S(2)}, u32[]{:S(2)}) %collective-permute-start.2) | collective-permute-done | bytes 131104 | tf_op jit(solution)/shard_map/ppermute | solution.py:363
  122.6 2.6 %collective-permute-start.19 = (bf16[512,128]{1,0:T(8,128)(2,1)S(1)}, bf16[512,128]{1,0:T(8,128)(2,1)S(1)}, u32[]{:S(2)}, u32[]{:S(2)}) collective-permute-start(bf16[512,128]{1,0:T(8,128)(2,1)S(1)} %get-tuple-element.41), channel_id=1, source_target_pairs={{0,128},{64,192},{128,0},{192,64},{1,129},{65,193},{129,1},{193,65... | collective-permute-start | bytes 393224 | tf_op jit(solution)/shard_map/ppermute | solution.py:476
  125.2 5.0 %collective-permute-done.3.x2 = bf16[512,128]{1,0:T(8,128)(2,1)S(1)} collective-permute-done((bf16[512,128]{1,0:T(8,128)(2,1)S(1)}, bf16[512,128]{1,0:T(8,128)(2,1)S(1)}, u32[]{:S(2)}, u32[]{:S(2)}) %collective-permute-start.3) | collective-permute-done | bytes 131104 | tf_op jit(solution)/shard_map/ppermute | solution.py:363
  130.6 7.4 %collective-permute-done.4.x3 = bf16[512,128]{1,0:T(8,128)(2,1)S(1)} collective-permute-done((bf16[512,128]{1,0:T(8,128)(2,1)S(1)}, bf16[512,128]{1,0:T(8,128)(2,1)S(1)}, u32[]{:S(2)}, u32[]{:S(2)}) %collective-permute-start.4) | collective-permute-done | bytes 131104 | tf_op jit(solution)/shard_map/ppermute | solution.py:363
  138.0 3.7 %shard_map.140 = (bf16[512,128]{1,0:T(8,128)(2,1)S(1)}, bf16[512,128]{1,0:T(8,128)(2,1)S(1)}, bf16[512,128]{1,0:T(8,128)(2,1)S(1)}, bf16[512,128]{1,0:T(8,128)(2,1)S(1)}) custom-call(s32[1]{0:T(128)} %bitcast.me_ref, bf16[512,128]{1,0:T(8,128)(2,1)S(1)} %get-tuple-element.28.refs_8_.x0, bf16[512,128]{1,0:T(8,128)(2,1)S(1)} %collective-permute-done.2.x1, ...), custom_call_target="tpu_custom_call" | custom-call | tf_op jit(solution)/shard_map/pallas_call | solution.py:479
  141.7 1.9 %collective-permute-start.15 = (bf16[512,128]{1,0:T(8,128)(2,1)S(1)}, bf16[512,128]{1,0:T(8,128)(2,1)S(1)}, u32[]{:S(2)}, u32[]{:S(2)}) collective-permute-start(bf16[512,128]{1,0:T(8,128)(2,1)S(1)} %get-tuple-element.36), channel_id=1, source_target_pairs={{0,64},{64,128},{128,192},{192,0},{1,65},{65,129},{129,193},{193,1... | collective-permute-start | bytes 393224 | tf_op jit(solution)/shard_map/ppermute | solution.py:363
  143.6 1.7 %collective-permute-start.16 = (bf16[512,128]{1,0:T(8,128)(2,1)S(1)}, bf16[512,128]{1,0:T(8,128)(2,1)S(1)}, u32[]{:S(2)}, u32[]{:S(2)}) collective-permute-start(bf16[512,128]{1,0:T(8,128)(2,1)S(1)} %get-tuple-element.37), channel_id=1, source_target_pairs={{0,128},{64,192},{128,0},{192,64},{1,129},{65,193},{129,1},{193,65... | collective-permute-start | bytes 393224 | tf_op jit(solution)/shard_map/ppermute | solution.py:363
  145.4 4.0 %collective-permute-start.17 = (bf16[512,128]{1,0:T(8,128)(2,1)S(1)}, bf16[512,128]{1,0:T(8,128)(2,1)S(1)}, u32[]{:S(2)}, u32[]{:S(2)}) collective-permute-start(bf16[512,128]{1,0:T(8,128)(2,1)S(1)} %get-tuple-element.38), channel_id=1, source_target_pairs={{0,192},{64,0},{128,64},{192,128},{1,193},{65,1},{129,65},{193,129... | collective-permute-start | bytes 393224 | tf_op jit(solution)/shard_map/ppermute | solution.py:363
  149.4 3.7 %shard_map.141 = (bf16[512,128]{1,0:T(8,128)(2,1)S(1)}, bf16[512,128]{1,0:T(8,128)(2,1)S(1)}, bf16[512,128]{1,0:T(8,128)(2,1)S(1)}, bf16[512,128]{1,0:T(8,128)(2,1)S(1)}) custom-call(s32[1]{0:T(128)} %bitcast.me_ref, bf16[512,128]{1,0:T(8,128)(2,1)S(1)} %get-tuple-element.39.x0, bf16[512,128]{1,0:T(8,128)(2,1)S(1)} %collective-permute-done.18.x1, ...), custom_call_target="tpu_custom_call" | custom-call | tf_op jit(solution)/shard_map/pallas_call | solution.py:479
  153.2 4.7 %collective-permute-start.22 = (bf16[512,128]{1,0:T(8,128)(2,1)S(1)}, bf16[512,128]{1,0:T(8,128)(2,1)S(1)}, u32[]{:S(2)}, u32[]{:S(2)}) collective-permute-start(bf16[512,128]{1,0:T(8,128)(2,1)S(1)} %get-tuple-element.45), channel_id=1, source_target_pairs={{0,128},{64,192},{128,0},{192,64},{1,129},{65,193},{129,1},{193,65... | collective-permute-start | bytes 393224 | tf_op jit(solution)/shard_map/ppermute | solution.py:363
  157.9 4.0 %collective-permute-start.23 = (bf16[512,128]{1,0:T(8,128)(2,1)S(1)}, bf16[512,128]{1,0:T(8,128)(2,1)S(1)}, u32[]{:S(2)}, u32[]{:S(2)}) collective-permute-start(bf16[512,128]{1,0:T(8,128)(2,1)S(1)} %get-tuple-element.46), channel_id=1, source_target_pairs={{0,192},{64,0},{128,64},{192,128},{1,193},{65,1},{129,65},{193,129... | collective-permute-start | bytes 393224 | tf_op jit(solution)/shard_map/ppermute | solution.py:363
  161.9 5.4 %collective-permute-done.22.refs_6_ = bf16[512,128]{1,0:T(8,128)(2,1)S(1)} collective-permute-done((bf16[512,128]{1,0:T(8,128)(2,1)S(1)}, bf16[512,128]{1,0:T(8,128)(2,1)S(1)}, u32[]{:S(2)}, u32[]{:S(2)}) %collective-permute-start.22) | collective-permute-done | bytes 131104 | tf_op jit(solution)/shard_map/ppermute | solution.py:363
  (78 shorter events, 21.7 us)
Async XLA Ops:
  1.2 14.9 %copy-start.1 = (bf16[8,512,128]{2,1,0:T(8,128)(2,1)S(1)}, bf16[8,512,128]{2,1,0:T(8,128)(2,1)}, u32[]{:S(2)}) copy-start(bf16[8,512,128]{2,1,0:T(8,128)(2,1)} %x_ref.5) | copy-start | bytes 3145732
  2.1 5.2 %collective-permute-start = (f32[2,8,512]{2,1,0:T(8,128)S(1)}, f32[2,8,512]{2,1,0:T(8,128)S(1)}, u32[]{:S(2)}, u32[]{:S(2)}) collective-permute-start(f32[2,8,512]{2,1,0:T(8,128)S(1)} %shard_map.127.left_ref), channel_id=1, source_target_pairs={{0,64},{64,0},{128,192},{192,128},{1,65},{65,1},{129,193},{193,129... | collective-permute-start | bytes 98312 | tf_op jit(solution)/shard_map/ppermute | solution.py:394
  7.4 8.7 %collective-permute-start.1 = (f32[2,8,512]{2,1,0:T(8,128)S(1)}, f32[2,8,512]{2,1,0:T(8,128)S(1)}, u32[]{:S(2)}, u32[]{:S(2)}) collective-permute-start(f32[2,8,512]{2,1,0:T(8,128)S(1)} %shard_map.128.left_ref), channel_id=1, source_target_pairs={{0,128},{64,192},{128,0},{192,64},{1,129},{65,193},{129,1},{193,65... | collective-permute-start | bytes 98312 | tf_op jit(solution)/shard_map/ppermute | solution.py:396
  18.8 24.4 %all-to-all-start = ((bf16[64,8,8,128]{3,2,1,0:T(8,128)(2,1)}), bf16[64,8,8,128]{3,2,1,0:T(8,128)(2,1)S(1)}, u32[]{:S(2)}, u32[]{:S(2)}) async-start(bf16[64,8,8,128]{3,2,1,0:T(8,128)(2,1)} %shard_map.130), calls=%async_computation | async-start | bytes 2097152 | tf_op jit(solution)/shard_map/all_to_all | solution.py:405
  43.2 13.2 %copy-start.19 = (bf16[512]{0:T(512)(128)(2,1)S(1)}, bf16[512]{0:T(512)(128)(2,1)}, u32[]{:S(2)}) copy-start(bf16[512]{0:T(512)(128)(2,1)} %param.21) | copy-start | bytes 3076
  43.2 13.3 %copy-start.18 = (bf16[128]{0:T(256)(128)(2,1)S(1)}, bf16[128]{0:T(256)(128)(2,1)}, u32[]{:S(2)}) copy-start(bf16[128]{0:T(256)(128)(2,1)} %param.23) | copy-start | bytes 772
  48.5 54.5 %copy-start.3 = (bf16[512,512]{1,0:T(8,128)(2,1)S(1)}, bf16[512,512]{1,0:T(8,128)(2,1)}, u32[]{:S(2)}) copy-start(bf16[512,512]{1,0:T(8,128)(2,1)} %constant.57.clone.refs_0_.table_ref) | copy-start | bytes 1572868
  48.5 55.5 %copy-start.17 = (f32[128]{0:T(128)S(1)}, f32[128]{0:T(128)}, u32[]{:S(2)}) copy-start(f32[128]{0:T(128)} %param.14) | copy-start | bytes 1540
  48.5 57.4 %all-to-all-start.1 = ((bf16[64,8,8,128]{3,2,1,0:T(8,128)(2,1)}), bf16[64,8,8,128]{3,2,1,0:T(8,128)(2,1)}, u32[]{:S(2)}, u32[]{:S(2)}) async-start(bf16[64,8,8,128]{3,2,1,0:T(8,128)(2,1)} %bitcast.3), calls=%async_computation.1 | async-start | bytes 2097152 | tf_op jit(solution)/shard_map/all_to_all | solution.py:450
  57.4 22.6 %collective-permute-start.5 = (bf16[64,1152]{1,0:T(8,128)(2,1)S(1)}, bf16[64,1152]{1,0:T(8,128)(2,1)S(1)}, u32[]{:S(2)}, u32[]{:S(2)}) collective-permute-start(bf16[64,1152]{1,0:T(8,128)(2,1)S(1)} %shard_map.137.refs_0_), channel_id=1, source_target_pairs={{0,64},{64,128},{128,192},{192,0},{1,65},{65,129},{129,193},{193,1... | collective-permute-start | bytes 442376 | tf_op jit(solution)/shard_map/ppermute | solution.py:363
  60.0 23.9 %collective-permute-start.6 = (bf16[64,1152]{1,0:T(8,128)(2,1)S(1)}, bf16[64,1152]{1,0:T(8,128)(2,1)S(1)}, u32[]{:S(2)}, u32[]{:S(2)}) collective-permute-start(bf16[64,1152]{1,0:T(8,128)(2,1)S(1)} %shard_map.137.refs_0_), channel_id=1, source_target_pairs={{0,128},{64,192},{128,0},{192,64},{1,129},{65,193},{129,1},{193,65... | collective-permute-start | bytes 442376 | tf_op jit(solution)/shard_map/ppermute | solution.py:363
  64.5 19.4 %collective-permute-start.7 = (bf16[64,1152]{1,0:T(8,128)(2,1)S(1)}, bf16[64,1152]{1,0:T(8,128)(2,1)S(1)}, u32[]{:S(2)}, u32[]{:S(2)}) collective-permute-start(bf16[64,1152]{1,0:T(8,128)(2,1)S(1)} %shard_map.137.refs_0_), channel_id=1, source_target_pairs={{0,192},{64,0},{128,64},{192,128},{1,193},{65,1},{129,65},{193,129... | collective-permute-start | bytes 442376 | tf_op jit(solution)/shard_map/ppermute | solution.py:363
  84.9 14.6 %collective-permute-start.8 = (bf16[128,1152]{1,0:T(8,128)(2,1)}, bf16[128,1152]{1,0:T(8,128)(2,1)S(1)}, u32[]{:S(2)}, u32[]{:S(2)}) collective-permute-start(bf16[128,1152]{1,0:T(8,128)(2,1)} %get-tuple-element.32.refs_0_), channel_id=1, source_target_pairs={{0,16},{1,17},{2,18},{3,19},{4,20},{5,21},{6,22},{7,23},{8,24},{9,... | collective-permute-start | bytes 884744 | tf_op jit(solution)/shard_map/ppermute | solution.py:437
  86.2 22.7 %collective-permute-start.10 = (bf16[128,1152]{1,0:T(8,128)(2,1)}, bf16[128,1152]{1,0:T(8,128)(2,1)}, u32[]{:S(2)}, u32[]{:S(2)}) collective-permute-start(bf16[128,1152]{1,0:T(8,128)(2,1)} %get-tuple-element.32.refs_0_), channel_id=1, source_target_pairs={{0,32},{1,33},{2,34},{3,35},{4,36},{5,37},{6,38},{7,39},{8,40},{9,... | collective-permute-start | bytes 884744 | tf_op jit(solution)/shard_map/ppermute | solution.py:437
  86.8 22.1 %collective-permute-start.9 = (bf16[128,1152]{1,0:T(8,128)(2,1)}, bf16[128,1152]{1,0:T(8,128)(2,1)}, u32[]{:S(2)}, u32[]{:S(2)}) collective-permute-start(bf16[128,1152]{1,0:T(8,128)(2,1)} %get-tuple-element.33.refs_1_), channel_id=1, source_target_pairs={{0,2},{1,3},{2,4},{3,5},{4,6},{5,7},{6,0},{7,1},{8,10},{9,11},{10,... | collective-permute-start | bytes 884744 | tf_op jit(solution)/shard_map/ppermute | solution.py:437
  88.3 20.6 %collective-permute-start.11 = (bf16[128,1152]{1,0:T(8,128)(2,1)}, bf16[128,1152]{1,0:T(8,128)(2,1)}, u32[]{:S(2)}, u32[]{:S(2)}) collective-permute-start(bf16[128,1152]{1,0:T(8,128)(2,1)} %get-tuple-element.33.refs_1_), channel_id=1, source_target_pairs={{0,4},{1,5},{2,6},{3,7},{4,0},{5,1},{6,2},{7,3},{8,12},{9,13},{10,... | collective-permute-start | bytes 884744 | tf_op jit(solution)/shard_map/ppermute | solution.py:437
  91.0 18.0 %collective-permute-start.12 = (bf16[128,1152]{1,0:T(8,128)(2,1)}, bf16[128,1152]{1,0:T(8,128)(2,1)}, u32[]{:S(2)}, u32[]{:S(2)}) collective-permute-start(bf16[128,1152]{1,0:T(8,128)(2,1)} %get-tuple-element.32.refs_0_), channel_id=1, source_target_pairs={{0,48},{1,49},{2,50},{3,51},{4,52},{5,53},{6,54},{7,55},{8,56},{9,... | collective-permute-start | bytes 884744 | tf_op jit(solution)/shard_map/ppermute | solution.py:437
  100.2 8.7 %collective-permute-start.13 = (bf16[128,1152]{1,0:T(8,128)(2,1)}, bf16[128,1152]{1,0:T(8,128)(2,1)}, u32[]{:S(2)}, u32[]{:S(2)}) collective-permute-start(bf16[128,1152]{1,0:T(8,128)(2,1)} %get-tuple-element.33.refs_1_), channel_id=1, source_target_pairs={{0,6},{1,7},{2,0},{3,1},{4,2},{5,3},{6,4},{7,5},{8,14},{9,15},{10,... | collective-permute-start | bytes 884744 | tf_op jit(solution)/shard_map/ppermute | solution.py:437
  109.0 29.1 %copy-start.13 = (f32[512]{0:T(512)S(1)}, f32[512]{0:T(512)}, u32[]{:S(2)}) copy-start(f32[512]{0:T(512)} %param.19) | copy-start | bytes 6148
  110.7 27.4 %collective-permute-start.14 = (bf16[1024,1152]{1,0:T(8,128)(2,1)S(1)}, bf16[1024,1152]{1,0:T(8,128)(2,1)S(1)}, u32[]{:S(2)}, u32[]{:S(2)}) collective-permute-start(bf16[1024,1152]{1,0:T(8,128)(2,1)S(1)} %shard_map.139.wa_ref), channel_id=1, source_target_pairs={{0,1},{1,0},{2,3},{3,2},{4,5},{5,4},{6,7},{7,6},{8,9},{9,8},{10,11... | collective-permute-start | bytes 7077896 | tf_op jit(solution)/shard_map/ppermute | solution.py:473
  110.8 11.8 %collective-permute-start.2 = (bf16[512,128]{1,0:T(8,128)(2,1)S(1)}, bf16[512,128]{1,0:T(8,128)(2,1)S(1)}, u32[]{:S(2)}, u32[]{:S(2)}) collective-permute-start(bf16[512,128]{1,0:T(8,128)(2,1)S(1)} %get-tuple-element.29), channel_id=1, source_target_pairs={{0,64},{64,128},{128,192},{192,0},{1,65},{65,129},{129,193},{193,1... | collective-permute-start | bytes 393224 | tf_op jit(solution)/shard_map/ppermute | solution.py:363
  115.2 15.0 %collective-permute-start.3 = (bf16[512,128]{1,0:T(8,128)(2,1)S(1)}, bf16[512,128]{1,0:T(8,128)(2,1)S(1)}, u32[]{:S(2)}, u32[]{:S(2)}) collective-permute-start(bf16[512,128]{1,0:T(8,128)(2,1)S(1)} %get-tuple-element.30), channel_id=1, source_target_pairs={{0,128},{64,192},{128,0},{192,64},{1,129},{65,193},{129,1},{193,65... | collective-permute-start | bytes 393224 | tf_op jit(solution)/shard_map/ppermute | solution.py:363
  116.7 21.4 %collective-permute-start.4 = (bf16[512,128]{1,0:T(8,128)(2,1)S(1)}, bf16[512,128]{1,0:T(8,128)(2,1)S(1)}, u32[]{:S(2)}, u32[]{:S(2)}) collective-permute-start(bf16[512,128]{1,0:T(8,128)(2,1)S(1)} %get-tuple-element.31), channel_id=1, source_target_pairs={{0,192},{64,0},{128,64},{192,128},{1,193},{65,1},{129,65},{193,129... | collective-permute-start | bytes 393224 | tf_op jit(solution)/shard_map/ppermute | solution.py:363
  118.9 26.5 %collective-permute-start.18 = (bf16[512,128]{1,0:T(8,128)(2,1)S(1)}, bf16[512,128]{1,0:T(8,128)(2,1)S(1)}, u32[]{:S(2)}, u32[]{:S(2)}) collective-permute-start(bf16[512,128]{1,0:T(8,128)(2,1)S(1)} %get-tuple-element.40), channel_id=1, source_target_pairs={{0,64},{64,128},{128,192},{192,0},{1,65},{65,129},{129,193},{193,1... | collective-permute-start | bytes 393224 | tf_op jit(solution)/shard_map/ppermute | solution.py:476
  122.6 26.9 %collective-permute-start.19 = (bf16[512,128]{1,0:T(8,128)(2,1)S(1)}, bf16[512,128]{1,0:T(8,128)(2,1)S(1)}, u32[]{:S(2)}, u32[]{:S(2)}) collective-permute-start(bf16[512,128]{1,0:T(8,128)(2,1)S(1)} %get-tuple-element.41), channel_id=1, source_target_pairs={{0,128},{64,192},{128,0},{192,64},{1,129},{65,193},{129,1},{193,65... | collective-permute-start | bytes 393224 | tf_op jit(solution)/shard_map/ppermute | solution.py:476
  130.3 19.2 %collective-permute-start.20 = (bf16[512,128]{1,0:T(8,128)(2,1)S(1)}, bf16[512,128]{1,0:T(8,128)(2,1)S(1)}, u32[]{:S(2)}, u32[]{:S(2)}) collective-permute-start(bf16[512,128]{1,0:T(8,128)(2,1)S(1)} %get-tuple-element.42), channel_id=1, source_target_pairs={{0,192},{64,0},{128,64},{192,128},{1,193},{65,1},{129,65},{193,129... | collective-permute-start | bytes 393224 | tf_op jit(solution)/shard_map/ppermute | solution.py:476
  141.7 16.2 %collective-permute-start.15 = (bf16[512,128]{1,0:T(8,128)(2,1)S(1)}, bf16[512,128]{1,0:T(8,128)(2,1)S(1)}, u32[]{:S(2)}, u32[]{:S(2)}) collective-permute-start(bf16[512,128]{1,0:T(8,128)(2,1)S(1)} %get-tuple-element.36), channel_id=1, source_target_pairs={{0,64},{64,128},{128,192},{192,0},{1,65},{65,129},{129,193},{193,1... | collective-permute-start | bytes 393224 | tf_op jit(solution)/shard_map/ppermute | solution.py:363
  143.6 18.3 %collective-permute-start.16 = (bf16[512,128]{1,0:T(8,128)(2,1)S(1)}, bf16[512,128]{1,0:T(8,128)(2,1)S(1)}, u32[]{:S(2)}, u32[]{:S(2)}) collective-permute-start(bf16[512,128]{1,0:T(8,128)(2,1)S(1)} %get-tuple-element.37), channel_id=1, source_target_pairs={{0,128},{64,192},{128,0},{192,64},{1,129},{65,193},{129,1},{193,65... | collective-permute-start | bytes 393224 | tf_op jit(solution)/shard_map/ppermute | solution.py:363
  145.4 16.5 %collective-permute-start.17 = (bf16[512,128]{1,0:T(8,128)(2,1)S(1)}, bf16[512,128]{1,0:T(8,128)(2,1)S(1)}, u32[]{:S(2)}, u32[]{:S(2)}) collective-permute-start(bf16[512,128]{1,0:T(8,128)(2,1)S(1)} %get-tuple-element.38), channel_id=1, source_target_pairs={{0,192},{64,0},{128,64},{192,128},{1,193},{65,1},{129,65},{193,129... | collective-permute-start | bytes 393224 | tf_op jit(solution)/shard_map/ppermute | solution.py:363
  153.1 8.8 %collective-permute-start.21 = (bf16[512,128]{1,0:T(8,128)(2,1)S(1)}, bf16[512,128]{1,0:T(8,128)(2,1)S(1)}, u32[]{:S(2)}, u32[]{:S(2)}) collective-permute-start(bf16[512,128]{1,0:T(8,128)(2,1)S(1)} %get-tuple-element.44), channel_id=1, source_target_pairs={{0,64},{64,128},{128,192},{192,0},{1,65},{65,129},{129,193},{193,1... | collective-permute-start | bytes 393224 | tf_op jit(solution)/shard_map/ppermute | solution.py:363
  153.2 14.1 %collective-permute-start.22 = (bf16[512,128]{1,0:T(8,128)(2,1)S(1)}, bf16[512,128]{1,0:T(8,128)(2,1)S(1)}, u32[]{:S(2)}, u32[]{:S(2)}) collective-permute-start(bf16[512,128]{1,0:T(8,128)(2,1)S(1)} %get-tuple-element.45), channel_id=1, source_target_pairs={{0,128},{64,192},{128,0},{192,64},{1,129},{65,193},{129,1},{193,65... | collective-permute-start | bytes 393224 | tf_op jit(solution)/shard_map/ppermute | solution.py:363
  157.9 9.5 %collective-permute-start.23 = (bf16[512,128]{1,0:T(8,128)(2,1)S(1)}, bf16[512,128]{1,0:T(8,128)(2,1)S(1)}, u32[]{:S(2)}, u32[]{:S(2)}) collective-permute-start(bf16[512,128]{1,0:T(8,128)(2,1)S(1)} %get-tuple-element.46), channel_id=1, source_target_pairs={{0,192},{64,0},{128,64},{192,128},{1,193},{65,1},{129,65},{193,129... | collective-permute-start | bytes 393224 | tf_op jit(solution)/shard_map/ppermute | solution.py:363
  (14 other events, 47.0 us)
